TPU v7x, 256 devices: a whole 4x4x8 slice. The times are simulated.
256 devices in a mesh: tiles: 64 (over z, x, core), views: 4 (over y).
Axes of the slice: x: 4, y: 4, z: 8, core: 2. Of those that a mesh axis runs over, the one named last changes fastest.
Arguments:
- ref_features: bfloat16 [64, 8, 4096], P('tiles'), may hold values from -6 to 6
- partner_lines: bfloat16 [64, 4, 8, 8192], P('tiles'), may hold values from -6 to 6
- line_owner: int32 [64, 32, 1], P('tiles'), may hold values from 0 to 63; in each aligned block of 32 rows (0 to 31, 32 to 63, ..., all dimensions but the last counted through in order) at most 2 rows name the same one
- line_index: int32 [64, 32], P('tiles'), may hold values from 0 to 7
- line_offset: int32 [64, 32], P('tiles'), may hold values from 0 to 64
- neighbours: int32 [64, 4], replicated, may hold values from -1 to 63, as said below
- conv1_weight: bfloat16 [3, 3, 3, 8, 32], replicated, may hold values from -0.4375 to 0.4375
- conv1_bias: float32 [32], replicated, may hold values from -3 to 3
- conv2_weight: bfloat16 [3, 3, 3, 32, 32], replicated, may hold values from -0.21875 to 0.21875
- conv2_bias: float32 [32], replicated, may hold values from -3 to 3
Outputs:
- regularized: float32 [64, 64, 8, 4096], P('tiles', 'views')
Inputs may be any that keep to these rules, and one draw needn't show every extreme that they name: `line_owner`: among the 32 requests of one tile (aligned blocks of rows), no owner is named more than 2 times. Tile positions in a grid of 16 rows and 4 columns are a permutation of the tiles; neighbours lists the tiles above, below, left and right, -1 at the grid's edge.
All inputs are finite; a program needn't handle non-finite values.
Results may differ from a plain program's by a relative error of at most 0.0019.
Values may be sent and summed in bfloat16 or wider, within the bound.
No kernel may reach another device: no remote copies, remote signals or barrier semaphores. Data moves between devices by JAX's collectives and lax.ppermute only.
A program may use at most 128 MiB of HBM per device.

v0:
```python
from functools import partial

import jax
import jax.numpy as jnp
from jax import lax
from jax.sharding import PartitionSpec as P

C = 32
G = 8
CH = 32
NDISP = 64
W = 128
SW = 256
NPV = 4
H = 8


def with_halo(cells, sides, width):
    for axis, dim in sides:
        count = lax.axis_size(axis)
        ends = count - 1
        head = lax.slice_in_dim(cells, 0, width, axis=dim)
        tail = lax.slice_in_dim(cells, cells.shape[dim] - width, cells.shape[dim], axis=dim)
        cells = jnp.concatenate(
            [
                lax.ppermute(tail, axis, [(i, (i + 1) % count) for i in range(ends)]),
                cells,
                lax.ppermute(head, axis, [((i + 1) % count, i) for i in range(ends)]),
            ],
            axis=dim,
        )
    return cells


def pick_slot(received, link):
    piece = received[jnp.maximum(link, 0)]
    return jnp.where(link >= 0, piece, jnp.zeros((), piece.dtype))


def pad_volume(volume, neighbours, channels):
    own_tile = lax.axis_index("tiles")
    disp_local, tile_rows, flat_width = volume.shape
    tile_width = flat_width // channels
    deeper = with_halo(volume, (("views", 0),), 1)
    own_links = neighbours[own_tile]
    zero_value = jnp.zeros((), volume.dtype)
    bottom_row = deeper[:, tile_rows - 1, :]
    top_row = deeper[:, 0, :]
    to_below = (neighbours[:, 0] == own_tile)[:, None, None]
    to_above = (neighbours[:, 1] == own_tile)[:, None, None]
    row_send = jnp.where(to_below, bottom_row[None], jnp.where(to_above, top_row[None], zero_value))
    row_recv = lax.all_to_all(row_send, "tiles", split_axis=0, concat_axis=0, tiled=True)
    above_row = pick_slot(row_recv, own_links[0])
    below_row = pick_slot(row_recv, own_links[1])
    tall_block = jnp.concatenate([above_row[:, None, :], deeper, below_row[:, None, :]], axis=1)
    grid_cells = tall_block.reshape(disp_local + 2, tile_rows + 2, tile_width, channels)

    def split_column(column):
        inner = column[:, 1 : tile_rows + 1, :].reshape(disp_local + 2, tile_rows * channels)
        corners = jnp.concatenate([column[:, 0, :], column[:, tile_rows + 1, :]], axis=1)
        return (inner, corners)

    first_inner, first_corner = split_column(grid_cells[:, :, 0, :])
    last_inner, last_corner = split_column(grid_cells[:, :, tile_width - 1, :])
    to_right = (neighbours[:, 2] == own_tile)[:, None, None]
    to_left = (neighbours[:, 3] == own_tile)[:, None, None]
    inner_send = jnp.where(
        to_right, last_inner[None], jnp.where(to_left, first_inner[None], zero_value)
    )
    corner_send = jnp.where(
        to_right, last_corner[None], jnp.where(to_left, first_corner[None], zero_value)
    )
    inner_recv, corner_recv = (
        lax.all_to_all(inner_send, "tiles", split_axis=0, concat_axis=0, tiled=True),
        lax.all_to_all(corner_send, "tiles", split_axis=0, concat_axis=0, tiled=True),
    )

    def rebuild(link):
        inner_part = pick_slot(inner_recv, link).reshape(disp_local + 2, tile_rows, channels)
        corner_part = pick_slot(corner_recv, link)
        return jnp.concatenate(
            [corner_part[:, None, :channels], inner_part, corner_part[:, None, channels:]], axis=1
        )

    left_col = rebuild(own_links[2])
    right_col = rebuild(own_links[3])
    return jnp.concatenate([left_col[:, :, None, :], grid_cells, right_col[:, :, None, :]], axis=2)


def conv_layer(padded, kernel, bias):
    moved = jnp.transpose(padded, (3, 0, 1, 2))[None]
    output = lax.conv_general_dilated(
        moved,
        kernel,
        (1, 1, 1),
        "VALID",
        dimension_numbers=("NCDHW", "DHWIO", "NCDHW"),
        preferred_element_type=jnp.float32,
    )
    return output[0] + bias[:, None, None, None]


def cut_band(band_length, line_row, begin_at):
    return lax.dynamic_slice_in_dim(line_row, begin_at, band_length)


def on_device(
    ref_features,
    partner_lines,
    line_owner,
    line_index,
    line_offset,
    neighbours,
    conv1_weight,
    conv1_bias,
    conv2_weight,
    conv2_bias,
):
    tiles_count = lax.axis_size("tiles")
    views_count = lax.axis_size("views")
    view_slot = lax.axis_index("views")
    disp_local = NDISP // views_count
    owners = line_owner[0, :, 0]
    indices = line_index[0]
    offsets = line_offset[0]
    request_count = owners.shape[0]
    capacity = max(2, 2 * request_count // tiles_count)
    request_order = jnp.arange(request_count, dtype=jnp.int32)
    same_owner = (owners[:, None] == owners[None, :]) & (
        request_order[None, :] < request_order[:, None]
    )
    rank_in = jnp.sum(same_owner.astype(jnp.int32), axis=1)
    slot_of = owners * capacity + rank_in
    line_id = request_order // H * H + indices
    wanted = jnp.full((tiles_count * capacity,), -1, jnp.int32).at[slot_of].set(line_id)
    shifts = jnp.zeros((tiles_count * capacity,), jnp.int32).at[slot_of].set(offsets)
    asked_for = lax.all_to_all(
        jnp.stack([wanted, shifts]), "tiles", split_axis=1, concat_axis=1, tiled=True
    )
    stored = partner_lines[0].reshape(NPV * H, SW * C)
    present = (asked_for[0] >= 0)[:, None]
    fetched = stored[jnp.maximum(asked_for[0], 0)]
    band_length = (W + disp_local) * C
    slicer = jax.vmap(partial(cut_band, band_length))
    whole_lines = jnp.where(present, fetched, jnp.zeros((), fetched.dtype))
    landed = lax.all_to_all(whole_lines, "tiles", split_axis=0, concat_axis=0, tiled=True)
    own_lines = landed[slot_of]
    starts = (offsets + disp_local * view_slot) * C
    line_bands = slicer(own_lines, starts)
    view_total = jnp.sum(line_bands.reshape(NPV, H, band_length).astype(jnp.float32), axis=0)
    own_features = ref_features[0].astype(jnp.float32)
    slabs = []
    for shift_step in range(disp_local):
        window = lax.slice_in_dim(view_total, shift_step * C, shift_step * C + W * C, axis=1)
        slabs.append((window * own_features).reshape(H, W * G, C // G).sum(axis=2))
    cost_volume = (jnp.stack(slabs) * (1.0 / (NPV * (C // G)))).astype(jnp.bfloat16)
    first = conv_layer(pad_volume(cost_volume, neighbours, G), conv1_weight, conv1_bias)
    hidden = jax.nn.relu(first).astype(jnp.bfloat16)
    hidden = jnp.transpose(hidden, (1, 2, 3, 0)).reshape(disp_local, H, W * CH)
    second = conv_layer(pad_volume(hidden, neighbours, CH), conv2_weight, conv2_bias)
    return jnp.transpose(second, (1, 2, 3, 0)).reshape(1, disp_local, H, W * CH)


def solution(mesh):
    return jax.shard_map(
        on_device,
        mesh=mesh,
        in_specs=(
            P("tiles", None, None),
            P("tiles", None, None, None),
            P("tiles", None, None),
            P("tiles", None),
            P("tiles", None),
            P(),
            P(),
            P(),
            P(),
            P(),
        ),
        out_specs=P("tiles", "views", None, None),
        check_vma=False,
    )
```

profile of v0, /device:TPU:1, one launch (start us, length us, event | category | flops | bytes accessed | tf_op | source)
XLA Modules:
  0.0 836.5 jit_solution(1270033963900822879)
XLA Ops:
  4.1 22.9 %all_to_all.45 = s32[2,64,2]{2,0,1:T(2,128)S(1)} all-to-all(s32[2,64,2]{2,0,1:T(2,128)S(1)} %copy.382), channel_id=1, replica_groups=mesh['tiles'=64,'views'=4] {'tiles'}, dimensions={1} | all-to-all | bytes 2048 | tf_op jit(solution)/shard_map/all_to_all | solution.py:137
  42.4 49.8 %all-to-all-done.1 = bf16[64,2,8192]{2,1,0:T(2,128)(2,1)} async-done(((bf16[64,2,8192]{2,1,0:T(2,128)(2,1)}), bf16[64,2,8192]{2,1,0:T(2,128)(2,1)}, u32[]{:S(2)}, u32[]{:S(2)}) %all-to-all-start.1) | async-done | bytes 2097184 | tf_op jit(solution)/shard_map/all_to_all | solution.py:146
  95.8 72.8 %while.1 = (s32[]{:T(128)}, bf16[32,8192]{1,0:T(8,128)(2,1)S(1)}, s32[32,2]{0,1:T(2,128)S(1)}, bf16[32,4608]{1,0:T(8,128)(2,1)S(1)}, s32[]{:T(128)}, /*index=5*/s32[]{:T(128)}) while((s32[]{:T(128)}, bf16[32,8192]{1,0:T(8,128)(2,1)S(1)}, s32[32,2]{0,1:T(2,128)S(1)}, bf16[32,4608]{1,0:T(8,128)(2,1)S(1)}, s32[]{:T(128)}, /*index=5*/s32[]{:T(128)}) %tuple.61), condition=%wide.while_cond, body=%wide.while_body.sunk | while | flops 2 | bytes 36977 | solution.py:104
  238.2 8.4 %all-to-all-start.2 = ((bf16[64,18,1024]{2,1,0:T(8,128)(2,1)}), bf16[64,18,1024]{2,1,0:T(8,128)(2,1)}, u32[]{:S(2)}, u32[]{:S(2)}) async-start(bf16[64,18,1024]{2,1,0:T(8,128)(2,1)} %select_select_fusion.1), calls=%async_computation.2 | async-start | bytes 6291456 | tf_op jit(solution)/shard_map/all_to_all | solution.py:52
  254.2 64.8 %all-to-all-done.2 = bf16[64,18,1024]{2,1,0:T(8,128)(2,1)} async-done(((bf16[64,18,1024]{2,1,0:T(8,128)(2,1)}), bf16[64,18,1024]{2,1,0:T(8,128)(2,1)}, u32[]{:S(2)}, u32[]{:S(2)}) %all-to-all-start.2) | async-done | bytes 2359328 | tf_op jit(solution)/shard_map/all_to_all | solution.py:52
  323.8 6.7 all-to-all-start.3
  333.2 7.4 all-to-all-done.3
  345.3 11.5 %all-to-all-done.4 = bf16[64,2,576]{2,1,0:T(2,128)(2,1)S(1)} async-done(((bf16[64,2,576]{2,1,0:T(2,128)(2,1)}), bf16[64,2,576]{2,1,0:T(2,128)(2,1)S(1)}, u32[]{:S(2)}, u32[]{:S(2)}) %all-to-all-start.4) | async-done | bytes 147488 | tf_op jit(solution)/shard_map/all_to_all | solution.py:74
  363.7 10.5 %copy.428 = bf16[8,18,10,1,8,17]{0,4,5,2,1,3:T(8,128)(2,1)} copy(bf16[8,18,10,1,8,17]{5,4,0,2,1,3:T(8,128)(2,1)S(1)} %reshape.358) | data formatting | bytes 783360 | tf_op jit(solution)/shard_map/conv_general_dilated | solution.py:92
  375.5 12.0 %broadcast_select_fusion.1 = f32[16,8,8,17,32]{4,2,3,1,0:T(8,128)S(1)} fusion(pred[8,17]{0,1:T(8,128)(4,1)S(1)} %copy-done.19, bf16[3,3,3,8,32]{4,3,2,1,0:T(8,128)(2,1)S(1)} %copy-done.17, bf16[8,18,10,1,7,2]{0,4,5,2,1,3:T(8,128)(2,1)S(1)} %slice.301, bf16[8,18,10,1,8,17]{0,4,5,2,1,3:T(8,128)(2,1)} %copy.428), kind=kOutput, calls=%fused_computation.31 | convolution fusion | flops 242518528 | bytes 2674184 | tf_op jit(solution)/shard_map/conv_general_dilated | solution.py:92
  396.1 5.4 copy.431
  401.4 5.9 reshape.335
  413.4 5.8 select_select_fusion
  419.2 7.0 all-to-all-start.5
  427.0 273.9 %all-to-all-done.5 = bf16[64,18,4096]{2,1,0:T(8,128)(2,1)} async-done(((bf16[64,18,4096]{2,1,0:T(8,128)(2,1)}), bf16[64,18,4096]{2,1,0:T(8,128)(2,1)}, u32[]{:S(2)}, u32[]{:S(2)}) %all-to-all-start.5) | async-done | bytes 9437216 | tf_op jit(solution)/shard_map/all_to_all | solution.py:52
  706.4 8.5 %pad_maximum_fusion = bf16[18,10,128,32]{3,1,2,0:T(8,128)(2,1)S(1)} fusion(bf16[18,1,128,32]{3,1,2,0:T(2,128)(2,1)S(1)} %select_n.297, bf16[1,8,128,32]{3,1,2,0:T(8,128)(2,1)S(1)} %copy.434, bf16[16,8,128,32]{3,1,2,0:T(8,128)(2,1)} %copy-done.2, bf16[1,8,128,32]{3,1,2,0:T(8,128)(2,1)S(1)} %copy.433, bf16[18,1,128,32]{3,1,2,0:T(2,128)(2,1)S(1)} %select_n.296), kind=kLoop, calls=%fused_computation.10 | loop fusion | flops 7372800 | bytes 2949120 | tf_op jit(solution)/shard_map/concatenate | solution.py:55
  719.9 10.7 %all-to-all-start.6 = ((bf16[64,2,576]{2,1,0:T(2,128)(2,1)}), bf16[64,2,576]{2,1,0:T(2,128)(2,1)S(1)}, u32[]{:S(2)}, u32[]{:S(2)}) async-start(bf16[64,2,576]{2,1,0:T(2,128)(2,1)} %reshape.430), calls=%async_computation.6 | async-start | bytes 327680 | tf_op jit(solution)/shard_map/all_to_all | solution.py:75
  732.0 10.3 %all-to-all-done.6 = bf16[64,2,576]{2,1,0:T(2,128)(2,1)S(1)} async-done(((bf16[64,2,576]{2,1,0:T(2,128)(2,1)}), bf16[64,2,576]{2,1,0:T(2,128)(2,1)S(1)}, u32[]{:S(2)}, u32[]{:S(2)}) %all-to-all-start.6) | async-done | bytes 147488 | tf_op jit(solution)/shard_map/all_to_all | solution.py:75
  746.7 8.8 %copy.444 = bf16[18,10,128,32]{2,3,1,0:T(8,128)(2,1)S(1)} copy(bf16[18,10,128,32]{3,1,2,0:T(8,128)(2,1)} %copy-done.3) | data formatting | bytes 2949120 | tf_op jit(solution)/shard_map/concatenate | solution.py:55
  756.6 13.4 %all-to-all-done.7 = bf16[64,18,256]{2,1,0:T(8,128)(2,1)S(1)} async-done(((bf16[64,18,256]{2,1,0:T(8,128)(2,1)}), bf16[64,18,256]{2,1,0:T(8,128)(2,1)S(1)}, u32[]{:S(2)}, u32[]{:S(2)}) %all-to-all-start.7) | async-done | bytes 589856 | tf_op jit(solution)/shard_map/all_to_all | solution.py:74
  777.4 10.9 %reshape.365 = bf16[32,18,10,1,8,17]{5,4,0,2,1,3:T(8,128)(2,1)} reshape(bf16[32,18,10,1,136]{4,0,2,1,3:T(8,128)(2,1)S(1)} %pad.4) | data formatting | bytes 3133440 | tf_op jit(solution)/shard_map/conv_general_dilated | solution.py:92
  788.3 15.3 %copy.447 = bf16[32,18,10,1,8,17]{0,4,5,2,1,3:T(8,128)(2,1)} copy(bf16[32,18,10,1,8,17]{5,4,0,2,1,3:T(8,128)(2,1)} %reshape.365) | data formatting | bytes 3133440 | tf_op jit(solution)/shard_map/conv_general_dilated | solution.py:92
  805.0 17.0 %broadcast_select_fusion = f32[16,8,8,17,32]{4,2,3,1,0:T(8,128)S(1)} fusion(pred[8,17]{0,1:T(8,128)(4,1)S(1)} %copy-done.19, bf16[3,3,3,32,32]{4,3,2,1,0:T(8,128)(2,1)S(1)} %copy-done.16, bf16[32,18,10,1,7,2]{0,4,5,2,1,3:T(8,128)(2,1)S(1)} %slice.319, bf16[32,18,10,1,8,17]{0,4,5,2,1,3:T(8,128)(2,1)} %copy.447), kind=kOutput, calls=%fused_computation.30 | convolution fusion | flops 968402944 | bytes 4011656 | tf_op jit(solution)/shard_map/conv_general_dilated | solution.py:92
  829.1 7.2 reshape.336
  (377 shorter events, 234.6 us)
Async XLA Ops:
  0.0 27.2 %copy-start = (bf16[1,4,8,8192]{3,2,1,0:T(8,128)(2,1)S(1)}, bf16[1,4,8,8192]{3,2,1,0:T(8,128)(2,1)}, u32[]{:S(2)}) copy-start(bf16[1,4,8,8192]{3,2,1,0:T(8,128)(2,1)} %param.11) | copy-start | bytes 1572868
  33.8 8.5 %copy-start.18 = (s32[1,32]{1,0:T(1,128)S(1)}, s32[1,32]{1,0:T(1,128)}, u32[]{:S(2)}) copy-start(s32[1,32]{1,0:T(1,128)} %param.14) | copy-start | bytes 388
  37.0 55.2 %all-to-all-start.1 = ((bf16[64,2,8192]{2,1,0:T(2,128)(2,1)}), bf16[64,2,8192]{2,1,0:T(2,128)(2,1)}, u32[]{:S(2)}, u32[]{:S(2)}) async-start(bf16[64,2,8192]{2,1,0:T(2,128)(2,1)} %broadcast_select_fusion.2), calls=%async_computation.1 | async-start | bytes 4194304 | tf_op jit(solution)/shard_map/all_to_all | solution.py:146
  42.4 126.3 %copy-start.12 = (bf16[1,8,4096]{2,1,0:T(8,128)(2,1)S(1)}, bf16[1,8,4096]{2,1,0:T(8,128)(2,1)}, u32[]{:S(2)}) copy-start(bf16[1,8,4096]{2,1,0:T(8,128)(2,1)} %param.10) | copy-start | bytes 196612
  219.3 4.3 copy-start.7
  219.3 4.3 copy-start.8
  219.3 4.3 copy-start.9
  219.3 4.3 copy-start.10
  219.3 4.3 copy-start.11
  220.7 12.2 %copy-start.13 = (s32[64,4]{0,1:T(4,128)S(1)}, s32[64,4]{0,1:T(4,128)}, u32[]{:S(2)}) copy-start(s32[64,4]{0,1:T(4,128)} %param.15) | copy-start | bytes 3076
  228.3 4.5 collective-permute-start
  231.5 4.5 collective-permute-start.1
  238.2 80.8 %all-to-all-start.2 = ((bf16[64,18,1024]{2,1,0:T(8,128)(2,1)}), bf16[64,18,1024]{2,1,0:T(8,128)(2,1)}, u32[]{:S(2)}, u32[]{:S(2)}) async-start(bf16[64,18,1024]{2,1,0:T(8,128)(2,1)} %select_select_fusion.1), calls=%async_computation.2 | async-start | bytes 6291456 | tf_op jit(solution)/shard_map/all_to_all | solution.py:52
  323.8 16.8 %all-to-all-start.3 = ((bf16[64,2,144]{2,1,0:T(2,128)(2,1)}), bf16[64,2,144]{2,1,0:T(2,128)(2,1)S(1)}, u32[]{:S(2)}, u32[]{:S(2)}) async-start(bf16[64,2,144]{2,1,0:T(2,128)(2,1)} %reshape.426), calls=%async_computation.3 | async-start | bytes 131072 | tf_op jit(solution)/shard_map/all_to_all | solution.py:75
  340.6 16.2 %all-to-all-start.4 = ((bf16[64,2,576]{2,1,0:T(2,128)(2,1)}), bf16[64,2,576]{2,1,0:T(2,128)(2,1)S(1)}, u32[]{:S(2)}, u32[]{:S(2)}) async-start(bf16[64,2,576]{2,1,0:T(2,128)(2,1)} %reshape.428), calls=%async_computation.4 | async-start | bytes 327680 | tf_op jit(solution)/shard_map/all_to_all | solution.py:74
  363.6 11.9 %copy-start.17 = (bf16[3,3,3,8,32]{4,3,2,1,0:T(8,128)(2,1)S(1)}, bf16[3,3,3,8,32]{4,3,2,1,0:T(8,128)(2,1)}, u32[]{:S(2)}) copy-start(bf16[3,3,3,8,32]{4,3,2,1,0:T(8,128)(2,1)} %param.16) | copy-start | bytes 41476
  363.6 11.9 %copy-start.19 = (pred[8,17]{0,1:T(8,128)(4,1)S(1)}, pred[8,17]{0,1:T(8,128)(4,1)}, u32[]{:S(2)}) copy-start(pred[8,17]{0,1:T(8,128)(4,1)} %constant.95) | copy-start | bytes 412
  392.8 16.1 %collective-permute-start.2 = (bf16[1,8,4096]{2,1,0:T(8,128)(2,1)S(1)}, bf16[1,8,4096]{2,1,0:T(8,128)(2,1)S(1)}, u32[]{:S(2)}, u32[]{:S(2)}) collective-permute-start(bf16[1,8,4096]{2,1,0:T(8,128)(2,1)S(1)} %slice.233), channel_id=1, source_target_pairs={{0,1},{1,2},{2,3},{4,5},{5,6},{6,7},{8,9},{9,10},{10,11},{12,13},{... | collective-permute-start | bytes 196616 | tf_op jit(solution)/shard_map/ppermute | solution.py:26
  407.6 5.0 collective-permute-start.3
  419.2 281.6 %all-to-all-start.5 = ((bf16[64,18,4096]{2,1,0:T(8,128)(2,1)}), bf16[64,18,4096]{2,1,0:T(8,128)(2,1)}, u32[]{:S(2)}, u32[]{:S(2)}) async-start(bf16[64,18,4096]{2,1,0:T(8,128)(2,1)} %select_select_fusion), calls=%async_computation.5 | async-start | bytes 25165824 | tf_op jit(solution)/shard_map/all_to_all | solution.py:52
  719.9 22.4 %all-to-all-start.6 = ((bf16[64,2,576]{2,1,0:T(2,128)(2,1)}), bf16[64,2,576]{2,1,0:T(2,128)(2,1)S(1)}, u32[]{:S(2)}, u32[]{:S(2)}) async-start(bf16[64,2,576]{2,1,0:T(2,128)(2,1)} %reshape.430), calls=%async_computation.6 | async-start | bytes 327680 | tf_op jit(solution)/shard_map/all_to_all | solution.py:75
  742.3 27.7 %all-to-all-start.7 = ((bf16[64,18,256]{2,1,0:T(8,128)(2,1)}), bf16[64,18,256]{2,1,0:T(8,128)(2,1)S(1)}, u32[]{:S(2)}, u32[]{:S(2)}) async-start(bf16[64,18,256]{2,1,0:T(8,128)(2,1)} %select_select_fusion.2), calls=%async_computation.7 | async-start | bytes 1572864 | tf_op jit(solution)/shard_map/all_to_all | solution.py:74
  788.3 16.7 %copy-start.16 = (bf16[3,3,3,32,32]{4,3,2,1,0:T(8,128)(2,1)S(1)}, bf16[3,3,3,32,32]{4,3,2,1,0:T(8,128)(2,1)}, u32[]{:S(2)}) copy-start(bf16[3,3,3,32,32]{4,3,2,1,0:T(8,128)(2,1)} %param.18) | copy-start | bytes 165892
  824.4 11.9 %copy-start.1 = (bf16[1,4,8,8192]{3,2,1,0:T(8,128)(2,1)S(1)}, bf16[1,4,8,8192]{3,2,1,0:T(8,128)(2,1)}, u32[]{:S(2)}) copy-start(bf16[1,4,8,8192]{3,2,1,0:T(8,128)(2,1)} %param.11) | copy-start | bytes 1572868
  (7 other events, 21.5 us)
where the time goes:
time: 845 us; the launch traced here: 837 us
  waiting for transfers between devices  438 us (52%)
  local copies, waits for them, and re-layouts  226 us (27%)
  other arithmetic  56.8 us (7%)
  starting transfers between devices  56 us (7%)
  matrix products  29 us (3%)
  blocking collectives  22.9 us (3%)
    all_to_all x2, waiting for transfers between devices, pad_volume(): lax.all_to_all(row_send, 'tiles', split_axis=0, concat_axis=0, tiled=True)  339 us
    gather x128, local copies, waits for them, and re-layouts  71.4 us
    all_to_all x1, waiting for transfers between devices, on_device(): lax.all_to_all(whole_lines, 'tiles', split_axis=0, concat_axis=0, tiled=T...  49.8 us
    conv_general_dilated x8, local copies, waits for them, and re-layouts, conv_layer(): lax.conv_general_dilated(moved, kernel, (1, 1, 1), 'VALID', dimension_num...  46 us
    conv_general_dilated x2, matrix products, conv_layer(): lax.conv_general_dilated(moved, kernel, (1, 1, 1), 'VALID', dimension_num...  29 us
    all_to_all x2, waiting for transfers between devices, pad_volume(): lax.all_to_all(inner_send, 'tiles', split_axis=0, concat_axis=0, tiled=True)  24.9 us
    all_to_all x1, blocking collectives, on_device(): lax.all_to_all(jnp.stack([wanted, shifts]), 'tiles', split_axis=1, concat...  22.9 us
    reduce_sum x16, other arithmetic, on_device(): slabs.append((window * own_features).reshape(H, W * G, C // G).sum(axis=2))  21.4 us
  transfers between devices with their start and end apart: 11, of which 9 were waited for; matrix products, arithmetic and copies ran while one was open for 3% of the time, Pallas kernels for 0%

commit v1 on v0

v1 whole, which is shorter than its diff:
```python
import jax
import jax.numpy as jnp
import numpy as np
from jax import lax
from jax.experimental import pallas as pl
from jax.experimental.pallas import tpu as pltpu
from jax.sharding import Mesh, PartitionSpec as P

C = 32
G = 8
CH = 32
NDISP = 64
W = 128
NPV = 4
H = 8
LINE = 64
PIECE = 560
SLOTS = 55
PART = SLOTS * 16
BLOCKS = 18
ROWS = BLOCKS * 16
DL = 16
ZB, XB, CB = 8, 4, 2

bf16 = jnp.bfloat16
f32 = jnp.float32


def group_sum_matrix():
    table = np.zeros((256, 256), np.float32)
    for j in range(8):
        for ch in range(C):
            row, g = j * C + ch, ch // 4
            for b in range(3):
                table[row, b * 64 + j * G + g] = 1.0 / 16
                if j == 7:
                    table[row, 192 + b * 16 + g] = 1.0 / 16
                if j == 0:
                    table[row, 192 + b * 16 + 8 + g] = 1.0 / 16
    return np.concatenate([table, table], axis=0)


def taps(cols_in, cols_out):
    picks = np.zeros((len(cols_in), len(cols_out), 3), np.float32)
    for p, j in enumerate(cols_in):
        for q, n in enumerate(cols_out):
            if 0 <= j - n + 1 < 3:
                picks[p, q, j - n + 1] = 1.0
    return picks


def spread_first(kernel):
    out_cols = list(range(8)) + [7, 0] * 3 + [50, 50]
    center = jnp.einsum("jne,abego->abjgno", taps(range(8), out_cols), kernel.astype(f32))
    edges = jnp.einsum("jne,abego->abjgno", taps([-1, 8], out_cols), kernel.astype(f32))
    width = len(out_cols) * CH
    center = center.reshape(3, 192, width)
    edges = edges.reshape(3, 48, width)
    return jnp.concatenate([center, edges, jnp.zeros((3, 16, width), f32)], axis=1).astype(bf16)


def spread_second(kernel):
    center = jnp.einsum("jne,abeko->abjkno", taps(range(8), range(8)), kernel.astype(f32))
    edges = jnp.einsum("jne,abeko->abjkno", taps([-1, 8], range(8)), kernel.astype(f32))
    center = center.reshape(3, 768, 256)
    edges = edges.reshape(3, 192, 256)
    return jnp.concatenate([center, edges, jnp.zeros((3, 64, 256), f32)], axis=1).astype(bf16)


def select_body(tabs, links, where_am_i, pieces, out, stage, padded, shifted):
    tau = where_am_i[0]
    core = where_am_i[1]
    view = where_am_i[2]

    def look(tile, side):
        return jnp.where(tile >= 0, links[jnp.maximum(tile, 0) * 4 + side], -1)

    up, down, left, right = [links[tau * 4 + side] for side in range(4)]
    tiles = [
        [up, look(left, 0), look(right, 0)],
        [tau, left, right],
        [down, look(left, 1), look(right, 1)],
    ]
    stage[...] = jnp.zeros(stage.shape, f32)
    padded[...] = jnp.zeros(padded.shape, f32)
    lane = lax.broadcasted_iota(jnp.int32, (56, 128), 1)

    def put_line(hh, band, column):
        source = tiles[band][column]
        row = hh - 2 if band == 1 else (6 + hh if band == 0 else hh - 10)
        entry = tabs[jnp.maximum(source, 0) * 8 + row]
        owner = entry >> 10
        index = (entry >> 7) & 7
        start = (entry & 127) + 2

        @pl.when((source >= 0) & ((owner & 1) == core))
        def _():
            base = pl.multiple_of((owner >> 1) * PIECE + index * LINE, 16)
            padded[8 : 8 + LINE, :] = pieces[pl.ds(base, LINE), :].astype(f32)
            first = (start >> 2) + 7
            turn = (start & 3) * 32
            lower = padded[pl.ds(first, 56), :]
            upper = padded[pl.ds(first + 1, 56), :]
            shifted[...] = pltpu.roll(
                jnp.where(lane >= turn, lower, upper), (128 - turn) & 127, 1
            )
            for dest in range(4):
                if column == 0:
                    stage[pl.ds(dest * PART + hh, 37, 16), :] = shifted[4 * dest : 4 * dest + 37, :]
                elif column == 1:
                    stage[pl.ds(dest * PART + 37 * 16 + hh, 7, 16), :] = shifted[
                        4 * dest + 30 : 4 * dest + 37, :
                    ]
                else:
                    stage[pl.ds(dest * PART + 44 * 16 + hh, 7, 16), :] = shifted[
                        4 * dest : 4 * dest + 7, :
                    ]

    for hh in range(12):
        for column in range(3):
            put_line(hh, 0 if hh < 2 else (1 if hh < 10 else 2), column)

    halo_center = jnp.where(view < 2, up, down)
    halo_left = jnp.where(view < 2, tiles[0][1], tiles[2][1])
    halo_right = jnp.where(view < 2, tiles[0][2], tiles[2][2])
    halo_row = jnp.where(view < 2, view, view + 8)

    def mine(tile):
        return (tile >= 0) & ((tile & 1) == core)

    def base_of(tile, extra):
        return pl.multiple_of((jnp.maximum(tile, 0) >> 1) * PIECE + extra, 16)

    @pl.when(mine(halo_center))
    def _():
        cells = pieces[pl.ds(base_of(halo_center, 512), 32), :].astype(f32)
        for dest in range(4):
            stage[pl.ds(dest * PART + 12 + view, 32, 16), :] = cells

    def put_pair(cells, slot, row):
        for dest in range(4):
            for k in range(2):
                stage[pl.ds(dest * PART + (slot + k) * 16 + row, 1), :] = cells[k : k + 1]

    @pl.when(mine(halo_left))
    def _():
        cells = pieces[pl.ds(base_of(halo_left, 528), 16), :].astype(f32)
        put_pair(cells[14:16], 51, halo_row)

    @pl.when(mine(halo_right))
    def _():
        cells = pieces[pl.ds(base_of(halo_right, 512), 16), :].astype(f32)
        put_pair(cells[0:2], 53, halo_row)

    @pl.when(mine(left))
    def _():
        cells = pieces[pl.ds(base_of(left, 544), 16), :].astype(f32)
        for k in range(2):
            put_pair(cells[4 * k + 2 : 4 * k + 4], 51, 2 + 2 * view + k)

    @pl.when(mine(right))
    def _():
        cells = pieces[pl.ds(base_of(right, 544), 16), :].astype(f32)
        for k in range(2):
            put_pair(cells[4 * k : 4 * k + 2], 53, 2 + 2 * view + k)

    out[...] = stage[...].astype(bf16)


def select_pieces(tabs, links, where_am_i, pieces):
    return pl.pallas_call(
        select_body,
        out_shape=jax.ShapeDtypeStruct((4 * PART, 128), bf16),
        grid_spec=pltpu.PrefetchScalarGridSpec(
            num_scalar_prefetch=3,
            grid=(1,),
            in_specs=[pl.BlockSpec(pieces.shape, lambda i, *_: (0, 0))],
            out_specs=pl.BlockSpec((4 * PART, 128), lambda i, *_: (0, 0)),
            scratch_shapes=[
                pltpu.VMEM((4 * PART, 128), f32),
                pltpu.VMEM((88, 128), f32),
                pltpu.VMEM((56, 128), f32),
            ],
        ),
        name="select_pieces",
    )(tabs, links, where_am_i, pieces)


def slot_of(block, half):
    if block == 0:
        return 37 + half
    if block == BLOCKS - 1:
        return 44 + half
    return 2 * (block - 1) + half


def volume_body(
    facts, bands, ref, summing, first, first_bias, second, second_bias, out,
    turned, refx, factors, sums, padded, hidden, keep, wide,
):
    view = facts[0]
    lane16 = lax.broadcasted_iota(jnp.int32, (16, 128), 1)
    sub8 = lax.broadcasted_iota(jnp.int32, (8, 128), 0)

    def total(slot):
        cells = bands[slot * 16 : slot * 16 + 16, :].astype(f32)
        for u in range(1, 4):
            at = u * PART + slot * 16
            cells = cells + bands[at : at + 16, :].astype(f32)
        return cells

    lanes = [lane16 >= 32 * m for m in range(4)]
    current = total(0)
    for slot in range(51):
        following = total(slot + 1)
        turned[slot] = current
        for m in range(1, 4):
            turned[m * 51 + slot] = pltpu.roll(
                jnp.where(lanes[m], current, following), 128 - 32 * m, 1
            )
        if slot < 32:
            block, half = 1 + slot // 2, slot % 2
            halo = pltpu.roll(current[8:16], 4, 0)
            own = pltpu.roll(ref[:, slot * 128 : slot * 128 + 128].astype(f32), 2, 0)
            refx[block * 2 + half, 0:8] = jnp.where(sub8 < 2, halo, own)
            refx[block * 2 + half, 8:16] = jnp.where(sub8 < 2, own, halo)
        current = following
    for half in range(2):
        refx[half] = total(51 + half)
        refx[2 * (BLOCKS - 1) + half] = total(53 + half)

    row = lax.broadcasted_iota(jnp.int32, (ROWS, 128), 0)
    high, block = row & 15, row >> 4
    inside = (high >= jnp.where(facts[1] >= 0, 0, 1)) & (high <= jnp.where(facts[2] >= 0, 9, 8))
    inside &= (block >= jnp.where(facts[3] >= 0, 0, 1))
    inside &= (block <= jnp.where(facts[4] >= 0, BLOCKS - 1, BLOCKS - 2))
    keep[...] = jnp.where(inside, 1.0, 0.0)
    sums[ROWS:, :] = jnp.zeros((sums.shape[0] - ROWS, 256), f32)
    hidden[ROWS:, :] = jnp.zeros((hidden.shape[0] - ROWS, 512), f32)

    def cost_step(q, carry):
        for m in range(4):
            dd = 4 * q + m
            for block in range(BLOCKS):
                for half in range(2):
                    product = refx[2 * block + half] * turned[m * 51 + slot_of(block, half) + q]
                    top = product.astype(bf16)
                    rest = (product - top.astype(f32)).astype(bf16)
                    at = block * 16
                    factors[at : at + 16, half * 128 : half * 128 + 128] = top
                    factors[at : at + 16, 256 + half * 128 : 384 + half * 128] = rest
            cells = jnp.dot(factors[...], summing[...], preferred_element_type=f32)
            depth = 16 * view + dd - 2
            sums[0:ROWS, :] = jnp.where((depth >= 0) & (depth < NDISP), cells, 0.0)
            for block in range(BLOCKS):
                at = block * 16
                lo = max(block - 1, 0) * 16
                hi = min(block + 1, BLOCKS - 1) * 16
                left = jnp.where(lane16 < 64, sums[at : at + 16, 0:128], sums[at + 1 : at + 17, 0:128])
                half = sums[at + 2 : at + 18, 128:256]
                for b in range(3):
                    half = jnp.where(lane16 >= 64 + 16 * b, sums[lo + b : lo + b + 16, 128:256], half)
                    half = jnp.where(lane16 >= 72 + 16 * b, sums[hi + b : hi + b + 16, 128:256], half)
                line = pl.multiple_of(dd * ROWS + at, 16)
                padded[pl.ds(line, 16), 0:128] = left.astype(bf16)
                padded[pl.ds(line, 16), 128:256] = half.astype(bf16)
        return carry

    lax.fori_loop(0, 5, cost_step, 0)

    lane8 = lax.broadcasted_iota(jnp.int32, (8, 128), 1)

    def hidden_step(step, carry):
        cells = jnp.broadcast_to(first_bias[...], (ROWS, 512))
        for a in range(3):
            at = pl.multiple_of((step + a) * ROWS, 16)
            cells = cells + jnp.dot(padded[pl.ds(at, ROWS), :], first[a], preferred_element_type=f32)
        depth = 16 * view + step - 1
        live = jnp.where((depth >= 0) & (depth < NDISP), keep[...], 0.0) > 0.5
        for part in range(4):
            span = slice(part * 128, part * 128 + 128)
            hidden[0:ROWS, span] = jnp.where(live, jnp.maximum(cells[:, span], 0.0), 0.0)

        def block_cells(block):
            at, lo, hi = block * 16, (block - 1) * 16, (block + 1) * 16
            parts = []
            for b in range(3):
                parts.append(hidden[at + b : at + b + 8, 0:128])
                parts.append(hidden[at + b : at + b + 8, 128:256])
            edge = hidden[hi + 1 : hi + 9, 256:384]
            edge = jnp.where(lane8 < 96, hidden[lo + 1 : lo + 9, 256:384], edge)
            edge = jnp.where(lane8 < 64, hidden[hi : hi + 8, 256:384], edge)
            parts.append(jnp.where(lane8 < 32, hidden[lo : lo + 8, 256:384], edge))
            edge = hidden[hi + 2 : hi + 10, 384:512]
            parts.append(jnp.where(lane8 < 32, hidden[lo + 2 : lo + 10, 384:512], edge))
            return parts

        for pair in range(8):
            one = block_cells(1 + 2 * pair)
            two = block_cells(2 + 2 * pair)
            at = pl.multiple_of(step * 128 + pair * 16, 16)
            for part in range(8):
                wide[pl.ds(at, 16), part * 128 : part * 128 + 128] = jnp.concatenate(
                    [one[part], two[part]], axis=0
                ).astype(bf16)
        return carry

    lax.fori_loop(0, DL + 2, hidden_step, 0)

    def output_step(step, carry):
        cells = jnp.broadcast_to(second_bias[...], (512, 256))
        for a in range(3):
            at = pl.multiple_of((step * 4 + a) * 128, 128)
            cells = cells + jnp.dot(wide[pl.ds(at, 512), :], second[a], preferred_element_type=f32)
        for d in range(4):
            for block in range(16):
                at = d * 128 + block * 8
                out[step * 4 + d, :, block * 256 : block * 256 + 256] = cells[at : at + 8, :]
        return carry

    lax.fori_loop(0, 4, output_step, 0)


def volume(facts, bands, ref, first, first_bias, second, second_bias):
    operands = (bands, ref, jnp.asarray(group_sum_matrix(), bf16), first, first_bias, second, second_bias)

    def whole(x):
        return pl.BlockSpec(x.shape, lambda i, *_: (0,) * x.ndim)

    return pl.pallas_call(
        volume_body,
        out_shape=jax.ShapeDtypeStruct((DL, H, W * CH), f32),
        grid_spec=pltpu.PrefetchScalarGridSpec(
            num_scalar_prefetch=1,
            grid=(1,),
            in_specs=[whole(x) for x in operands],
            out_specs=pl.BlockSpec((DL, H, W * CH), lambda i, *_: (0, 0, 0)),
            scratch_shapes=[
                pltpu.VMEM((4 * 51, 16, 128), f32),
                pltpu.VMEM((2 * BLOCKS, 16, 128), f32),
                pltpu.VMEM((ROWS, 512), bf16),
                pltpu.VMEM((ROWS + 16, 256), f32),
                pltpu.VMEM((20 * ROWS, 256), bf16),
                pltpu.VMEM((ROWS + 16, 512), f32),
                pltpu.VMEM((ROWS, 128), f32),
                pltpu.VMEM((18 * 128, 1024), bf16),
            ],
        ),
        name="volume",
    )(facts, *operands)


def on_device(
    ref_features, partner_lines, line_owner, line_index, line_offset, neighbours,
    conv1_weight, conv1_bias, conv2_weight, conv2_bias,
):
    view = lax.axis_index("views")
    core = lax.axis_index("c")
    tile = (lax.axis_index("z") * XB + lax.axis_index("x")) * CB + core
    ref = ref_features[0]

    lines = lax.dynamic_index_in_dim(partner_lines[0], view, 0, keepdims=False)
    halo_row = lax.dynamic_slice_in_dim(ref, (view + 6) % 8, 1, axis=0)
    sides = lax.dynamic_slice_in_dim(ref, 2 * view, 2, axis=0)
    sides = jnp.concatenate([sides[:, 0:256], sides[:, 3840:4096]], axis=1)
    payload = jnp.concatenate(
        [
            lines.reshape(8 * LINE, 128),
            halo_row.reshape(32, 128),
            sides.reshape(8, 128),
            jnp.zeros((8, 128), bf16),
        ],
        axis=0,
    )
    row = lax.all_gather(payload, "x", axis=0, tiled=True)
    pieces = lax.all_gather(row, "z", axis=0, tiled=True)

    coded = line_owner[0, :, 0] * 1024 + line_index[0] * 128 + line_offset[0]
    coded = lax.dynamic_slice_in_dim(coded, view * 8, 8)
    tabs = lax.all_to_all(
        jnp.broadcast_to(coded[None], (64, 8)), ("z", "x", "c"), split_axis=0, concat_axis=0, tiled=True
    ).reshape(512)
    links = neighbours.reshape(256)

    other = tile + 1 - 2 * core
    theirs = select_pieces(tabs, links, jnp.stack([other, core, view]), pieces)
    swapped = lax.ppermute(theirs, "c", [(0, 1), (1, 0)])
    own = select_pieces(tabs, links, jnp.stack([tile, core, view]), pieces)
    bands = lax.all_to_all(own + swapped, "views", split_axis=0, concat_axis=0, tiled=True)

    facts = jnp.concatenate([view[None], neighbours[tile]])
    first = spread_first(conv1_weight)
    second = spread_second(conv2_weight)
    first_bias = jnp.tile(conv1_bias, 16)[None]
    second_bias = jnp.tile(conv2_bias, 8)[None]
    return volume(facts, bands, ref, first, first_bias, second, second_bias)[None]


def solution(mesh):
    fine = Mesh(mesh.devices.reshape(ZB, XB, CB, NPV), ("z", "x", "c", "views"))
    tiles = ("z", "x", "c")
    return jax.shard_map(
        on_device,
        mesh=fine,
        in_specs=(
            P(tiles, None, None),
            P(tiles, None, None, None),
            P(tiles, None, None),
            P(tiles, None),
            P(tiles, None),
            P(),
            P(),
            P(),
            P(),
            P(),
        ),
        out_specs=P(tiles, "views", None, None),
        check_vma=False,
    )
```

time: 845 us -> 171 us (0.20)
  waiting for transfers between devices: 438 us -> 45.5 us
  local copies, waits for them, and re-layouts: 226 us -> 29.3 us
  other arithmetic: 56.8 us -> 7.97 us
  starting transfers between devices: 56 us -> 19.4 us
  Pallas kernels: 0 us -> 34.7 us
  matrix products: 29 us -> 6.61 us
  blocking collectives: 22.9 us -> 13 us
    all_to_all x7 -> x2, waiting for transfers between devices: 431 us -> 7.93 us  [the longest x1 7.92 us: on_device(): lax.all_to_all(jnp.broadcast_to(coded[None], (64, 8)), ('z', 'x', 'c'), s...]
    gather x131 -> x0, local copies, waits for them, and re-layouts: 78.7 us -> none
    conv_general_dilated x8 -> x0, local copies, waits for them, and re-layouts: 46 us -> none  [conv_layer(): lax.conv_general_dilated(moved, kernel, (1, 1, 1), 'VALID', dimension_num...]
    all_gather x0 -> x1, waiting for transfers between devices: none -> 37.6 us  [on_device(): pieces = lax.all_gather(row, 'z', axis=0, tiled=True)]
    pallas_call x0 -> x3, Pallas kernels: none -> 34.7 us  [the longest x1 23.1 us: volume(): pl.pallas_call(volume_body, out_shape=jax.ShapeDtypeStruct((DL, H, W * CH...]
    conv_general_dilated x2 -> x0, matrix products: 29 us -> none  [conv_layer(): lax.conv_general_dilated(moved, kernel, (1, 1, 1), 'VALID', dimension_num...]
    all_to_all x7 -> x2, starting transfers between devices: 47 us -> 18.7 us  [the longest x1 14.1 us: on_device(): lax.all_to_all(jnp.broadcast_to(coded[None], (64, 8)), ('z', 'x', 'c'), s...]
    all_to_all x1 -> x0, blocking collectives: 22.9 us -> none  [on_device(): lax.all_to_all(jnp.stack([wanted, shifts]), 'tiles', split_axis=1, concat...]
  transfers between devices with their start and end apart: 11 -> 4, of which waited for: 9 -> 2; matrix products, arithmetic and copies ran while one was open for 3% -> 23% of each run, Pallas kernels for 0% -> 3%
where the time goes in v1:
time: 171 us; the launch traced here: 170 us
  waiting for transfers between devices  45.5 us (27%)
  Pallas kernels  34.7 us (20%)
  local copies, waits for them, and re-layouts  29.3 us (17%)
  starting transfers between devices  19.4 us (11%)
  between operations  13.7 us (8%)
  blocking collectives  13 us (8%)
  other arithmetic  7.97 us (5%)
  matrix products  6.61 us (4%)
    all_gather x1, waiting for transfers between devices, on_device(): pieces = lax.all_gather(row, 'z', axis=0, tiled=True)  37.6 us
    pallas_call x1, Pallas kernels, volume(): pl.pallas_call(volume_body, out_shape=jax.ShapeDtypeStruct((DL, H, W * CH...  23.1 us
    all_to_all x1, starting transfers between devices, on_device(): lax.all_to_all(jnp.broadcast_to(coded[None], (64, 8)), ('z', 'x', 'c'), s...  14.1 us
    all_gather x1, blocking collectives, on_device(): row = lax.all_gather(payload, 'x', axis=0, tiled=True)  13 us
    pallas_call x2, Pallas kernels, select_pieces(): pl.pallas_call(select_body, out_shape=jax.ShapeDtypeStruct((4 * PART, 128...  11.6 us
    all_to_all x1, waiting for transfers between devices, on_device(): lax.all_to_all(jnp.broadcast_to(coded[None], (64, 8)), ('z', 'x', 'c'), s...  7.92 us
    reshape x1, local copies, waits for them, and re-layouts, spread_second(): center = center.reshape(3, 768, 256)  6.58 us
    transpose x1, local copies, waits for them, and re-layouts, spread_second(): jnp.einsum('jne,abeko->abjkno', taps(range(8), range(8)), kernel.astype(f...  5.09 us
  transfers between devices with their start and end apart: 4, of which 2 were waited for; matrix products, arithmetic and copies ran while one was open for 23% of the time, Pallas kernels for 3%

profile of v1, /device:TPU:1, one launch (start us, length us, event | category | flops | bytes accessed | tf_op | source)
XLA Modules:
  0.0 170.1 jit_solution(16466476929550542962)
XLA Ops:
  6.6 0.9 dynamic-slice_reduce_fusion
  7.6 0.9 dynamic-slice_bitcast_fusion
  8.8 13.0 %all_gather.6 = bf16[2240,128]{1,0:T(8,128)(2,1)} all-gather(bf16[560,128]{1,0:T(8,128)(2,1)S(1)} %maximum_maximum_fusion.2), channel_id=1, replica_groups=mesh['z'=8,'x'=4,'c'=2,'views'=4] {'x'}, dimensions={0}, use_global_device_ids=true | all-gather | bytes 716800 | tf_op jit(solution)/shard_map/all_gather | solution.py:375
  22.6 14.1 %all-to-all-start = ((s32[64,1,8]{2,1,0:T(1,128)}), s32[64,1,8]{2,1,0:T(1,128)S(1)}, u32[]{:S(2)}, u32[]{:S(2)}) async-start(s32[64,1,8]{2,1,0:T(1,128)} %broadcast_in_dim.22), calls=%async_computation | async-start | bytes 65536 | tf_op jit(solution)/shard_map/all_to_all | solution.py:380
  38.1 7.9 %all-to-all-done = s32[64,1,8]{2,1,0:T(1,128)S(1)} async-done(((s32[64,1,8]{2,1,0:T(1,128)}), s32[64,1,8]{2,1,0:T(1,128)S(1)}, u32[]{:S(2)}, u32[]{:S(2)}) %all-to-all-start) | async-done | bytes 2080 | tf_op jit(solution)/shard_map/all_to_all | solution.py:380
  46.5 0.7 reduce.7
  48.0 37.6 %all-gather.2.cloned.1.call-done.pieces = bf16[17920,128]{1,0:T(8,128)(2,1)} async-done(((bf16[2240,128]{1,0:T(8,128)(2,1)}), bf16[17920,128]{1,0:T(8,128)(2,1)}) %all-gather.2.cloned.1.call-update) | async-done | bytes 4587536 | tf_op jit(solution)/shard_map/all_gather | solution.py:376
  85.6 5.9 %select_pieces.3 = bf16[3520,128]{1,0:T(8,128)(2,1)} custom-call(s32[512]{0:T(512)} %reshape.52.tabs, s32[256]{0:T(256)} %reshape.53.links, s32[3]{0:T(128)} %add_add_fusion.1.where_am_i, bf16[17920,128]{1,0:T(8,128)(2,1)} %all-gather.2.cloned.1.call-done.pieces), custom_call_target="tpu_custom_call" | custom-call | tf_op jit(solution)/shard_map/select_pieces/pallas_call | solution.py:171
  91.4 0.7 collective-permute-start
  92.8 1.5 fusion
  94.3 1.1 convert_bitcast_fusion.1
  95.5 3.6 %convert_bitcast_fusion = bf16[3,3,8,32,8,32]{5,4,3,1,0,2:T(8,128)(2,1)} fusion(bf16[8,8,3,1,1,1]{1,2,5,4,3,0:T(4,128)(2,1)S(1)} %copy-done.5, bf16[3,3,3,32,32]{4,3,2,1,0:T(8,128)(2,1)S(1)} %copy-done.2), kind=kOutput, calls=%fused_computation | convolution fusion | flops 3538944 | bytes 1235328 | tf_op jit(solution)/shard_map/jne,abeko->abjkno/dot_general | solution.py:63
  99.0 5.8 %select_pieces.2 = bf16[3520,128]{1,0:T(8,128)(2,1)} custom-call(s32[512]{0:T(512)} %reshape.52.tabs, s32[256]{0:T(256)} %reshape.53.links, s32[3]{0:T(128)} %add_add_fusion.where_am_i, bf16[17920,128]{1,0:T(8,128)(2,1)} %all-gather.2.cloned.1.call-done.pieces), custom_call_target="tpu_custom_call" | custom-call | tf_op jit(solution)/shard_map/select_pieces/pallas_call | solution.py:171
  104.8 2.6 %add.53 = bf16[3520,128]{1,0:T(8,128)(2,1)} add(bf16[3520,128]{1,0:T(8,128)(2,1)} %select_pieces.2, bf16[3520,128]{1,0:T(8,128)(2,1)} %collective-permute-done) | non-fusion elementwise | flops 450560 | bytes 2703360 | tf_op jit(solution)/shard_map/add | solution.py:389
  107.4 4.5 %all-to-all-start.1 = ((bf16[4,880,128]{2,1,0:T(8,128)(2,1)}), bf16[4,880,128]{2,1,0:T(8,128)(2,1)}, u32[]{:S(2)}, u32[]{:S(2)}) async-start(bf16[4,880,128]{2,1,0:T(8,128)(2,1)} %bitcast.65), calls=%async_computation.1 | async-start | bytes 1802240 | tf_op jit(solution)/shard_map/all_to_all | solution.py:389
  112.6 5.1 %copy.39 = bf16[3,3,8,32,8,32]{5,4,3,2,1,0:T(8,128)(2,1)} copy(bf16[3,3,8,32,8,32]{5,4,3,1,0,2:T(8,128)(2,1)} %convert_bitcast_fusion) | data formatting | bytes 2359296 | tf_op jit(solution)/shard_map/jne,abeko->abjkno/transpose | solution.py:63
  117.6 6.6 %reshape.59 = bf16[3,768,256]{2,1,0:T(8,128)(2,1)} reshape(bf16[3,3,8,32,8,32]{5,4,3,2,1,0:T(8,128)(2,1)} %copy.39) | data formatting | bytes 2359296 | tf_op jit(solution)/shard_map/reshape | solution.py:65
  124.2 2.4 %copy.41 = bf16[3,3,2,32,8,32]{5,4,3,2,1,0:T(8,128)(2,1)} copy(bf16[3,3,2,32,8,32]{5,4,3,1,0,2:T(8,128)(2,1)} %fusion) | data formatting | bytes 589824 | tf_op jit(solution)/shard_map/jne,abeko->abjkno/transpose | solution.py:64
  126.6 2.7 %reshape.60 = bf16[3,192,256]{2,1,0:T(8,128)(2,1)} reshape(bf16[3,3,2,32,8,32]{5,4,3,2,1,0:T(8,128)(2,1)} %copy.41) | data formatting | bytes 589824 | tf_op jit(solution)/shard_map/reshape | solution.py:66
  129.4 1.8 %copy.35 = bf16[3,3,8,8,16,32]{5,4,3,2,1,0:T(8,128)(2,1)} copy(bf16[3,3,8,8,16,32]{5,4,3,1,0,2:T(8,128)(2,1)S(1)} %convert_bitcast_fusion.1) | data formatting | bytes 1179648 | tf_op jit(solution)/shard_map/jne,abego->abjgno/transpose | solution.py:54
  131.3 3.7 %reshape.57 = bf16[3,192,512]{2,1,0:T(8,128)(2,1)S(1)} reshape(bf16[3,3,8,8,16,32]{5,4,3,2,1,0:T(8,128)(2,1)} %copy.35) | data formatting | bytes 1179648 | tf_op jit(solution)/shard_map/reshape | solution.py:57
  137.7 1.1 maximum_maximum_fusion.1.first
  138.7 1.5 maximum_maximum_fusion.second
  140.2 23.1 %volume.1 = f32[16,8,4096]{2,1,0:T(8,128)} custom-call(s32[5]{0:T(128)} %pad_add_fusion.facts, bf16[3520,128]{1,0:T(8,128)(2,1)} %bitcast.9.bands, bf16[8,4096]{1,0:T(8,128)(2,1)} %bitcast.66, bf16[512,256]{1,0:T(8,128)(2,1)} %constant.73.clone.summing, bf16[3,256,512]{2,1,0:T(8,128)(2,1)} %maximum_maximum_fusion.1.first, ...), custom_call_target="tpu_custom_call" | custom-call | tf_op jit(solution)/shard_map/volume/pallas_call | solution.py:330
  (64 shorter events, 7.6 us)
Async XLA Ops:
  6.5 1.9 %copy-start = (bf16[1,4,8,8192]{3,2,1,0:T(8,128)(2,1)S(1)}, bf16[1,4,8,8192]{3,2,1,0:T(8,128)(2,1)}, u32[]{:S(2)}) copy-start(bf16[1,4,8,8192]{3,2,1,0:T(8,128)(2,1)} %param.16) | copy-start | bytes 1572868
  6.5 15.3 %copy-start.14 = (s32[1,32,1]{1,2,0:T(1,128)S(1)}, s32[1,32,1]{1,2,0:T(1,128)}, u32[]{:S(2)}) copy-start(s32[1,32,1]{1,2,0:T(1,128)} %param.17) | copy-start | bytes 388
  6.5 15.3 %copy-start.13 = (s32[1,32]{1,0:T(1,128)S(1)}, s32[1,32]{1,0:T(1,128)}, u32[]{:S(2)}) copy-start(s32[1,32]{1,0:T(1,128)} %param.18) | copy-start | bytes 388
  6.5 15.3 %copy-start.12 = (s32[1,32]{1,0:T(1,128)S(1)}, s32[1,32]{1,0:T(1,128)}, u32[]{:S(2)}) copy-start(s32[1,32]{1,0:T(1,128)} %param.19) | copy-start | bytes 388
  6.5 30.8 %copy-start.7 = (s32[64,4]{0,1:T(4,128)S(1)}, s32[64,4]{0,1:T(4,128)}, u32[]{:S(2)}) copy-start(s32[64,4]{0,1:T(4,128)} %param.20) | copy-start | bytes 3076
  6.5 79.0 %all-gather.2.cloned.1.call-start = ((), (), s32[]{:S(2)}) async-start(), calls=%async_computation.2 | async-start | bytes 5160960 | tf_op jit(solution)/shard_map/all_gather | solution.py:376
  22.6 23.5 %all-to-all-start = ((s32[64,1,8]{2,1,0:T(1,128)}), s32[64,1,8]{2,1,0:T(1,128)S(1)}, u32[]{:S(2)}, u32[]{:S(2)}) async-start(s32[64,1,8]{2,1,0:T(1,128)} %broadcast_in_dim.22), calls=%async_computation | async-start | bytes 65536 | tf_op jit(solution)/shard_map/all_to_all | solution.py:380
  47.9 44.8 %copy-start.2 = (bf16[3,3,3,32,32]{4,3,2,1,0:T(8,128)(2,1)S(1)}, bf16[3,3,3,32,32]{4,3,2,1,0:T(8,128)(2,1)}, u32[]{:S(2)}) copy-start(bf16[3,3,3,32,32]{4,3,2,1,0:T(8,128)(2,1)} %param.23) | copy-start | bytes 165892
  48.0 44.8 %copy-start.9 = (bf16[2,8,3,1,1,1]{1,2,5,4,3,0:T(4,128)(2,1)S(1)}, bf16[2,8,3,1,1,1]{1,2,5,4,3,0:T(4,128)(2,1)}, u32[]{:S(2)}) copy-start(bf16[2,8,3,1,1,1]{1,2,5,4,3,0:T(4,128)(2,1)} %constant.110) | copy-start | bytes 292
  48.0 46.4 %copy-start.4 = (bf16[3,3,3,8,32]{4,3,2,1,0:T(8,128)(2,1)S(1)}, bf16[3,3,3,8,32]{4,3,2,1,0:T(8,128)(2,1)}, u32[]{:S(2)}) copy-start(bf16[3,3,3,8,32]{4,3,2,1,0:T(8,128)(2,1)} %param.21) | copy-start | bytes 41476
  48.0 46.4 %copy-start.6 = (bf16[8,16,3,1,1,1]{1,2,5,4,3,0:T(4,128)(2,1)S(1)}, bf16[8,16,3,1,1,1]{1,2,5,4,3,0:T(4,128)(2,1)}, u32[]{:S(2)}) copy-start(bf16[8,16,3,1,1,1]{1,2,5,4,3,0:T(4,128)(2,1)} %constant.109) | copy-start | bytes 2308
  91.4 13.4 %collective-permute-start = (bf16[3520,128]{1,0:T(8,128)(2,1)}, bf16[3520,128]{1,0:T(8,128)(2,1)}, u32[]{:S(2)}, u32[]{:S(2)}) collective-permute-start(bf16[3520,128]{1,0:T(8,128)(2,1)} %select_pieces.3), channel_id=1, source_target_pairs={{0,4},{4,0},{1,5},{5,1},{2,6},{6,2},{3,7},{7,3},{8,12},{12,8},{9,1... | collective-permute-start | bytes 2703368 | tf_op jit(solution)/shard_map/ppermute | solution.py:387
  94.3 1.1 copy-start.5
  107.4 4.6 %copy-start.8 = (bf16[2,16,3,1,1,1]{1,2,5,4,3,0:T(4,128)(2,1)S(1)}, bf16[2,16,3,1,1,1]{1,2,5,4,3,0:T(4,128)(2,1)}, u32[]{:S(2)}) copy-start(bf16[2,16,3,1,1,1]{1,2,5,4,3,0:T(4,128)(2,1)} %constant.108) | copy-start | bytes 580
  107.4 32.8 %all-to-all-start.1 = ((bf16[4,880,128]{2,1,0:T(8,128)(2,1)}), bf16[4,880,128]{2,1,0:T(8,128)(2,1)}, u32[]{:S(2)}, u32[]{:S(2)}) async-start(bf16[4,880,128]{2,1,0:T(8,128)(2,1)} %bitcast.65), calls=%async_computation.1 | async-start | bytes 1802240 | tf_op jit(solution)/shard_map/all_to_all | solution.py:389
  135.0 0.7 copy-start.10
  135.0 1.3 copy-start.11
  135.0 3.7 %copy-start.1 = (bf16[3,768,256]{2,1,0:T(8,128)(2,1)S(1)}, bf16[3,768,256]{2,1,0:T(8,128)(2,1)}, u32[]{:S(2)}) copy-start(bf16[3,768,256]{2,1,0:T(8,128)(2,1)} %reshape.59) | copy-start | bytes 3538948
  135.1 3.6 %copy-start.3 = (bf16[3,192,256]{2,1,0:T(8,128)(2,1)S(1)}, bf16[3,192,256]{2,1,0:T(8,128)(2,1)}, u32[]{:S(2)}) copy-start(bf16[3,192,256]{2,1,0:T(8,128)(2,1)} %reshape.60) | copy-start | bytes 884740
Sparse Core Ops, SparseCore 0:
  21.9 63.5 all-gather.1

commit v2 on v1

--- a/solution.py
+++ b/solution.py
@@ -382,17 +382,20 @@
     ).reshape(512)
     links = neighbours.reshape(256)
 
+    first = spread_first(conv1_weight)
+    second = spread_second(conv2_weight)
+    first_bias = jnp.tile(conv1_bias, 16)[None]
+    second_bias = jnp.tile(conv2_bias, 8)[None]
+    facts = jnp.concatenate([view[None], neighbours[tile]])
     other = tile + 1 - 2 * core
+    tabs, links, first, second, first_bias, second_bias, facts = lax.optimization_barrier(
+        (tabs, links, first, second, first_bias, second_bias, facts)
+    )
     theirs = select_pieces(tabs, links, jnp.stack([other, core, view]), pieces)
     swapped = lax.ppermute(theirs, "c", [(0, 1), (1, 0)])
     own = select_pieces(tabs, links, jnp.stack([tile, core, view]), pieces)
     bands = lax.all_to_all(own + swapped, "views", split_axis=0, concat_axis=0, tiled=True)
 
-    facts = jnp.concatenate([view[None], neighbours[tile]])
-    first = spread_first(conv1_weight)
-    second = spread_second(conv2_weight)
-    first_bias = jnp.tile(conv1_bias, 16)[None]
-    second_bias = jnp.tile(conv2_bias, 8)[None]
     return volume(facts, bands, ref, first, first_bias, second, second_bias)[None]
 
 

time: 171 us -> 148 us (0.87)
  the two profiles are of different devices: /device:TPU:1 before, /device:TPU:6 now
where the time goes in v2:
time: 148 us
  Pallas kernels  35.8 us (24%)
  blocking collectives  32.4 us (22%)
  waiting for transfers between devices  22.9 us (15%)
  local copies, waits for them, and re-layouts  19.7 us (13%)
  between operations  13.7 us (9%)
  starting transfers between devices  11.7 us (8%)
  other arithmetic  6.62 us (4%)
  matrix products  4.65 us (3%)
    pallas_call x1, Pallas kernels, volume(): pl.pallas_call(volume_body, out_shape=jax.ShapeDtypeStruct((DL, H, W * CH...  23.1 us
    all_gather x1, waiting for transfers between devices, on_device(): pieces = lax.all_gather(row, 'z', axis=0, tiled=True)  22.9 us
    all_to_all x1, blocking collectives, on_device(): lax.all_to_all(own + swapped, 'views', split_axis=0, concat_axis=0, tiled...  18 us
    all_gather x1, blocking collectives, on_device(): row = lax.all_gather(payload, 'x', axis=0, tiled=True)  14.4 us
    pallas_call x2, Pallas kernels, select_pieces(): pl.pallas_call(select_body, out_shape=jax.ShapeDtypeStruct((4 * PART, 128...  12.8 us
    all_to_all x1, starting transfers between devices, on_device(): lax.all_to_all(jnp.broadcast_to(coded[None], (64, 8)), ('z', 'x', 'c'), s...  11.7 us
    reshape x1, local copies, waits for them, and re-layouts, spread_second(): center = center.reshape(3, 768, 256)  5.85 us
  transfers between devices with their start and end apart: 3, of which 1 were waited for; matrix products, arithmetic and copies ran while one was open for 18% of the time, Pallas kernels for 4%

profile of v2, /device:TPU:6, one launch (start us, length us, event | category | flops | bytes accessed | tf_op | source)
XLA Modules:
  0.0 147.5 jit_solution(14722838874949287859)
XLA Ops:
  6.6 1.0 dynamic-slice_bitcast_fusion
  7.6 0.9 dynamic-slice_reduce_fusion
  8.9 14.4 %all_gather.6 = bf16[2240,128]{1,0:T(8,128)(2,1)} all-gather(bf16[560,128]{1,0:T(8,128)(2,1)S(1)} %maximum_maximum_fusion.2), channel_id=1, replica_groups=mesh['z'=8,'x'=4,'c'=2,'views'=4] {'x'}, dimensions={0}, use_global_device_ids=true | all-gather | bytes 716800 | tf_op jit(solution)/shard_map/all_gather | solution.py:375
  24.0 11.7 %all-to-all-start = ((s32[64,1,8]{2,1,0:T(1,128)}), s32[64,1,8]{2,1,0:T(1,128)S(1)}, u32[]{:S(2)}, u32[]{:S(2)}) async-start(s32[64,1,8]{2,1,0:T(1,128)} %broadcast_in_dim.21), calls=%async_computation | async-start | bytes 65536 | tf_op jit(solution)/shard_map/all_to_all | solution.py:380
  36.2 1.2 reshape.55
  37.4 1.1 convert_bitcast_fusion.1
  39.0 2.3 %reshape.54 = bf16[3,192,512]{2,1,0:T(8,128)(2,1)S(1)} reshape(bf16[3,3,8,8,16,32]{5,4,3,2,1,0:T(8,128)(2,1)S(1)} %copy.35) | data formatting | bytes 1179648 | tf_op jit(solution)/shard_map/reshape | solution.py:57
  41.5 1.5 fusion
  43.0 0.8 reshape.57
  43.9 1.7 %convert_bitcast_fusion = bf16[3,3,8,32,8,32]{5,4,3,1,0,2:T(8,128)(2,1)S(1)} fusion(bf16[8,8,3,1,1,1]{1,2,5,4,3,0:T(4,128)(2,1)S(1)} %copy-done.4, bf16[3,3,3,32,32]{4,3,2,1,0:T(8,128)(2,1)S(1)} %copy-done.1), kind=kOutput, calls=%fused_computation | convolution fusion | flops 3538944 | bytes 1235328 | tf_op jit(solution)/shard_map/jne,abeko->abjkno/dot_general | solution.py:63
  45.6 2.4 %copy.39 = bf16[3,3,8,32,8,32]{5,4,3,2,1,0:T(8,128)(2,1)} copy(bf16[3,3,8,32,8,32]{5,4,3,1,0,2:T(8,128)(2,1)S(1)} %convert_bitcast_fusion) | data formatting | bytes 2359296 | tf_op jit(solution)/shard_map/jne,abeko->abjkno/transpose | solution.py:63
  48.0 5.9 %reshape.56 = bf16[3,768,256]{2,1,0:T(8,128)(2,1)S(1)} reshape(bf16[3,3,8,32,8,32]{5,4,3,2,1,0:T(8,128)(2,1)} %copy.39) | data formatting | bytes 2359296 | tf_op jit(solution)/shard_map/reshape | solution.py:65
  54.7 1.1 maximum_maximum_fusion.1.first
  55.8 1.5 %maximum_maximum_fusion.second = bf16[3,1024,256]{2,1,0:T(8,128)(2,1)} fusion(bf16[3,192,256]{2,1,0:T(8,128)(2,1)S(1)} %reshape.57, bf16[3,768,256]{2,1,0:T(8,128)(2,1)S(1)} %reshape.56, bf16[1024]{0:T(1024)(128)(2,1)S(1)} %pad.16.clone), kind=kLoop, calls=%fused_computation.2 | loop fusion | flops 4718592 | bytes 3049472 | tf_op jit(solution)/shard_map/concatenate | solution.py:67
  58.6 0.7 broadcast_in_dim_tile.6.first_bias
  59.3 0.7 broadcast_in_dim_tile.7.second_bias
  60.5 0.7 reduce.7
  61.2 0.7 reshape.52.tabs
  61.9 22.9 %all-gather.2.cloned.1.call-done.pieces = bf16[17920,128]{1,0:T(8,128)(2,1)} async-done(((bf16[2240,128]{1,0:T(8,128)(2,1)}), bf16[17920,128]{1,0:T(8,128)(2,1)}) %all-gather.2.cloned.1.call-update) | async-done | bytes 4587536 | tf_op jit(solution)/shard_map/all_gather | solution.py:376
  84.8 6.6 %select_pieces.3 = bf16[3520,128]{1,0:T(8,128)(2,1)} custom-call(s32[512]{0:T(512)} %reshape.52.tabs, s32[256]{0:T(256)} %reshape.53.links, s32[3]{0:T(128)} %add_add_fusion.1.where_am_i, bf16[17920,128]{1,0:T(8,128)(2,1)} %all-gather.2.cloned.1.call-done.pieces), custom_call_target="tpu_custom_call" | custom-call | tf_op jit(solution)/shard_map/select_pieces/pallas_call | solution.py:171
  92.0 6.1 %select_pieces.2 = bf16[3520,128]{1,0:T(8,128)(2,1)} custom-call(s32[512]{0:T(512)} %reshape.52.tabs, s32[256]{0:T(256)} %reshape.53.links, s32[3]{0:T(128)} %add_add_fusion.where_am_i, bf16[17920,128]{1,0:T(8,128)(2,1)} %all-gather.2.cloned.1.call-done.pieces), custom_call_target="tpu_custom_call" | custom-call | tf_op jit(solution)/shard_map/select_pieces/pallas_call | solution.py:171
  98.2 1.4 add.53
  99.6 18.0 %all_to_all.17 = bf16[4,880,128]{2,1,0:T(8,128)(2,1)} all-to-all(bf16[4,880,128]{2,1,0:T(8,128)(2,1)S(1)} %bitcast.65), channel_id=1, replica_groups=mesh['z'=8,'x'=4,'c'=2,'views'=4] {'views'}, dimensions={0} | all-to-all | bytes 1802240 | tf_op jit(solution)/shard_map/all_to_all | solution.py:397
  117.6 23.1 %volume.1 = f32[16,8,4096]{2,1,0:T(8,128)} custom-call(s32[5]{0:T(128)} %pad_add_fusion.facts, bf16[3520,128]{1,0:T(8,128)(2,1)} %bitcast.66, bf16[8,4096]{1,0:T(8,128)(2,1)} %bitcast.67, bf16[512,256]{1,0:T(8,128)(2,1)} %constant.73.clone.summing, bf16[3,256,512]{2,1,0:T(8,128)(2,1)} %maximum_maximum_fusion.1.first, ...), custom_call_target="tpu_custom_call" | custom-call | tf_op jit(solution)/shard_map/volume/pallas_call | solution.py:330
  (61 shorter events, 5.6 us)
Async XLA Ops:
  6.5 2.0 %copy-start = (bf16[1,4,8,8192]{3,2,1,0:T(8,128)(2,1)S(1)}, bf16[1,4,8,8192]{3,2,1,0:T(8,128)(2,1)}, u32[]{:S(2)}) copy-start(bf16[1,4,8,8192]{3,2,1,0:T(8,128)(2,1)} %param.16) | copy-start | bytes 1572868
  6.5 29.2 %copy-start.8 = (bf16[2,16,3,1,1,1]{1,2,5,4,3,0:T(4,128)(2,1)S(1)}, bf16[2,16,3,1,1,1]{1,2,5,4,3,0:T(4,128)(2,1)}, u32[]{:S(2)}) copy-start(bf16[2,16,3,1,1,1]{1,2,5,4,3,0:T(4,128)(2,1)} %constant.108) | copy-start | bytes 580
  6.5 16.7 %copy-start.11 = (s32[1,32]{1,0:T(1,128)S(1)}, s32[1,32]{1,0:T(1,128)}, u32[]{:S(2)}) copy-start(s32[1,32]{1,0:T(1,128)} %param.19) | copy-start | bytes 388
  6.5 16.8 %copy-start.12 = (s32[1,32]{1,0:T(1,128)S(1)}, s32[1,32]{1,0:T(1,128)}, u32[]{:S(2)}) copy-start(s32[1,32]{1,0:T(1,128)} %param.18) | copy-start | bytes 388
  6.5 16.8 %copy-start.13 = (s32[1,32,1]{1,2,0:T(1,128)S(1)}, s32[1,32,1]{1,2,0:T(1,128)}, u32[]{:S(2)}) copy-start(s32[1,32,1]{1,2,0:T(1,128)} %param.17) | copy-start | bytes 388
  6.5 29.2 %copy-start.3 = (bf16[3,3,3,8,32]{4,3,2,1,0:T(8,128)(2,1)S(1)}, bf16[3,3,3,8,32]{4,3,2,1,0:T(8,128)(2,1)}, u32[]{:S(2)}) copy-start(bf16[3,3,3,8,32]{4,3,2,1,0:T(8,128)(2,1)} %param.21) | copy-start | bytes 41476
  6.6 78.3 %all-gather.2.cloned.1.call-start = ((), (), s32[]{:S(2)}) async-start(), calls=%async_computation.2 | async-start | bytes 5160960 | tf_op jit(solution)/shard_map/all_gather | solution.py:376
  23.3 14.1 %copy-start.5 = (bf16[8,16,3,1,1,1]{1,2,5,4,3,0:T(4,128)(2,1)S(1)}, bf16[8,16,3,1,1,1]{1,2,5,4,3,0:T(4,128)(2,1)}, u32[]{:S(2)}) copy-start(bf16[8,16,3,1,1,1]{1,2,5,4,3,0:T(4,128)(2,1)} %constant.109) | copy-start | bytes 2308
  24.0 36.0 %all-to-all-start = ((s32[64,1,8]{2,1,0:T(1,128)}), s32[64,1,8]{2,1,0:T(1,128)S(1)}, u32[]{:S(2)}, u32[]{:S(2)}) async-start(s32[64,1,8]{2,1,0:T(1,128)} %broadcast_in_dim.21), calls=%async_computation | async-start | bytes 65536 | tf_op jit(solution)/shard_map/all_to_all | solution.py:380
  39.0 2.4 %copy-start.7 = (bf16[2,8,3,1,1,1]{1,2,5,4,3,0:T(4,128)(2,1)S(1)}, bf16[2,8,3,1,1,1]{1,2,5,4,3,0:T(4,128)(2,1)}, u32[]{:S(2)}) copy-start(bf16[2,8,3,1,1,1]{1,2,5,4,3,0:T(4,128)(2,1)} %constant.110) | copy-start | bytes 292
  42.9 0.9 copy-start.1
  42.9 0.9 copy-start.4
  48.0 6.0 %copy-start.6 = (s32[64,4]{0,1:T(4,128)S(1)}, s32[64,4]{0,1:T(4,128)}, u32[]{:S(2)}) copy-start(s32[64,4]{0,1:T(4,128)} %param.20) | copy-start | bytes 3076
  48.0 6.7 %copy-start.2 = (bf16[3,48,512]{2,1,0:T(8,128)(2,1)S(1)}, bf16[3,48,512]{2,1,0:T(8,128)(2,1)}, u32[]{:S(2)}) copy-start(bf16[3,48,512]{2,1,0:T(8,128)(2,1)} %reshape.55) | copy-start | bytes 442372
  55.8 2.8 %copy-start.9 = (f32[32]{0:T(128)S(1)}, f32[32]{0:T(128)}, u32[]{:S(2)}) copy-start(f32[32]{0:T(128)} %param.22) | copy-start | bytes 388
  55.8 3.5 %copy-start.10 = (f32[32]{0:T(128)S(1)}, f32[32]{0:T(128)}, u32[]{:S(2)}) copy-start(f32[32]{0:T(128)} %param.24) | copy-start | bytes 388
  91.4 6.7 %collective-permute-start = (bf16[3520,128]{1,0:T(8,128)(2,1)}, bf16[3520,128]{1,0:T(8,128)(2,1)S(1)}, u32[]{:S(2)}, u32[]{:S(2)}) collective-permute-start(bf16[3520,128]{1,0:T(8,128)(2,1)} %select_pieces.3), channel_id=1, source_target_pairs={{0,4},{4,0},{1,5},{5,1},{2,6},{6,2},{3,7},{7,3},{8,12},{12,8},{9,1... | collective-permute-start | bytes 2703368 | tf_op jit(solution)/shard_map/ppermute | solution.py:395
Sparse Core Ops, SparseCore 0:
  23.4 61.3 all-gather.1

commit v3 on v2

--- a/solution.py
+++ b/solution.py
@@ -40,37 +40,75 @@
     return np.concatenate([table, table], axis=0)
 
 
-def taps(cols_in, cols_out):
-    picks = np.zeros((len(cols_in), len(cols_out), 3), np.float32)
-    for p, j in enumerate(cols_in):
-        for q, n in enumerate(cols_out):
-            if 0 <= j - n + 1 < 3:
-                picks[p, q, j - n + 1] = 1.0
-    return picks
-
-
-def spread_first(kernel):
-    out_cols = list(range(8)) + [7, 0] * 3 + [50, 50]
-    center = jnp.einsum("jne,abego->abjgno", taps(range(8), out_cols), kernel.astype(f32))
-    edges = jnp.einsum("jne,abego->abjgno", taps([-1, 8], out_cols), kernel.astype(f32))
-    width = len(out_cols) * CH
-    center = center.reshape(3, 192, width)
-    edges = edges.reshape(3, 48, width)
-    return jnp.concatenate([center, edges, jnp.zeros((3, 16, width), f32)], axis=1).astype(bf16)
-
-
-def spread_second(kernel):
-    center = jnp.einsum("jne,abeko->abjkno", taps(range(8), range(8)), kernel.astype(f32))
-    edges = jnp.einsum("jne,abeko->abjkno", taps([-1, 8], range(8)), kernel.astype(f32))
-    center = center.reshape(3, 768, 256)
-    edges = edges.reshape(3, 192, 256)
-    return jnp.concatenate([center, edges, jnp.zeros((3, 64, 256), f32)], axis=1).astype(bf16)
-
-
-def select_body(tabs, links, where_am_i, pieces, out, stage, padded, shifted):
+def spread_body(k1, k2, first, second):
+    def repeat(cells, count):
+        row = lax.broadcasted_iota(jnp.int32, (CH, count * CH), 0)
+        lane = lax.broadcasted_iota(jnp.int32, (CH, count * CH), 1)
+        copies = jnp.where((lane & 31) == row, 1.0, 0.0).astype(bf16)
+        return jnp.dot(cells, copies, preferred_element_type=f32)
+
+    wide1 = repeat(k1[...], 16)
+    wide2 = repeat(k2[...], 8)
+    lane1 = lax.broadcasted_iota(jnp.int32, (8, 512), 1) >> 5
+    lane2 = lax.broadcasted_iota(jnp.int32, (CH, 256), 1) >> 5
+    col1 = jnp.where(lane1 < 8, lane1, jnp.where(lane1 < 14, jnp.where((lane1 & 1) == 0, 7, 0), 50))
+
+    def line(cells, depth, a, b, j, col):
+        result = jnp.zeros(col.shape, f32)
+        for e in range(3):
+            at = ((a * 3 + b) * 3 + e) * depth
+            result = jnp.where(col == j + 1 - e, cells[at : at + depth], result)
+        return result
+
+    for a in range(3):
+        for b in range(3):
+            for j in range(0, 8, 2):
+                pair = [line(wide1, G, a, b, j + i, col1) for i in range(2)]
+                first[a, b * 64 + j * 8 : b * 64 + j * 8 + 16, :] = jnp.concatenate(pair, 0).astype(bf16)
+            pair = [line(wide1, G, a, b, j, col1) for j in (-1, 8)]
+            first[a, 192 + b * 16 : 208 + b * 16, :] = jnp.concatenate(pair, 0).astype(bf16)
+            for j in range(8):
+                at = b * 256 + j * 32
+                second[a, at : at + 32, :] = line(wide2, CH, a, b, j, lane2).astype(bf16)
+            for side, j in enumerate((-1, 8)):
+                at = 768 + b * 64 + side * 32
+                second[a, at : at + 32, :] = line(wide2, CH, a, b, j, lane2).astype(bf16)
+        first[a, 240:256, :] = jnp.zeros((16, 512), bf16)
+        second[a, 960:1024, :] = jnp.zeros((64, 256), bf16)
+
+
+def spread_weights(k1, k2):
+    return pl.pallas_call(
+        spread_body,
+        out_shape=(
+            jax.ShapeDtypeStruct((3, 256, 512), bf16),
+            jax.ShapeDtypeStruct((3, 1024, 256), bf16),
+        ),
+        name="spread_weights",
+    )(k1.reshape(27 * G, CH), k2.reshape(27 * CH, CH))
+
+
+def select_body(links, where_am_i, *refs):
+    chunks = refs[:16]
+    out, pieces, stage, padded, shifted, rows, tabs, arrived, listed = refs[16:]
     tau = where_am_i[0]
     core = where_am_i[1]
     view = where_am_i[2]
+    here = where_am_i[3]
+
+    copies = []
+    for spot, chunk in enumerate(chunks):
+        at = spot * 2 * PIECE
+        copies.append(
+            pltpu.make_async_copy(chunk, pieces.at[at : at + 2 * PIECE], arrived.at[spot])
+        )
+        copies[-1].start()
+
+    def home(owner):
+        dz = ((owner >> 3) - (here >> 3)) & 7
+        dx = ((owner >> 1) - (here >> 1)) & 3
+        turn = jnp.where(dx == 0, 0, jnp.where(dx == 3, 1, dx + 1))
+        return dz * 4 + turn
 
     def look(tile, side):
         return jnp.where(tile >= 0, links[jnp.maximum(tile, 0) * 4 + side], -1)
@@ -84,18 +122,27 @@
     stage[...] = jnp.zeros(stage.shape, f32)
     padded[...] = jnp.zeros(padded.shape, f32)
     lane = lax.broadcasted_iota(jnp.int32, (56, 128), 1)
+    for copy in copies:
+        copy.wait()
+    for spot in range(32):
+        cells = pieces[spot * PIECE + 544 : spot * PIECE + 560, :].astype(f32)
+        rows[spot : spot + 1, :] = cells[8:9].astype(jnp.int32)
+    listing = pltpu.make_async_copy(rows, tabs, listed)
+    listing.start()
+    listing.wait()
 
     def put_line(hh, band, column):
         source = tiles[band][column]
         row = hh - 2 if band == 1 else (6 + hh if band == 0 else hh - 10)
-        entry = tabs[jnp.maximum(source, 0) * 8 + row]
-        owner = entry >> 10
-        index = (entry >> 7) & 7
-        start = (entry & 127) + 2
+        known = jnp.maximum(source, 0)
+        spot, column_at = home(known), (known & 1) * 24 + row
+        owner = tabs[spot, column_at]
+        index = tabs[spot, column_at + 8]
+        start = tabs[spot, column_at + 16] + 2
 
         @pl.when((source >= 0) & ((owner & 1) == core))
         def _():
-            base = pl.multiple_of((owner >> 1) * PIECE + index * LINE, 16)
+            base = pl.multiple_of(home(owner) * PIECE + index * LINE, 16)
             padded[8 : 8 + LINE, :] = pieces[pl.ds(base, LINE), :].astype(f32)
             first = (start >> 2) + 7
             turn = (start & 3) * 32
@@ -105,16 +152,13 @@
                 jnp.where(lane >= turn, lower, upper), (128 - turn) & 127, 1
             )
             for dest in range(4):
+                begin = ((view + dest) & 3) * 4
                 if column == 0:
-                    stage[pl.ds(dest * PART + hh, 37, 16), :] = shifted[4 * dest : 4 * dest + 37, :]
+                    stage[pl.ds(dest * PART + hh, 37, 16), :] = shifted[pl.ds(begin, 37), :]
                 elif column == 1:
-                    stage[pl.ds(dest * PART + 37 * 16 + hh, 7, 16), :] = shifted[
-                        4 * dest + 30 : 4 * dest + 37, :
-                    ]
+                    stage[pl.ds(dest * PART + 37 * 16 + hh, 7, 16), :] = shifted[pl.ds(begin + 30, 7), :]
                 else:
-                    stage[pl.ds(dest * PART + 44 * 16 + hh, 7, 16), :] = shifted[
-                        4 * dest : 4 * dest + 7, :
-                    ]
+                    stage[pl.ds(dest * PART + 44 * 16 + hh, 7, 16), :] = shifted[pl.ds(begin, 7), :]
 
     for hh in range(12):
         for column in range(3):
@@ -129,7 +173,7 @@
         return (tile >= 0) & ((tile & 1) == core)
 
     def base_of(tile, extra):
-        return pl.multiple_of((jnp.maximum(tile, 0) >> 1) * PIECE + extra, 16)
+        return pl.multiple_of(home(jnp.maximum(tile, 0)) * PIECE + extra, 16)
 
     @pl.when(mine(halo_center))
     def _():
@@ -167,23 +211,28 @@
     out[...] = stage[...].astype(bf16)
 
 
-def select_pieces(tabs, links, where_am_i, pieces):
+def select_pieces(links, where_am_i, chunks):
     return pl.pallas_call(
         select_body,
         out_shape=jax.ShapeDtypeStruct((4 * PART, 128), bf16),
         grid_spec=pltpu.PrefetchScalarGridSpec(
-            num_scalar_prefetch=3,
+            num_scalar_prefetch=2,
             grid=(1,),
-            in_specs=[pl.BlockSpec(pieces.shape, lambda i, *_: (0, 0))],
+            in_specs=[pl.BlockSpec(memory_space=pl.ANY)] * 16,
             out_specs=pl.BlockSpec((4 * PART, 128), lambda i, *_: (0, 0)),
             scratch_shapes=[
+                pltpu.VMEM((32 * PIECE, 128), bf16),
                 pltpu.VMEM((4 * PART, 128), f32),
                 pltpu.VMEM((88, 128), f32),
                 pltpu.VMEM((56, 128), f32),
+                pltpu.VMEM((32, 128), jnp.int32),
+                pltpu.SMEM((32, 128), jnp.int32),
+                pltpu.SemaphoreType.DMA((16,)),
+                pltpu.SemaphoreType.DMA,
             ],
         ),
         name="select_pieces",
-    )(tabs, links, where_am_i, pieces)
+    )(links, where_am_i, *chunks)
 
 
 def slot_of(block, half):
@@ -195,7 +244,7 @@
 
 
 def volume_body(
-    facts, bands, ref, summing, first, first_bias, second, second_bias, out,
+    facts, band0, band1, band2, band3, ref, summing, first, first_bias, second, second_bias, out,
     turned, refx, factors, sums, padded, hidden, keep, wide,
 ):
     view = facts[0]
@@ -203,11 +252,10 @@
     sub8 = lax.broadcasted_iota(jnp.int32, (8, 128), 0)
 
     def total(slot):
-        cells = bands[slot * 16 : slot * 16 + 16, :].astype(f32)
-        for u in range(1, 4):
-            at = u * PART + slot * 16
-            cells = cells + bands[at : at + 16, :].astype(f32)
-        return cells
+        span = slice(slot * 16, slot * 16 + 16)
+        return (band0[span, :].astype(f32) + band1[span, :].astype(f32)) + (
+            band2[span, :].astype(f32) + band3[span, :].astype(f32)
+        )
 
     lanes = [lane16 >= 32 * m for m in range(4)]
     current = total(0)
@@ -322,7 +370,7 @@
 
 
 def volume(facts, bands, ref, first, first_bias, second, second_bias):
-    operands = (bands, ref, jnp.asarray(group_sum_matrix(), bf16), first, first_bias, second, second_bias)
+    operands = (*bands, ref, jnp.asarray(group_sum_matrix(), bf16), first, first_bias, second, second_bias)
 
     def whole(x):
         return pl.BlockSpec(x.shape, lambda i, *_: (0,) * x.ndim)
@@ -363,39 +411,54 @@
     halo_row = lax.dynamic_slice_in_dim(ref, (view + 6) % 8, 1, axis=0)
     sides = lax.dynamic_slice_in_dim(ref, 2 * view, 2, axis=0)
     sides = jnp.concatenate([sides[:, 0:256], sides[:, 3840:4096]], axis=1)
+    names = jnp.stack([line_owner[0, :, 0], line_index[0], line_offset[0]])
+    names = lax.dynamic_slice_in_dim(names, view * 8, 8, axis=1).astype(bf16).reshape(24)
+    twin = lax.ppermute(names, "c", [(0, 1), (1, 0)])
+    names = jnp.where(core == 0, jnp.concatenate([names, twin]), jnp.concatenate([twin, names]))
     payload = jnp.concatenate(
         [
             lines.reshape(8 * LINE, 128),
             halo_row.reshape(32, 128),
             sides.reshape(8, 128),
-            jnp.zeros((8, 128), bf16),
+            jnp.pad(names[None], ((0, 7), (0, 80))),
         ],
         axis=0,
     )
-    row = lax.all_gather(payload, "x", axis=0, tiled=True)
-    pieces = lax.all_gather(row, "z", axis=0, tiled=True)
-
-    coded = line_owner[0, :, 0] * 1024 + line_index[0] * 128 + line_offset[0]
-    coded = lax.dynamic_slice_in_dim(coded, view * 8, 8)
-    tabs = lax.all_to_all(
-        jnp.broadcast_to(coded[None], (64, 8)), ("z", "x", "c"), split_axis=0, concat_axis=0, tiled=True
-    ).reshape(512)
+    def shift(x, axis, by):
+        count = lax.axis_size(axis)
+        return lax.ppermute(x, axis, [(i, (i + by) % count) for i in range(count)])
+
+    one, two, three = shift(payload, "x", 1), shift(payload, "x", -1), shift(payload, "x", 2)
+    chunks = [[None, None] for _ in range(8)]
+    chunks[0] = [jnp.concatenate([payload, one]), jnp.concatenate([two, three])]
+    for k in range(1, 4):
+        for i in range(2):
+            chunks[-k % 8][i] = shift(chunks[(1 - k) % 8][i], "z", 1)
+            chunks[k][i] = shift(chunks[k - 1][i], "z", -1)
+    chunks[4] = [shift(chunks[5][0], "z", 1), shift(chunks[3][1], "z", -1)]
+    chunks = [chunk for pair in chunks for chunk in pair]
+
     links = neighbours.reshape(256)
 
-    first = spread_first(conv1_weight)
-    second = spread_second(conv2_weight)
+    first, second = spread_weights(conv1_weight, conv2_weight)
     first_bias = jnp.tile(conv1_bias, 16)[None]
     second_bias = jnp.tile(conv2_bias, 8)[None]
     facts = jnp.concatenate([view[None], neighbours[tile]])
     other = tile + 1 - 2 * core
-    tabs, links, first, second, first_bias, second_bias, facts = lax.optimization_barrier(
-        (tabs, links, first, second, first_bias, second_bias, facts)
+    asked = jnp.stack([other, core, view, tile])
+    wanted = jnp.stack([tile, core, view, tile])
+    links, asked, wanted, first, second, first_bias, second_bias, facts = lax.optimization_barrier(
+        (links, asked, wanted, first, second, first_bias, second_bias, facts)
     )
-    theirs = select_pieces(tabs, links, jnp.stack([other, core, view]), pieces)
+    theirs = select_pieces(links, asked, chunks)
     swapped = lax.ppermute(theirs, "c", [(0, 1), (1, 0)])
-    own = select_pieces(tabs, links, jnp.stack([tile, core, view]), pieces)
-    bands = lax.all_to_all(own + swapped, "views", split_axis=0, concat_axis=0, tiled=True)
-
+    own = select_pieces(links, wanted, chunks)
+
+    def part(step):
+        span = slice(step * PART, (step + 1) * PART)
+        return own[span] + swapped[span]
+
+    bands = [part(0)] + [shift(part(step), "views", step) for step in (1, 2, 3)]
     return volume(facts, bands, ref, first, first_bias, second, second_bias)[None]
 
 

time: 148 us -> 122 us (0.82)
  the two profiles are of different devices: /device:TPU:6 before, /device:TPU:1 now
where the time goes in v3:
time: 122 us
  Pallas kernels  40.3 us (33%)
  starting transfers between devices  36.1 us (30%)
  waiting for transfers between devices  35.9 us (29%)
  local copies, waits for them, and re-layouts  5.1 us (4%)
  other arithmetic  4.2 us (3%)
    ppermute x20, waiting for transfers between devices, shift(): return lax.ppermute(x, axis, [(i, (i + by) % count) for i in range(count)])  35.9 us
    ppermute x20, starting transfers between devices, shift(): return lax.ppermute(x, axis, [(i, (i + by) % count) for i in range(count)])  30.8 us
    pallas_call x1, Pallas kernels, volume(): pl.pallas_call(volume_body, out_shape=jax.ShapeDtypeStruct((DL, H, W * CH...  23.2 us
    pallas_call x2, Pallas kernels, select_pieces(): pl.pallas_call(select_body, out_shape=jax.ShapeDtypeStruct((4 * PART, 128...  13.9 us
    ppermute x1, starting transfers between devices, on_device(): twin = lax.ppermute(names, 'c', [(0, 1), (1, 0)])  3.2 us
    pallas_call x1, Pallas kernels, spread_weights(): pl.pallas_call(spread_body, out_shape=(jax.ShapeDtypeStruct((3, 256, 512)...  3.14 us
  transfers between devices with their start and end apart: 22, of which 14 were waited for; matrix products, arithmetic and copies ran while one was open for 4% of the time, Pallas kernels for 8%

profile of v3, /device:TPU:1, one launch (start us, length us, event | category | flops | bytes accessed | tf_op | source)
XLA Modules:
  0.0 121.9 jit_solution(14435170468166325922)
XLA Ops:
  0.9 3.2 %collective-permute-start = (bf16[24]{0:T(256)(128)(2,1)S(1)}, bf16[24]{0:T(256)(128)(2,1)S(1)}, u32[]{:S(2)}, u32[]{:S(2)}) collective-permute-start(bf16[24]{0:T(256)(128)(2,1)S(1)} %reshape.92), channel_id=1, source_target_pairs={{0,4},{4,0},{1,5},{5,1},{2,6},{6,2},{3,7},{7,3},{8,12},{12,8},{9,1... | collective-permute-start | bytes 152 | tf_op jit(solution)/shard_map/ppermute | solution.py:416
  6.4 2.7 %collective-permute-start.2 = (bf16[560,128]{1,0:T(8,128)(2,1)S(1)}, bf16[560,128]{1,0:T(8,128)(2,1)S(1)}, u32[]{:S(2)}, u32[]{:S(2)}) collective-permute-start(bf16[560,128]{1,0:T(8,128)(2,1)S(1)} %pad_maximum_fusion), channel_id=1, source_target_pairs={{0,24},{8,0},{16,8},{24,16},{1,25},{9,1},{17,9},{25,17},{2,26},{10... | collective-permute-start | bytes 430088 | tf_op jit(solution)/shard_map/ppermute | solution.py:429
  9.1 3.8 %collective-permute-done.1 = bf16[560,128]{1,0:T(8,128)(2,1)S(1)} collective-permute-done((bf16[560,128]{1,0:T(8,128)(2,1)S(1)}, bf16[560,128]{1,0:T(8,128)(2,1)S(1)}, u32[]{:S(2)}, u32[]{:S(2)}) %collective-permute-start.1) | collective-permute-done | bytes 143392 | tf_op jit(solution)/shard_map/ppermute | solution.py:429
  15.4 5.5 %collective-permute-start.5 = (bf16[1120,128]{1,0:T(8,128)(2,1)S(1)}, bf16[1120,128]{1,0:T(8,128)(2,1)S(1)}, u32[]{:S(2)}, u32[]{:S(2)}) collective-permute-start(bf16[1120,128]{1,0:T(8,128)(2,1)S(1)} %constant_dynamic-update-slice_fusion.5.refs_1_), channel_id=1, source_target_pairs={{0,224},{32,0},{64,32},{96,64},{128,96},{160,128},{192,160},{224,1... | collective-permute-start | bytes 860168 | tf_op jit(solution)/shard_map/ppermute | solution.py:429
  23.2 3.0 %collective-permute-done.5.refs_3_ = bf16[1120,128]{1,0:T(8,128)(2,1)S(1)} collective-permute-done((bf16[1120,128]{1,0:T(8,128)(2,1)S(1)}, bf16[1120,128]{1,0:T(8,128)(2,1)S(1)}, u32[]{:S(2)}, u32[]{:S(2)}) %collective-permute-start.5) | collective-permute-done | bytes 286752 | tf_op jit(solution)/shard_map/ppermute | solution.py:429
  26.2 3.4 %collective-permute-start.7 = (bf16[1120,128]{1,0:T(8,128)(2,1)S(1)}, bf16[1120,128]{1,0:T(8,128)(2,1)S(1)}, u32[]{:S(2)}, u32[]{:S(2)}) collective-permute-start(bf16[1120,128]{1,0:T(8,128)(2,1)S(1)} %collective-permute-done.5.refs_3_), channel_id=1, source_target_pairs={{0,224},{32,0},{64,32},{96,64},{128,96},{160,128},{192,160},{224,1... | collective-permute-start | bytes 860168 | tf_op jit(solution)/shard_map/ppermute | solution.py:429
  29.6 2.7 %collective-permute-done.4.refs_2_ = bf16[1120,128]{1,0:T(8,128)(2,1)S(1)} collective-permute-done((bf16[1120,128]{1,0:T(8,128)(2,1)S(1)}, bf16[1120,128]{1,0:T(8,128)(2,1)S(1)}, u32[]{:S(2)}, u32[]{:S(2)}) %collective-permute-start.4) | collective-permute-done | bytes 286752 | tf_op jit(solution)/shard_map/ppermute | solution.py:429
  32.4 3.4 %collective-permute-start.6 = (bf16[1120,128]{1,0:T(8,128)(2,1)S(1)}, bf16[1120,128]{1,0:T(8,128)(2,1)S(1)}, u32[]{:S(2)}, u32[]{:S(2)}) collective-permute-start(bf16[1120,128]{1,0:T(8,128)(2,1)S(1)} %collective-permute-done.4.refs_2_), channel_id=1, source_target_pairs={{0,224},{32,0},{64,32},{96,64},{128,96},{160,128},{192,160},{224,1... | collective-permute-start | bytes 860168 | tf_op jit(solution)/shard_map/ppermute | solution.py:429
  36.0 2.6 %collective-permute-done.7.refs_5_ = bf16[1120,128]{1,0:T(8,128)(2,1)S(1)} collective-permute-done((bf16[1120,128]{1,0:T(8,128)(2,1)S(1)}, bf16[1120,128]{1,0:T(8,128)(2,1)S(1)}, u32[]{:S(2)}, u32[]{:S(2)}) %collective-permute-start.7) | collective-permute-done | bytes 286752 | tf_op jit(solution)/shard_map/ppermute | solution.py:429
  38.5 3.4 %collective-permute-start.9 = (bf16[1120,128]{1,0:T(8,128)(2,1)S(1)}, bf16[1120,128]{1,0:T(8,128)(2,1)}, u32[]{:S(2)}, u32[]{:S(2)}) collective-permute-start(bf16[1120,128]{1,0:T(8,128)(2,1)S(1)} %collective-permute-done.7.refs_5_), channel_id=1, source_target_pairs={{0,224},{32,0},{64,32},{96,64},{128,96},{160,128},{192,160},{224,1... | collective-permute-start | bytes 860168 | tf_op jit(solution)/shard_map/ppermute | solution.py:429
  41.9 2.7 %collective-permute-done.6.refs_4_ = bf16[1120,128]{1,0:T(8,128)(2,1)S(1)} collective-permute-done((bf16[1120,128]{1,0:T(8,128)(2,1)S(1)}, bf16[1120,128]{1,0:T(8,128)(2,1)S(1)}, u32[]{:S(2)}, u32[]{:S(2)}) %collective-permute-start.6) | collective-permute-done | bytes 286752 | tf_op jit(solution)/shard_map/ppermute | solution.py:429
  44.7 3.4 %collective-permute-start.8 = (bf16[1120,128]{1,0:T(8,128)(2,1)S(1)}, bf16[1120,128]{1,0:T(8,128)(2,1)}, u32[]{:S(2)}, u32[]{:S(2)}) collective-permute-start(bf16[1120,128]{1,0:T(8,128)(2,1)S(1)} %collective-permute-done.6.refs_4_), channel_id=1, source_target_pairs={{0,224},{32,0},{64,32},{96,64},{128,96},{160,128},{192,160},{224,1... | collective-permute-start | bytes 860168 | tf_op jit(solution)/shard_map/ppermute | solution.py:429
  48.2 2.6 %collective-permute-done.9.refs_7_ = bf16[1120,128]{1,0:T(8,128)(2,1)} collective-permute-done((bf16[1120,128]{1,0:T(8,128)(2,1)S(1)}, bf16[1120,128]{1,0:T(8,128)(2,1)}, u32[]{:S(2)}, u32[]{:S(2)}) %collective-permute-start.9) | collective-permute-done | bytes 286752 | tf_op jit(solution)/shard_map/ppermute | solution.py:429
  50.8 3.5 %collective-permute-start.14 = (bf16[1120,128]{1,0:T(8,128)(2,1)}, bf16[1120,128]{1,0:T(8,128)(2,1)}, u32[]{:S(2)}, u32[]{:S(2)}) collective-permute-start(bf16[1120,128]{1,0:T(8,128)(2,1)} %collective-permute-done.9.refs_7_), channel_id=1, source_target_pairs={{0,224},{32,0},{64,32},{96,64},{128,96},{160,128},{192,160},{224,1... | collective-permute-start | bytes 860168 | tf_op jit(solution)/shard_map/ppermute | solution.py:429
  56.6 3.1 %spread_weights.1 = (bf16[3,256,512]{2,1,0:T(8,128)(2,1)}, bf16[3,1024,256]{2,1,0:T(8,128)(2,1)}) custom-call(bf16[216,32]{1,0:T(8,128)(2,1)} %bitcast.19, bf16[864,32]{1,0:T(8,128)(2,1)} %bitcast.16), custom_call_target="tpu_custom_call" | custom-call | tf_op jit(solution)/shard_map/spread_weights/pallas_call | solution.py:81
  60.9 2.3 %collective-permute-done.14.refs_9_ = bf16[1120,128]{1,0:T(8,128)(2,1)} collective-permute-done((bf16[1120,128]{1,0:T(8,128)(2,1)}, bf16[1120,128]{1,0:T(8,128)(2,1)}, u32[]{:S(2)}, u32[]{:S(2)}) %collective-permute-start.14) | collective-permute-done | bytes 286752 | tf_op jit(solution)/shard_map/ppermute | solution.py:429
  63.3 6.7 %select_pieces.3 = bf16[3520,128]{1,0:T(8,128)(2,1)} custom-call(s32[256]{0:T(256)} %reshape.86.links, s32[4]{0:T(128)} %get-tuple-element.20.where_am_i, bf16[1120,128]{1,0:T(8,128)(2,1)} %copy-done.2, bf16[1120,128]{1,0:T(8,128)(2,1)} %copy-done.1, bf16[1120,128]{1,0:T(8,128)(2,1)} %copy-done.5, bf16[1120,128]{1,0:T(8,128)(2,1)} %copy-done.4, ...), custom_call_target="tpu_custom_call" | custom-call | tf_op jit(solution)/shard_map/select_pieces/pallas_call | solution.py:215
  70.0 2.1 %collective-permute-start.18 = (bf16[3520,128]{1,0:T(8,128)(2,1)}, bf16[3520,128]{1,0:T(8,128)(2,1)S(1)}, u32[]{:S(2)}, u32[]{:S(2)}) collective-permute-start(bf16[3520,128]{1,0:T(8,128)(2,1)} %select_pieces.3), channel_id=1, source_target_pairs={{0,4},{4,0},{1,5},{5,1},{2,6},{6,2},{3,7},{7,3},{8,12},{12,8},{9,1... | collective-permute-start | bytes 2703368 | tf_op jit(solution)/shard_map/ppermute | solution.py:454
  72.1 7.2 %select_pieces.2 = bf16[3520,128]{1,0:T(8,128)(2,1)} custom-call(s32[256]{0:T(256)} %reshape.86.links, s32[4]{0:T(128)} %get-tuple-element.19.where_am_i, bf16[1120,128]{1,0:T(8,128)(2,1)} %copy-done.2, bf16[1120,128]{1,0:T(8,128)(2,1)} %copy-done.1, bf16[1120,128]{1,0:T(8,128)(2,1)} %copy-done.5, bf16[1120,128]{1,0:T(8,128)(2,1)} %copy-done.4, ...), custom_call_target="tpu_custom_call" | custom-call | tf_op jit(solution)/shard_map/select_pieces/pallas_call | solution.py:215
  79.4 2.1 %slice_add_fusion = (bf16[880,128]{1,0:T(8,128)(2,1)S(1)}, bf16[880,128]{1,0:T(8,128)(2,1)S(1)}, bf16[880,128]{1,0:T(8,128)(2,1)S(1)}, bf16[880,128]{1,0:T(8,128)(2,1)}) fusion(bf16[3520,128]{1,0:T(8,128)(2,1)S(1)} %collective-permute-done.18, bf16[3520,128]{1,0:T(8,128)(2,1)} %select_pieces.2), kind=kLoop, calls=%fused_computation | loop fusion | flops 450560 | bytes 2703360 | tf_op jit(solution)/shard_map/add | solution.py:459
  81.4 2.7 %collective-permute-start.21 = (bf16[880,128]{1,0:T(8,128)(2,1)S(1)}, bf16[880,128]{1,0:T(8,128)(2,1)S(1)}, u32[]{:S(2)}, u32[]{:S(2)}) collective-permute-start(bf16[880,128]{1,0:T(8,128)(2,1)S(1)} %get-tuple-element.25), channel_id=1, source_target_pairs={{0,3},{1,0},{2,1},{3,2},{4,7},{5,4},{6,5},{7,6},{8,11},{9,8},{10,9... | collective-permute-start | bytes 675848 | tf_op jit(solution)/shard_map/ppermute | solution.py:429
  85.2 8.7 %collective-permute-done.21.band3 = bf16[880,128]{1,0:T(8,128)(2,1)S(1)} collective-permute-done((bf16[880,128]{1,0:T(8,128)(2,1)S(1)}, bf16[880,128]{1,0:T(8,128)(2,1)S(1)}, u32[]{:S(2)}, u32[]{:S(2)}) %collective-permute-start.21) | collective-permute-done | bytes 225312 | tf_op jit(solution)/shard_map/ppermute | solution.py:429
  93.9 4.1 %collective-permute-done.19.band1 = bf16[880,128]{1,0:T(8,128)(2,1)S(1)} collective-permute-done((bf16[880,128]{1,0:T(8,128)(2,1)S(1)}, bf16[880,128]{1,0:T(8,128)(2,1)S(1)}, u32[]{:S(2)}, u32[]{:S(2)}) %collective-permute-start.19) | collective-permute-done | bytes 225312 | tf_op jit(solution)/shard_map/ppermute | solution.py:429
  98.7 23.2 %volume.1 = f32[16,8,4096]{2,1,0:T(8,128)} custom-call(s32[5]{0:T(128)} %pad_add_fusion.1.facts, bf16[880,128]{1,0:T(8,128)(2,1)} %get-tuple-element.28.band0, bf16[880,128]{1,0:T(8,128)(2,1)} %copy-done.13, bf16[880,128]{1,0:T(8,128)(2,1)} %copy-done.12, bf16[880,128]{1,0:T(8,128)(2,1)} %copy-done.11, bf16[8,4096]{1,0:T(8,128)(2,1)} %bitcast.17, ...), custom_call_target="tpu_custom_call" | custom-call | tf_op jit(solution)/shard_map/volume/pallas_call | solution.py:378
  (88 shorter events, 13.4 us)
Async XLA Ops:
  0.0 54.6 %copy-start.15 = (f32[32]{0:T(128)S(1)}, f32[32]{0:T(128)}, u32[]{:S(2)}) copy-start(f32[32]{0:T(128)} %param.20) | copy-start | bytes 388
  0.0 55.3 %copy-start.16 = (f32[32]{0:T(128)S(1)}, f32[32]{0:T(128)}, u32[]{:S(2)}) copy-start(f32[32]{0:T(128)} %param.18) | copy-start | bytes 388
  0.9 5.3 %collective-permute-start = (bf16[24]{0:T(256)(128)(2,1)S(1)}, bf16[24]{0:T(256)(128)(2,1)S(1)}, u32[]{:S(2)}, u32[]{:S(2)}) collective-permute-start(bf16[24]{0:T(256)(128)(2,1)S(1)} %reshape.92), channel_id=1, source_target_pairs={{0,4},{4,0},{1,5},{5,1},{2,6},{6,2},{3,7},{7,3},{8,12},{12,8},{9,1... | collective-permute-start | bytes 152 | tf_op jit(solution)/shard_map/ppermute | solution.py:416
  6.3 6.6 %collective-permute-start.1 = (bf16[560,128]{1,0:T(8,128)(2,1)S(1)}, bf16[560,128]{1,0:T(8,128)(2,1)S(1)}, u32[]{:S(2)}, u32[]{:S(2)}) collective-permute-start(bf16[560,128]{1,0:T(8,128)(2,1)S(1)} %pad_maximum_fusion), channel_id=1, source_target_pairs={{0,8},{8,16},{16,24},{24,0},{1,9},{9,17},{17,25},{25,1},{2,10},{10... | collective-permute-start | bytes 430088 | tf_op jit(solution)/shard_map/ppermute | solution.py:429
  6.4 8.4 %collective-permute-start.2 = (bf16[560,128]{1,0:T(8,128)(2,1)S(1)}, bf16[560,128]{1,0:T(8,128)(2,1)S(1)}, u32[]{:S(2)}, u32[]{:S(2)}) collective-permute-start(bf16[560,128]{1,0:T(8,128)(2,1)S(1)} %pad_maximum_fusion), channel_id=1, source_target_pairs={{0,24},{8,0},{16,8},{24,16},{1,25},{9,1},{17,9},{25,17},{2,26},{10... | collective-permute-start | bytes 430088 | tf_op jit(solution)/shard_map/ppermute | solution.py:429
  9.1 6.3 %collective-permute-start.3 = (bf16[560,128]{1,0:T(8,128)(2,1)S(1)}, bf16[560,128]{1,0:T(8,128)(2,1)S(1)}, u32[]{:S(2)}, u32[]{:S(2)}) collective-permute-start(bf16[560,128]{1,0:T(8,128)(2,1)S(1)} %pad_maximum_fusion), channel_id=1, source_target_pairs={{0,16},{8,24},{16,0},{24,8},{1,17},{9,25},{17,1},{25,9},{2,18},{10... | collective-permute-start | bytes 430088 | tf_op jit(solution)/shard_map/ppermute | solution.py:429
  12.9 10.3 %collective-permute-start.10 = (bf16[1120,128]{1,0:T(8,128)(2,1)S(1)}, bf16[1120,128]{1,0:T(8,128)(2,1)S(1)}, u32[]{:S(2)}, u32[]{:S(2)}) collective-permute-start(bf16[1120,128]{1,0:T(8,128)(2,1)S(1)} %constant_dynamic-update-slice_fusion.refs_0_), channel_id=1, source_target_pairs={{0,32},{32,64},{64,96},{96,128},{128,160},{160,192},{192,224},{224... | collective-permute-start | bytes 860168 | tf_op jit(solution)/shard_map/ppermute | solution.py:429
  15.4 10.8 %collective-permute-start.5 = (bf16[1120,128]{1,0:T(8,128)(2,1)S(1)}, bf16[1120,128]{1,0:T(8,128)(2,1)S(1)}, u32[]{:S(2)}, u32[]{:S(2)}) collective-permute-start(bf16[1120,128]{1,0:T(8,128)(2,1)S(1)} %constant_dynamic-update-slice_fusion.5.refs_1_), channel_id=1, source_target_pairs={{0,224},{32,0},{64,32},{96,64},{128,96},{160,128},{192,160},{224,1... | collective-permute-start | bytes 860168 | tf_op jit(solution)/shard_map/ppermute | solution.py:429
  20.9 11.4 %collective-permute-start.4 = (bf16[1120,128]{1,0:T(8,128)(2,1)S(1)}, bf16[1120,128]{1,0:T(8,128)(2,1)S(1)}, u32[]{:S(2)}, u32[]{:S(2)}) collective-permute-start(bf16[1120,128]{1,0:T(8,128)(2,1)S(1)} %constant_dynamic-update-slice_fusion.refs_0_), channel_id=1, source_target_pairs={{0,224},{32,0},{64,32},{96,64},{128,96},{160,128},{192,160},{224,1... | collective-permute-start | bytes 860168 | tf_op jit(solution)/shard_map/ppermute | solution.py:429
  21.7 14.1 %collective-permute-start.15 = (bf16[1120,128]{1,0:T(8,128)(2,1)S(1)}, bf16[1120,128]{1,0:T(8,128)(2,1)S(1)}, u32[]{:S(2)}, u32[]{:S(2)}) collective-permute-start(bf16[1120,128]{1,0:T(8,128)(2,1)S(1)} %constant_dynamic-update-slice_fusion.5.refs_1_), channel_id=1, source_target_pairs={{0,32},{32,64},{64,96},{96,128},{128,160},{160,192},{192,224},{224... | collective-permute-start | bytes 860168 | tf_op jit(solution)/shard_map/ppermute | solution.py:429
  23.2 12.8 %collective-permute-start.11 = (bf16[1120,128]{1,0:T(8,128)(2,1)S(1)}, bf16[1120,128]{1,0:T(8,128)(2,1)S(1)}, u32[]{:S(2)}, u32[]{:S(2)}) collective-permute-start(bf16[1120,128]{1,0:T(8,128)(2,1)S(1)} %collective-permute-done.10.refs_14_), channel_id=1, source_target_pairs={{0,32},{32,64},{64,96},{96,128},{128,160},{160,192},{192,224},{224... | collective-permute-start | bytes 860168 | tf_op jit(solution)/shard_map/ppermute | solution.py:429
  26.2 12.3 %collective-permute-start.7 = (bf16[1120,128]{1,0:T(8,128)(2,1)S(1)}, bf16[1120,128]{1,0:T(8,128)(2,1)S(1)}, u32[]{:S(2)}, u32[]{:S(2)}) collective-permute-start(bf16[1120,128]{1,0:T(8,128)(2,1)S(1)} %collective-permute-done.5.refs_3_), channel_id=1, source_target_pairs={{0,224},{32,0},{64,32},{96,64},{128,96},{160,128},{192,160},{224,1... | collective-permute-start | bytes 860168 | tf_op jit(solution)/shard_map/ppermute | solution.py:429
  32.4 12.3 %collective-permute-start.6 = (bf16[1120,128]{1,0:T(8,128)(2,1)S(1)}, bf16[1120,128]{1,0:T(8,128)(2,1)S(1)}, u32[]{:S(2)}, u32[]{:S(2)}) collective-permute-start(bf16[1120,128]{1,0:T(8,128)(2,1)S(1)} %collective-permute-done.4.refs_2_), channel_id=1, source_target_pairs={{0,224},{32,0},{64,32},{96,64},{128,96},{160,128},{192,160},{224,1... | collective-permute-start | bytes 860168 | tf_op jit(solution)/shard_map/ppermute | solution.py:429
  35.8 12.3 %collective-permute-start.16 = (bf16[1120,128]{1,0:T(8,128)(2,1)S(1)}, bf16[1120,128]{1,0:T(8,128)(2,1)S(1)}, u32[]{:S(2)}, u32[]{:S(2)}) collective-permute-start(bf16[1120,128]{1,0:T(8,128)(2,1)S(1)} %collective-permute-done.15.refs_15_), channel_id=1, source_target_pairs={{0,32},{32,64},{64,96},{96,128},{128,160},{160,192},{192,224},{224... | collective-permute-start | bytes 860168 | tf_op jit(solution)/shard_map/ppermute | solution.py:429
  36.0 12.2 %collective-permute-start.12 = (bf16[1120,128]{1,0:T(8,128)(2,1)S(1)}, bf16[1120,128]{1,0:T(8,128)(2,1)}, u32[]{:S(2)}, u32[]{:S(2)}) collective-permute-start(bf16[1120,128]{1,0:T(8,128)(2,1)S(1)} %collective-permute-done.11.refs_12_), channel_id=1, source_target_pairs={{0,32},{32,64},{64,96},{96,128},{128,160},{160,192},{192,224},{224... | collective-permute-start | bytes 860168 | tf_op jit(solution)/shard_map/ppermute | solution.py:429
  38.5 12.3 %collective-permute-start.9 = (bf16[1120,128]{1,0:T(8,128)(2,1)S(1)}, bf16[1120,128]{1,0:T(8,128)(2,1)}, u32[]{:S(2)}, u32[]{:S(2)}) collective-permute-start(bf16[1120,128]{1,0:T(8,128)(2,1)S(1)} %collective-permute-done.7.refs_5_), channel_id=1, source_target_pairs={{0,224},{32,0},{64,32},{96,64},{128,96},{160,128},{192,160},{224,1... | collective-permute-start | bytes 860168 | tf_op jit(solution)/shard_map/ppermute | solution.py:429
  44.7 16.3 %collective-permute-start.8 = (bf16[1120,128]{1,0:T(8,128)(2,1)S(1)}, bf16[1120,128]{1,0:T(8,128)(2,1)}, u32[]{:S(2)}, u32[]{:S(2)}) collective-permute-start(bf16[1120,128]{1,0:T(8,128)(2,1)S(1)} %collective-permute-done.6.refs_4_), channel_id=1, source_target_pairs={{0,224},{32,0},{64,32},{96,64},{128,96},{160,128},{192,160},{224,1... | collective-permute-start | bytes 860168 | tf_op jit(solution)/shard_map/ppermute | solution.py:429
  48.1 12.9 %collective-permute-start.17 = (bf16[1120,128]{1,0:T(8,128)(2,1)S(1)}, bf16[1120,128]{1,0:T(8,128)(2,1)}, u32[]{:S(2)}, u32[]{:S(2)}) collective-permute-start(bf16[1120,128]{1,0:T(8,128)(2,1)S(1)} %collective-permute-done.16.refs_13_), channel_id=1, source_target_pairs={{0,32},{32,64},{64,96},{96,128},{128,160},{160,192},{192,224},{224... | collective-permute-start | bytes 860168 | tf_op jit(solution)/shard_map/ppermute | solution.py:429
  48.2 12.8 %collective-permute-start.13 = (bf16[1120,128]{1,0:T(8,128)(2,1)}, bf16[1120,128]{1,0:T(8,128)(2,1)}, u32[]{:S(2)}, u32[]{:S(2)}) collective-permute-start(bf16[1120,128]{1,0:T(8,128)(2,1)} %collective-permute-done.12.refs_10_), channel_id=1, source_target_pairs={{0,32},{32,64},{64,96},{96,128},{128,160},{160,192},{192,224},{224... | collective-permute-start | bytes 860168 | tf_op jit(solution)/shard_map/ppermute | solution.py:429
  50.8 12.4 %collective-permute-start.14 = (bf16[1120,128]{1,0:T(8,128)(2,1)}, bf16[1120,128]{1,0:T(8,128)(2,1)}, u32[]{:S(2)}, u32[]{:S(2)}) collective-permute-start(bf16[1120,128]{1,0:T(8,128)(2,1)} %collective-permute-done.9.refs_7_), channel_id=1, source_target_pairs={{0,224},{32,0},{64,32},{96,64},{128,96},{160,128},{192,160},{224,1... | collective-permute-start | bytes 860168 | tf_op jit(solution)/shard_map/ppermute | solution.py:429
  70.0 9.4 %collective-permute-start.18 = (bf16[3520,128]{1,0:T(8,128)(2,1)}, bf16[3520,128]{1,0:T(8,128)(2,1)S(1)}, u32[]{:S(2)}, u32[]{:S(2)}) collective-permute-start(bf16[3520,128]{1,0:T(8,128)(2,1)} %select_pieces.3), channel_id=1, source_target_pairs={{0,4},{4,0},{1,5},{5,1},{2,6},{6,2},{3,7},{7,3},{8,12},{12,8},{9,1... | collective-permute-start | bytes 2703368 | tf_op jit(solution)/shard_map/ppermute | solution.py:454
  81.4 12.4 %collective-permute-start.21 = (bf16[880,128]{1,0:T(8,128)(2,1)S(1)}, bf16[880,128]{1,0:T(8,128)(2,1)S(1)}, u32[]{:S(2)}, u32[]{:S(2)}) collective-permute-start(bf16[880,128]{1,0:T(8,128)(2,1)S(1)} %get-tuple-element.25), channel_id=1, source_target_pairs={{0,3},{1,0},{2,1},{3,2},{4,7},{5,4},{6,5},{7,6},{8,11},{9,8},{10,9... | collective-permute-start | bytes 675848 | tf_op jit(solution)/shard_map/ppermute | solution.py:429
  84.2 9.7 %collective-permute-start.20 = (bf16[880,128]{1,0:T(8,128)(2,1)S(1)}, bf16[880,128]{1,0:T(8,128)(2,1)S(1)}, u32[]{:S(2)}, u32[]{:S(2)}) collective-permute-start(bf16[880,128]{1,0:T(8,128)(2,1)S(1)} %get-tuple-element.26), channel_id=1, source_target_pairs={{0,2},{1,3},{2,0},{3,1},{4,6},{5,7},{6,4},{7,5},{8,10},{9,11},{10,... | collective-permute-start | bytes 675848 | tf_op jit(solution)/shard_map/ppermute | solution.py:429
  84.5 13.5 %collective-permute-start.19 = (bf16[880,128]{1,0:T(8,128)(2,1)S(1)}, bf16[880,128]{1,0:T(8,128)(2,1)S(1)}, u32[]{:S(2)}, u32[]{:S(2)}) collective-permute-start(bf16[880,128]{1,0:T(8,128)(2,1)S(1)} %get-tuple-element.27), channel_id=1, source_target_pairs={{0,1},{1,2},{2,3},{3,0},{4,5},{5,6},{6,7},{7,4},{8,9},{9,10},{10,1... | collective-permute-start | bytes 675848 | tf_op jit(solution)/shard_map/ppermute | solution.py:429
  (15 other events, 388.5 us)

commit v4 on v3

v4 whole, which is shorter than its diff:
```python
import jax
import jax.numpy as jnp
import numpy as np
from jax import lax
from jax.experimental import pallas as pl
from jax.experimental.pallas import tpu as pltpu
from jax.sharding import Mesh, PartitionSpec as P

C = 32
G = 8
CH = 32
NDISP = 64
W = 128
NPV = 4
H = 8
LINE = 64
PIECE = 560
SLOTS = 55
PART = SLOTS * 16
BLOCKS = 18
ROWS = BLOCKS * 16
DL = 16
ZB, XB, CB = 8, 4, 2

bf16 = jnp.bfloat16
f32 = jnp.float32


def group_sum_matrix():
    table = np.zeros((256, 256), np.float32)
    for j in range(8):
        for ch in range(C):
            row, g = j * C + ch, ch // 4
            for b in range(3):
                table[row, b * 64 + j * G + g] = 1.0 / 16
                if j == 7:
                    table[row, 192 + b * 16 + g] = 1.0 / 16
                if j == 0:
                    table[row, 192 + b * 16 + 8 + g] = 1.0 / 16
    return np.concatenate([table, table], axis=0)


def spread_body(k1, k2, first, second):
    def repeat(cells, count):
        row = lax.broadcasted_iota(jnp.int32, (CH, count * CH), 0)
        lane = lax.broadcasted_iota(jnp.int32, (CH, count * CH), 1)
        copies = jnp.where((lane & 31) == row, 1.0, 0.0).astype(bf16)
        return jnp.dot(cells, copies, preferred_element_type=f32)

    wide1 = repeat(k1[...], 8)
    wide2 = repeat(k2[...], 8)
    lane1 = lax.broadcasted_iota(jnp.int32, (8, 256), 1) >> 5
    lane2 = lax.broadcasted_iota(jnp.int32, (CH, 256), 1) >> 5

    def line(cells, depth, a, b, j, col):
        result = jnp.zeros(col.shape, f32)
        for e in range(3):
            at = ((a * 3 + b) * 3 + e) * depth
            result = jnp.where(col == j + 1 - e, cells[at : at + depth], result)
        return result

    for a in range(3):
        for b in range(3):
            for j in range(0, 8, 2):
                pair = [line(wide1, G, a, b, j + i, lane1) for i in range(2)]
                first[a, b * 64 + j * 8 : b * 64 + j * 8 + 16, :] = jnp.concatenate(pair, 0).astype(bf16)
            pair = [line(wide1, G, a, b, j, lane1) for j in (-1, 8)]
            first[a, 192 + b * 16 : 208 + b * 16, :] = jnp.concatenate(pair, 0).astype(bf16)
            for j in range(8):
                at = b * 256 + j * 32
                second[a, at : at + 32, :] = line(wide2, CH, a, b, j, lane2).astype(bf16)
            for side, j in enumerate((-1, 8)):
                at = 768 + b * 64 + side * 32
                second[a, at : at + 32, :] = line(wide2, CH, a, b, j, lane2).astype(bf16)
        first[a, 240:256, :] = jnp.zeros((16, 256), bf16)
        second[a, 960:1024, :] = jnp.zeros((64, 256), bf16)


def spread_weights(k1, k2):
    return pl.pallas_call(
        spread_body,
        out_shape=(
            jax.ShapeDtypeStruct((3, 256, 256), bf16),
            jax.ShapeDtypeStruct((3, 1024, 256), bf16),
        ),
        name="spread_weights",
    )(k1.reshape(27 * G, CH), k2.reshape(27 * CH, CH))


def near(x):
    return pltpu.with_memory_space_constraint(x, pltpu.VMEM)


def merge_body(*refs):
    chunks, out, arrived = refs[:14], refs[14], refs[15]
    copies = []
    for spot, chunk in enumerate(chunks):
        at = spot * 2 * PIECE
        copies.append(pltpu.make_async_copy(chunk, out.at[at : at + 2 * PIECE], arrived.at[spot]))
        copies[-1].start()
    for copy in copies:
        copy.wait()


def merge_chunks(chunks):
    return pl.pallas_call(
        merge_body,
        out_shape=pltpu.VMEM((28 * PIECE, 128), bf16),
        compiler_params=pltpu.CompilerParams(vmem_limit_bytes=1 << 20),
        in_specs=[pl.BlockSpec(memory_space=pl.ANY)] * 14,
        out_specs=pl.BlockSpec(memory_space=pltpu.VMEM),
        scratch_shapes=[pltpu.SemaphoreType.DMA((14,))],
        name="merge_chunks",
    )(*chunks)


BUFFERS = 6


def select_body(links, where_am_i, *refs):
    early, late0, late1, out, stage, rows, tabs, listed = refs[:8]
    padded_all = refs[8 : 8 + BUFFERS]
    shifted_all = refs[8 + BUFFERS :]
    tau = where_am_i[0]
    core = where_am_i[1]
    view = where_am_i[2]
    here = where_am_i[3]

    def home(owner):
        dz = ((owner >> 3) - (here >> 3)) & 7
        dx = ((owner >> 1) - (here >> 1)) & 3
        turn = jnp.where(dx == 0, 0, jnp.where(dx == 3, 1, dx + 1))
        return (dz - (dz > 4).astype(jnp.int32)) * 4 + turn + jnp.where(dz == 4, 12, 0)

    def fetch(spot, extra, size):
        late = jnp.maximum(spot - 28, 0)
        near = pl.multiple_of(jnp.minimum(spot, 27) * PIECE + extra, 16)
        far = pl.multiple_of((late & 1) * PIECE + extra, 16)
        cells = jnp.where(late < 2, late0[pl.ds(far, size), :].astype(f32), late1[pl.ds(far, size), :].astype(f32))
        return jnp.where(spot < 28, early[pl.ds(near, size), :].astype(f32), cells)

    def look(tile, side):
        return jnp.where(tile >= 0, links[jnp.maximum(tile, 0) * 4 + side], -1)

    up, down, left, right = [links[tau * 4 + side] for side in range(4)]
    tiles = [
        [up, look(left, 0), look(right, 0)],
        [tau, left, right],
        [down, look(left, 1), look(right, 1)],
    ]
    for padded in padded_all:
        padded[0:8, :] = jnp.zeros((8, 128), f32)
        padded[72:88, :] = jnp.zeros((16, 128), f32)
    for slot in range(4 * SLOTS):
        stage[slot * 16 + 8 : slot * 16 + 16, :] = jnp.zeros((8, 128), f32)
        if slot % SLOTS >= 51:
            stage[slot * 16 : slot * 16 + 8, :] = jnp.zeros((8, 128), f32)
    lane = lax.broadcasted_iota(jnp.int32, (56, 128), 1)
    for spot in range(32):
        source = early if spot < 28 else (late0 if spot < 30 else late1)
        at = (spot if spot < 28 else spot & 1) * PIECE + 544
        cells = source[at : at + 16, :].astype(f32)
        rows[spot : spot + 1, :] = cells[8:9].astype(jnp.int32)
    listing = pltpu.make_async_copy(rows, tabs, listed)
    listing.start()
    listing.wait()

    def put_line(hh, band, column, number):
        padded, shifted = padded_all[number % BUFFERS], shifted_all[number % BUFFERS]
        source = tiles[band][column]
        row = hh - 2 if band == 1 else (6 + hh if band == 0 else hh - 10)
        known = jnp.maximum(source, 0)
        spot, column_at = home(known), (known & 1) * 24 + row
        owner = tabs[spot, column_at]
        index = tabs[spot, column_at + 8]
        start = tabs[spot, column_at + 16] + 2
        usable = (source >= 0) & ((owner & 1) == core)
        cells = fetch(home(owner), index * LINE, LINE)
        padded[8 : 8 + LINE, :] = jnp.where(usable, cells, 0.0)
        first = (start >> 2) + 7
        turn = (start & 3) * 32
        lower = padded[pl.ds(first, 56), :]
        upper = padded[pl.ds(first + 1, 56), :]
        shifted[...] = pltpu.roll(jnp.where(lane >= turn, lower, upper), (128 - turn) & 127, 1)
        for dest in range(4):
            begin = ((view + dest) & 3) * 4
            if column == 0:
                stage[pl.ds(dest * PART + hh, 37, 16), :] = shifted[pl.ds(begin, 37), :]
            elif column == 1:
                stage[pl.ds(dest * PART + 37 * 16 + hh, 7, 16), :] = shifted[pl.ds(begin + 30, 7), :]
            else:
                stage[pl.ds(dest * PART + 44 * 16 + hh, 7, 16), :] = shifted[pl.ds(begin, 7), :]

    for hh in range(12):
        for column in range(3):
            put_line(hh, 0 if hh < 2 else (1 if hh < 10 else 2), column, hh * 3 + column)

    above = view < 2
    halo = [jnp.where(above, tiles[0][k], tiles[2][k]) for k in range(3)]
    halo_row = jnp.where(above, view, view + 8)

    def features(tile, extra, size):
        cells = fetch(home(jnp.maximum(tile, 0)), extra, size)
        return jnp.where((tile >= 0) & ((tile & 1) == core), cells, 0.0)

    cells = features(halo[0], 512, 32)
    for dest in range(4):
        stage[pl.ds(dest * PART + 12 + view, 32, 16), :] = cells

    def put_pair(cells, slot, row):
        for dest in range(4):
            for k in range(2):
                stage[pl.ds(dest * PART + (slot + k) * 16 + row, 1), :] = cells[k : k + 1]

    put_pair(features(halo[1], 528, 16)[14:16], 51, halo_row)
    put_pair(features(halo[2], 512, 16)[0:2], 53, halo_row)
    left_cells = features(left, 544, 16)
    right_cells = features(right, 544, 16)
    for k in range(2):
        put_pair(left_cells[4 * k + 2 : 4 * k + 4], 51, 2 + 2 * view + k)
        put_pair(right_cells[4 * k : 4 * k + 2], 53, 2 + 2 * view + k)

    out[...] = stage[...].astype(bf16)


def select_pieces(links, where_am_i, early, late):
    return pl.pallas_call(
        select_body,
        out_shape=jax.ShapeDtypeStruct((4 * PART, 128), bf16),
        in_specs=[pl.BlockSpec(memory_space=pltpu.SMEM)] * 2 + [pl.BlockSpec(memory_space=pltpu.VMEM)] * 3,
        out_specs=pl.BlockSpec(memory_space=pltpu.VMEM),
        scratch_shapes=[
            pltpu.VMEM((4 * PART, 128), f32),
            pltpu.VMEM((32, 128), jnp.int32),
            pltpu.SMEM((32, 128), jnp.int32),
            pltpu.SemaphoreType.DMA,
        ]
        + [pltpu.VMEM((88, 128), f32)] * BUFFERS
        + [pltpu.VMEM((56, 128), f32)] * BUFFERS,
        compiler_params=pltpu.CompilerParams(vmem_limit_bytes=12 << 20),
        name="select_pieces",
    )(links, where_am_i, *[near(x) for x in (early, *late)])


def slot_of(block, half):
    if block == 0:
        return 37 + half
    if block == BLOCKS - 1:
        return 44 + half
    return 2 * (block - 1) + half


def volume_body(
    facts, band0, band1, band2, band3, ref, summing, first_bias, second_bias, first_far, second_far, out_far,
    turned, refx, factors, sums, padded, hidden, keep, wide, first, second, out, loaded, stored,
):
    first_copy = pltpu.make_async_copy(first_far, first, loaded.at[0])
    second_copy = pltpu.make_async_copy(second_far, second, loaded.at[1])
    first_copy.start()
    second_copy.start()
    view = facts[0]
    lane16 = lax.broadcasted_iota(jnp.int32, (16, 128), 1)
    sub8 = lax.broadcasted_iota(jnp.int32, (8, 128), 0)

    def total(slot):
        span = slice(slot * 16, slot * 16 + 16)
        return (band0[span, :].astype(f32) + band1[span, :].astype(f32)) + (
            band2[span, :].astype(f32) + band3[span, :].astype(f32)
        )

    lanes = [lane16 >= 32 * m for m in range(4)]
    current = total(0)
    for slot in range(51):
        following = total(slot + 1)
        turned[slot] = current
        for m in range(1, 4):
            turned[m * 51 + slot] = pltpu.roll(
                jnp.where(lanes[m], current, following), 128 - 32 * m, 1
            )
        if slot < 32:
            block, half = 1 + slot // 2, slot % 2
            halo = pltpu.roll(current[8:16], 4, 0)
            own = pltpu.roll(ref[:, slot * 128 : slot * 128 + 128].astype(f32), 2, 0)
            refx[block * 2 + half, 0:8] = jnp.where(sub8 < 2, halo, own)
            refx[block * 2 + half, 8:16] = jnp.where(sub8 < 2, own, halo)
        current = following
    for half in range(2):
        refx[half] = total(51 + half)
        refx[2 * (BLOCKS - 1) + half] = total(53 + half)

    row = lax.broadcasted_iota(jnp.int32, (ROWS, 128), 0)
    high, block = row & 15, row >> 4
    inside = (high >= jnp.where(facts[1] >= 0, 0, 1)) & (high <= jnp.where(facts[2] >= 0, 9, 8))
    inside &= (block >= jnp.where(facts[3] >= 0, 0, 1))
    inside &= (block <= jnp.where(facts[4] >= 0, BLOCKS - 1, BLOCKS - 2))
    keep[...] = jnp.where(inside, 1.0, 0.0)
    sums[ROWS:, :] = jnp.zeros((sums.shape[0] - ROWS, 256), f32)
    hidden[ROWS:, :] = jnp.zeros((hidden.shape[0] - ROWS, 256), f32)

    def cost_step(q, carry):
        for m in range(4):
            dd = 4 * q + m
            for block in range(BLOCKS):
                for half in range(2):
                    product = refx[2 * block + half] * turned[m * 51 + slot_of(block, half) + q]
                    top = product.astype(bf16)
                    rest = (product - top.astype(f32)).astype(bf16)
                    at = block * 16
                    factors[at : at + 16, half * 128 : half * 128 + 128] = top
                    factors[at : at + 16, 256 + half * 128 : 384 + half * 128] = rest
            cells = jnp.dot(factors[...], summing[...], preferred_element_type=f32)
            depth = 16 * view + dd - 2
            sums[0:ROWS, :] = jnp.where((depth >= 0) & (depth < NDISP), cells, 0.0)
            low = [
                [sums[block * 16 + b : block * 16 + b + 16, 128:256] for b in range(3)]
                for block in range(BLOCKS)
            ]
            mixed = [
                jnp.where(lane16 >= 96, cells[2], jnp.where(lane16 >= 80, cells[1], cells[0]))
                for cells in low
            ]
            from_right = (lane16 & 8) == 8
            for block in range(BLOCKS):
                at = block * 16
                head = jnp.where(lane16 < 64, sums[at : at + 16, 0:128], sums[at + 1 : at + 17, 0:128])
                edge = jnp.where(
                    from_right, mixed[min(block + 1, BLOCKS - 1)], mixed[max(block - 1, 0)]
                )
                tail = jnp.where(lane16 < 64, low[block][2], edge)
                line = pl.multiple_of(dd * ROWS + at, 16)
                padded[pl.ds(line, 16), 0:128] = head.astype(bf16)
                padded[pl.ds(line, 16), 128:256] = tail.astype(bf16)
        return carry

    lax.fori_loop(0, 5, cost_step, 0)

    lane8 = lax.broadcasted_iota(jnp.int32, (8, 128), 1)

    def hidden_step(step, carry):
        cells = jnp.broadcast_to(first_bias[...], (ROWS, 256))
        for a in range(3):
            at = pl.multiple_of((step + a) * ROWS, 16)
            cells = cells + jnp.dot(padded[pl.ds(at, ROWS), :], first[a], preferred_element_type=f32)
        depth = 16 * view + step - 1
        live = jnp.where((depth >= 0) & (depth < NDISP), keep[...], 0.0) > 0.5
        for part in range(2):
            span = slice(part * 128, part * 128 + 128)
            hidden[0:ROWS, span] = jnp.where(live, jnp.maximum(cells[:, span], 0.0), 0.0)

        def block_cells(block):
            at = block * 16
            parts, edges = [], []
            for b in range(3):
                parts.append(hidden[at + b : at + b + 8, 0:128])
                parts.append(hidden[at + b : at + b + 8, 128:256])
                before = hidden[at + b - 16 : at + b - 8, 128:256]
                after = hidden[at + b + 16 : at + b + 24, 0:128]
                edges.append(pltpu.roll(jnp.where(lane8 < 96, after, before), 96 if b == 1 else 32, 1))
            parts.append(jnp.where(lane8 < 64, edges[0], edges[1]))
            parts.append(edges[2])
            return parts

        for pair in range(8):
            one = block_cells(1 + 2 * pair)
            two = block_cells(2 + 2 * pair)
            at = pl.multiple_of(step * 128 + pair * 16, 16)
            for part in range(8):
                wide[pl.ds(at, 16), part * 128 : part * 128 + 128] = jnp.concatenate(
                    [one[part], two[part]], axis=0
                ).astype(bf16)
        return carry

    first_copy.wait()
    lax.fori_loop(0, DL + 2, hidden_step, 0)
    second_copy.wait()

    def stores(step):
        span = pl.ds(step * 4, 4)
        return pltpu.make_async_copy(out.at[span], out_far.at[span], stored.at[step])

    def output_step(step, carry):
        cells = jnp.broadcast_to(second_bias[...], (512, 256))
        for a in range(3):
            at = pl.multiple_of((step * 4 + a) * 128, 128)
            cells = cells + jnp.dot(wide[pl.ds(at, 512), :], second[a], preferred_element_type=f32)
        for d in range(4):
            for block in range(16):
                at = d * 128 + block * 8
                out[step * 4 + d, :, block * 256 : block * 256 + 256] = cells[at : at + 8, :]
        stores(step).start()
        return carry

    lax.fori_loop(0, 4, output_step, 0)
    for step in range(4):
        stores(step).wait()


def volume(facts, bands, ref, first, first_bias, second, second_bias):
    operands = (
        facts, *[near(band) for band in bands], ref, jnp.asarray(group_sum_matrix(), bf16),
        first_bias, second_bias,
    )
    return pl.pallas_call(
        volume_body,
        out_shape=jax.ShapeDtypeStruct((DL, H, W * CH), f32),
        in_specs=[pl.BlockSpec(memory_space=pltpu.SMEM)]
        + [pl.BlockSpec(memory_space=pltpu.VMEM)] * 8
        + [pl.BlockSpec(memory_space=pl.ANY)] * 2,
        out_specs=pl.BlockSpec(memory_space=pl.ANY),
        scratch_shapes=[
            pltpu.VMEM((4 * 51, 16, 128), f32),
            pltpu.VMEM((2 * BLOCKS, 16, 128), f32),
            pltpu.VMEM((ROWS, 512), bf16),
            pltpu.VMEM((ROWS + 16, 256), f32),
            pltpu.VMEM((20 * ROWS, 256), bf16),
            pltpu.VMEM((ROWS + 16, 256), f32),
            pltpu.VMEM((ROWS, 128), f32),
            pltpu.VMEM((18 * 128, 1024), bf16),
            pltpu.VMEM(first.shape, bf16),
            pltpu.VMEM(second.shape, bf16),
            pltpu.VMEM((DL, H, W * CH), f32),
            pltpu.SemaphoreType.DMA((2,)),
            pltpu.SemaphoreType.DMA((4,)),
        ],
        compiler_params=pltpu.CompilerParams(vmem_limit_bytes=48 << 20),
        name="volume",
    )(*operands, first, second)


def on_device(
    ref_features, partner_lines, line_owner, line_index, line_offset, neighbours,
    conv1_weight, conv1_bias, conv2_weight, conv2_bias,
):
    view = lax.axis_index("views")
    core = lax.axis_index("c")
    tile = (lax.axis_index("z") * XB + lax.axis_index("x")) * CB + core
    ref = ref_features[0]

    lines = lax.dynamic_index_in_dim(partner_lines[0], view, 0, keepdims=False)
    halo_row = lax.dynamic_slice_in_dim(ref, (view + 6) % 8, 1, axis=0)
    sides = lax.dynamic_slice_in_dim(ref, 2 * view, 2, axis=0)
    sides = jnp.concatenate([sides[:, 0:256], sides[:, 3840:4096]], axis=1)
    names = jnp.stack([line_owner[0, :, 0], line_index[0], line_offset[0]])
    names = lax.dynamic_slice_in_dim(names, view * 8, 8, axis=1).astype(bf16).reshape(24)
    twin = lax.ppermute(names, "c", [(0, 1), (1, 0)])
    names = jnp.where(core == 0, jnp.concatenate([names, twin]), jnp.concatenate([twin, names]))
    payload = jnp.concatenate(
        [
            lines.reshape(8 * LINE, 128),
            halo_row.reshape(32, 128),
            sides.reshape(8, 128),
            jnp.pad(names[None], ((0, 7), (0, 80))),
        ],
        axis=0,
    )
    def shift(x, axis, by):
        count = lax.axis_size(axis)
        return lax.ppermute(x, axis, [(i, (i + by) % count) for i in range(count)])

    one, two, three = shift(payload, "x", 1), shift(payload, "x", -1), shift(payload, "x", 2)
    chunks = [[None, None] for _ in range(8)]
    chunks[0] = [jnp.concatenate([payload, one]), jnp.concatenate([two, three])]
    for k in range(1, 4):
        for i in range(2):
            chunks[-k % 8][i] = shift(chunks[(1 - k) % 8][i], "z", 1)
            chunks[k][i] = shift(chunks[k - 1][i], "z", -1)
    last = [shift(chunks[5][0], "z", 1), shift(chunks[3][1], "z", -1)]
    early = merge_chunks([chunk for k in range(8) if k != 4 for chunk in chunks[k]])

    links = neighbours.reshape(256)

    first, second = spread_weights(conv1_weight, conv2_weight)
    first_bias = jnp.tile(conv1_bias, 8)[None]
    second_bias = jnp.tile(conv2_bias, 8)[None]
    facts = jnp.concatenate([view[None], neighbours[tile]])
    other = tile + 1 - 2 * core
    asked = jnp.stack([other, core, view, tile])
    wanted = jnp.stack([tile, core, view, tile])
    links, asked, wanted, first, second, first_bias, second_bias, facts = lax.optimization_barrier(
        (links, asked, wanted, first, second, first_bias, second_bias, facts)
    )
    theirs = select_pieces(links, asked, early, last)
    swapped = lax.ppermute(theirs, "c", [(0, 1), (1, 0)])
    own = select_pieces(links, wanted, early, last)

    def part(step):
        span = slice(step * PART, (step + 1) * PART)
        return own[span] + swapped[span]

    bands = [part(0)] + [shift(part(step), "views", step) for step in (1, 2, 3)]
    return volume(facts, bands, ref, first, first_bias, second, second_bias)[None]


def solution(mesh):
    fine = Mesh(mesh.devices.reshape(ZB, XB, CB, NPV), ("z", "x", "c", "views"))
    tiles = ("z", "x", "c")
    return jax.shard_map(
        on_device,
        mesh=fine,
        in_specs=(
            P(tiles, None, None),
            P(tiles, None, None, None),
            P(tiles, None, None),
            P(tiles, None),
            P(tiles, None),
            P(),
            P(),
            P(),
            P(),
            P(),
        ),
        out_specs=P(tiles, "views", None, None),
        check_vma=False,
    )
```

time: 122 us -> 107 us (0.88)
  Pallas kernels: 40.3 us -> 29.2 us
  other arithmetic: 4.2 us -> 1.19 us
  local copies, waits for them, and re-layouts: 5.1 us -> 2.71 us
    pallas_call x2, Pallas kernels: 13.9 us -> 6.26 us  [select_pieces(): pl.pallas_call(select_body, out_shape=jax.ShapeDtypeStruct((4 * PART, 128...]
    pallas_call x1, Pallas kernels: 23.2 us -> 18.3 us  [volume(): pl.pallas_call(volume_body, out_shape=jax.ShapeDtypeStruct((DL, H, W * CH...]
    add x1, other arithmetic: 2.06 us -> 0.12 us  [part(): return own[span] + swapped[span]]
    pallas_call x1 -> x2, Pallas kernels: 3.14 us -> 4.63 us  [the longest x1 2.89 us: spread_weights(): pl.pallas_call(spread_body, out_shape=(jax.ShapeDtypeStruct((3, 256, 256)...]
  transfers between devices with their start and end apart: 22 -> 22, of which waited for: 14 -> 15; matrix products, arithmetic and copies ran while one was open for 4% -> 3% of each run, Pallas kernels for 8% -> 7%
where the time goes in v4:
time: 107 us
  waiting for transfers between devices  37.1 us (35%)
  starting transfers between devices  36 us (34%)
  Pallas kernels  29.2 us (27%)
  local copies, waits for them, and re-layouts  2.71 us (3%)
  other arithmetic  1.19 us (1%)
    ppermute x20, waiting for transfers between devices, shift(): return lax.ppermute(x, axis, [(i, (i + by) % count) for i in range(count)])  37.1 us
    ppermute x20, starting transfers between devices, shift(): return lax.ppermute(x, axis, [(i, (i + by) % count) for i in range(count)])  30.9 us
    pallas_call x1, Pallas kernels, volume(): pl.pallas_call(volume_body, out_shape=jax.ShapeDtypeStruct((DL, H, W * CH...  18.3 us
    pallas_call x2, Pallas kernels, select_pieces(): pl.pallas_call(select_body, out_shape=jax.ShapeDtypeStruct((4 * PART, 128...  6.26 us
    ppermute x1, starting transfers between devices, on_device(): twin = lax.ppermute(names, 'c', [(0, 1), (1, 0)])  3.2 us
    pallas_call x1, Pallas kernels, spread_weights(): pl.pallas_call(spread_body, out_shape=(jax.ShapeDtypeStruct((3, 256, 256)...  2.89 us
  transfers between devices with their start and end apart: 22, of which 15 were waited for; matrix products, arithmetic and copies ran while one was open for 3% of the time, Pallas kernels for 7%

profile of v4, /device:TPU:1, one launch (start us, length us, event | category | flops | bytes accessed | tf_op | source)
XLA Modules:
  0.0 106.6 jit_solution(11515469580732922884)
XLA Ops:
  0.9 3.2 %collective-permute-start = (bf16[24]{0:T(256)(128)(2,1)S(1)}, bf16[24]{0:T(256)(128)(2,1)S(1)}, u32[]{:S(2)}, u32[]{:S(2)}) collective-permute-start(bf16[24]{0:T(256)(128)(2,1)S(1)} %reshape.92), channel_id=1, source_target_pairs={{0,4},{4,0},{1,5},{5,1},{2,6},{6,2},{3,7},{7,3},{8,12},{12,8},{9,1... | collective-permute-start | bytes 152 | tf_op jit(solution)/shard_map/ppermute | solution.py:445
  6.4 2.7 %collective-permute-start.2 = (bf16[560,128]{1,0:T(8,128)(2,1)S(1)}, bf16[560,128]{1,0:T(8,128)(2,1)S(1)}, u32[]{:S(2)}, u32[]{:S(2)}) collective-permute-start(bf16[560,128]{1,0:T(8,128)(2,1)S(1)} %pad_maximum_fusion), channel_id=1, source_target_pairs={{0,24},{8,0},{16,8},{24,16},{1,25},{9,1},{17,9},{25,17},{2,26},{10... | collective-permute-start | bytes 430088 | tf_op jit(solution)/shard_map/ppermute | solution.py:458
  9.1 3.8 %collective-permute-done.1 = bf16[560,128]{1,0:T(8,128)(2,1)S(1)} collective-permute-done((bf16[560,128]{1,0:T(8,128)(2,1)S(1)}, bf16[560,128]{1,0:T(8,128)(2,1)S(1)}, u32[]{:S(2)}, u32[]{:S(2)}) %collective-permute-start.1) | collective-permute-done | bytes 143392 | tf_op jit(solution)/shard_map/ppermute | solution.py:458
  13.0 1.8 %collective-permute-done.2 = bf16[560,128]{1,0:T(8,128)(2,1)S(1)} collective-permute-done((bf16[560,128]{1,0:T(8,128)(2,1)S(1)}, bf16[560,128]{1,0:T(8,128)(2,1)S(1)}, u32[]{:S(2)}, u32[]{:S(2)}) %collective-permute-start.2) | collective-permute-done | bytes 143392 | tf_op jit(solution)/shard_map/ppermute | solution.py:458
  15.4 5.5 %collective-permute-start.5 = (bf16[1120,128]{1,0:T(8,128)(2,1)S(1)}, bf16[1120,128]{1,0:T(8,128)(2,1)S(1)}, u32[]{:S(2)}, u32[]{:S(2)}) collective-permute-start(bf16[1120,128]{1,0:T(8,128)(2,1)S(1)} %constant_dynamic-update-slice_fusion.5.refs_1_), channel_id=1, source_target_pairs={{0,224},{32,0},{64,32},{96,64},{128,96},{160,128},{192,160},{224,1... | collective-permute-start | bytes 860168 | tf_op jit(solution)/shard_map/ppermute | solution.py:458
  23.2 3.0 %collective-permute-done.5.refs_3_ = bf16[1120,128]{1,0:T(8,128)(2,1)S(1)} collective-permute-done((bf16[1120,128]{1,0:T(8,128)(2,1)S(1)}, bf16[1120,128]{1,0:T(8,128)(2,1)S(1)}, u32[]{:S(2)}, u32[]{:S(2)}) %collective-permute-start.5) | collective-permute-done | bytes 286752 | tf_op jit(solution)/shard_map/ppermute | solution.py:458
  26.2 3.4 %collective-permute-start.7 = (bf16[1120,128]{1,0:T(8,128)(2,1)S(1)}, bf16[1120,128]{1,0:T(8,128)(2,1)S(1)}, u32[]{:S(2)}, u32[]{:S(2)}) collective-permute-start(bf16[1120,128]{1,0:T(8,128)(2,1)S(1)} %collective-permute-done.5.refs_3_), channel_id=1, source_target_pairs={{0,224},{32,0},{64,32},{96,64},{128,96},{160,128},{192,160},{224,1... | collective-permute-start | bytes 860168 | tf_op jit(solution)/shard_map/ppermute | solution.py:458
  29.6 2.7 %collective-permute-done.4.refs_2_ = bf16[1120,128]{1,0:T(8,128)(2,1)S(1)} collective-permute-done((bf16[1120,128]{1,0:T(8,128)(2,1)S(1)}, bf16[1120,128]{1,0:T(8,128)(2,1)S(1)}, u32[]{:S(2)}, u32[]{:S(2)}) %collective-permute-start.4) | collective-permute-done | bytes 286752 | tf_op jit(solution)/shard_map/ppermute | solution.py:458
  32.4 3.4 %collective-permute-start.6 = (bf16[1120,128]{1,0:T(8,128)(2,1)S(1)}, bf16[1120,128]{1,0:T(8,128)(2,1)}, u32[]{:S(2)}, u32[]{:S(2)}) collective-permute-start(bf16[1120,128]{1,0:T(8,128)(2,1)S(1)} %collective-permute-done.4.refs_2_), channel_id=1, source_target_pairs={{0,224},{32,0},{64,32},{96,64},{128,96},{160,128},{192,160},{224,1... | collective-permute-start | bytes 860168 | tf_op jit(solution)/shard_map/ppermute | solution.py:458
  35.9 2.6 %collective-permute-done.7.refs_5_ = bf16[1120,128]{1,0:T(8,128)(2,1)S(1)} collective-permute-done((bf16[1120,128]{1,0:T(8,128)(2,1)S(1)}, bf16[1120,128]{1,0:T(8,128)(2,1)S(1)}, u32[]{:S(2)}, u32[]{:S(2)}) %collective-permute-start.7) | collective-permute-done | bytes 286752 | tf_op jit(solution)/shard_map/ppermute | solution.py:458
  38.5 3.4 %collective-permute-start.9 = (bf16[1120,128]{1,0:T(8,128)(2,1)S(1)}, bf16[1120,128]{1,0:T(8,128)(2,1)}, u32[]{:S(2)}, u32[]{:S(2)}) collective-permute-start(bf16[1120,128]{1,0:T(8,128)(2,1)S(1)} %collective-permute-done.7.refs_5_), channel_id=1, source_target_pairs={{0,224},{32,0},{64,32},{96,64},{128,96},{160,128},{192,160},{224,1... | collective-permute-start | bytes 860168 | tf_op jit(solution)/shard_map/ppermute | solution.py:458
  41.9 2.7 %collective-permute-done.6.refs_4_ = bf16[1120,128]{1,0:T(8,128)(2,1)} collective-permute-done((bf16[1120,128]{1,0:T(8,128)(2,1)S(1)}, bf16[1120,128]{1,0:T(8,128)(2,1)}, u32[]{:S(2)}, u32[]{:S(2)}) %collective-permute-start.6) | collective-permute-done | bytes 286752 | tf_op jit(solution)/shard_map/ppermute | solution.py:458
  44.7 3.5 %collective-permute-start.8 = (bf16[1120,128]{1,0:T(8,128)(2,1)}, bf16[1120,128]{1,0:T(8,128)(2,1)}, u32[]{:S(2)}, u32[]{:S(2)}) collective-permute-start(bf16[1120,128]{1,0:T(8,128)(2,1)} %collective-permute-done.6.refs_4_), channel_id=1, source_target_pairs={{0,224},{32,0},{64,32},{96,64},{128,96},{160,128},{192,160},{224,1... | collective-permute-start | bytes 860168 | tf_op jit(solution)/shard_map/ppermute | solution.py:458
  48.3 2.5 %collective-permute-done.9.refs_7_ = bf16[1120,128]{1,0:T(8,128)(2,1)} collective-permute-done((bf16[1120,128]{1,0:T(8,128)(2,1)S(1)}, bf16[1120,128]{1,0:T(8,128)(2,1)}, u32[]{:S(2)}, u32[]{:S(2)}) %collective-permute-start.9) | collective-permute-done | bytes 286752 | tf_op jit(solution)/shard_map/ppermute | solution.py:458
  50.8 3.5 %collective-permute-start.17 = (bf16[1120,128]{1,0:T(8,128)(2,1)}, bf16[1120,128]{1,0:T(8,128)(2,1)S(1)}, u32[]{:S(2)}, u32[]{:S(2)}) collective-permute-start(bf16[1120,128]{1,0:T(8,128)(2,1)} %collective-permute-done.9.refs_7_), channel_id=1, source_target_pairs={{0,224},{32,0},{64,32},{96,64},{128,96},{160,128},{192,160},{224,1... | collective-permute-start | bytes 860168 | tf_op jit(solution)/shard_map/ppermute | solution.py:458
  54.9 2.9 %spread_weights.1 = (bf16[3,256,256]{2,1,0:T(8,128)(2,1)}, bf16[3,1024,256]{2,1,0:T(8,128)(2,1)}) custom-call(bf16[216,32]{1,0:T(8,128)(2,1)} %bitcast.19, bf16[864,32]{1,0:T(8,128)(2,1)} %bitcast.17), custom_call_target="tpu_custom_call" | custom-call | tf_op jit(solution)/shard_map/spread_weights/pallas_call | solution.py:80
  60.9 2.3 %collective-permute-done.17.refs_2_ = bf16[1120,128]{1,0:T(8,128)(2,1)S(1)} collective-permute-done((bf16[1120,128]{1,0:T(8,128)(2,1)}, bf16[1120,128]{1,0:T(8,128)(2,1)S(1)}, u32[]{:S(2)}, u32[]{:S(2)}) %collective-permute-start.17) | collective-permute-done | bytes 286752 | tf_op jit(solution)/shard_map/ppermute | solution.py:458
  63.2 3.1 %select_pieces.3 = bf16[3520,128]{1,0:T(8,128)(2,1)S(1)} custom-call(s32[256]{0:T(256)S(1)} %reshape.86.links, s32[4]{0:T(128)S(1)} %get-tuple-element.20.where_am_i, bf16[15680,128]{1,0:T(8,128)(2,1)S(1)} %merge_chunks.1.refs_0_, bf16[1120,128]{1,0:T(8,128)(2,1)S(1)} %collective-permute-done.16.refs_1_, bf16[1120,128]{1,0:T(8,128)(2,1)S(1)} %collective-permute-done.17.refs_2_), custom_call_target="tpu_custom_call" | custom-call | tf_op jit(solution)/shard_map/select_pieces/pallas_call | solution.py:227
  66.3 1.9 %collective-permute-start.18 = (bf16[3520,128]{1,0:T(8,128)(2,1)S(1)}, bf16[3520,128]{1,0:T(8,128)(2,1)S(1)}, u32[]{:S(2)}, u32[]{:S(2)}) collective-permute-start(bf16[3520,128]{1,0:T(8,128)(2,1)S(1)} %select_pieces.3), channel_id=1, source_target_pairs={{0,4},{4,0},{1,5},{5,1},{2,6},{6,2},{3,7},{7,3},{8,12},{12,8},{9,1... | collective-permute-start | bytes 2703368 | tf_op jit(solution)/shard_map/ppermute | solution.py:483
  68.2 3.1 %select_pieces.2 = bf16[3520,128]{1,0:T(8,128)(2,1)S(1)} custom-call(s32[256]{0:T(256)S(1)} %reshape.86.links, s32[4]{0:T(128)S(1)} %get-tuple-element.19.where_am_i, bf16[15680,128]{1,0:T(8,128)(2,1)S(1)} %merge_chunks.1.refs_0_, bf16[1120,128]{1,0:T(8,128)(2,1)S(1)} %collective-permute-done.16.refs_1_, bf16[1120,128]{1,0:T(8,128)(2,1)S(1)} %collective-permute-done.17.refs_2_), custom_call_target="tpu_custom_call" | custom-call | tf_op jit(solution)/shard_map/select_pieces/pallas_call | solution.py:227
  71.5 2.8 %collective-permute-start.21 = (bf16[880,128]{1,0:T(8,128)(2,1)S(1)}, bf16[880,128]{1,0:T(8,128)(2,1)S(1)}, u32[]{:S(2)}, u32[]{:S(2)}) collective-permute-start(bf16[880,128]{1,0:T(8,128)(2,1)S(1)} %get-tuple-element.25), channel_id=1, source_target_pairs={{0,3},{1,0},{2,1},{3,2},{4,7},{5,4},{6,5},{7,6},{8,11},{9,8},{10,9... | collective-permute-start | bytes 675848 | tf_op jit(solution)/shard_map/ppermute | solution.py:458
  75.4 8.5 %collective-permute-done.21.band3 = bf16[880,128]{1,0:T(8,128)(2,1)S(1)} collective-permute-done((bf16[880,128]{1,0:T(8,128)(2,1)S(1)}, bf16[880,128]{1,0:T(8,128)(2,1)S(1)}, u32[]{:S(2)}, u32[]{:S(2)}) %collective-permute-start.21) | collective-permute-done | bytes 225312 | tf_op jit(solution)/shard_map/ppermute | solution.py:458
  83.9 4.2 %collective-permute-done.19.band1 = bf16[880,128]{1,0:T(8,128)(2,1)S(1)} collective-permute-done((bf16[880,128]{1,0:T(8,128)(2,1)S(1)}, bf16[880,128]{1,0:T(8,128)(2,1)S(1)}, u32[]{:S(2)}, u32[]{:S(2)}) %collective-permute-start.19) | collective-permute-done | bytes 225312 | tf_op jit(solution)/shard_map/ppermute | solution.py:458
  88.1 18.3 %volume.1 = f32[16,8,4096]{2,1,0:T(8,128)} custom-call(s32[5]{0:T(128)S(1)} %pad_add_fusion.1.facts, bf16[880,128]{1,0:T(8,128)(2,1)S(1)} %get-tuple-element.28.band0, bf16[880,128]{1,0:T(8,128)(2,1)S(1)} %collective-permute-done.19.band1, bf16[880,128]{1,0:T(8,128)(2,1)S(1)} %collective-permute-done.20.band2, ...), custom_call_target="tpu_custom_call" | custom-call | tf_op jit(solution)/shard_map/volume/pallas_call | solution.py:403
  (71 shorter events, 11.1 us)
Async XLA Ops:
  0.0 54.6 %copy-start.6 = (f32[32]{0:T(128)S(1)}, f32[32]{0:T(128)}, u32[]{:S(2)}) copy-start(f32[32]{0:T(128)} %param.18) | copy-start | bytes 388
  0.0 54.7 %copy-start.7 = (f32[32]{0:T(128)S(1)}, f32[32]{0:T(128)}, u32[]{:S(2)}) copy-start(f32[32]{0:T(128)} %param.20) | copy-start | bytes 388
  0.9 5.3 %collective-permute-start = (bf16[24]{0:T(256)(128)(2,1)S(1)}, bf16[24]{0:T(256)(128)(2,1)S(1)}, u32[]{:S(2)}, u32[]{:S(2)}) collective-permute-start(bf16[24]{0:T(256)(128)(2,1)S(1)} %reshape.92), channel_id=1, source_target_pairs={{0,4},{4,0},{1,5},{5,1},{2,6},{6,2},{3,7},{7,3},{8,12},{12,8},{9,1... | collective-permute-start | bytes 152 | tf_op jit(solution)/shard_map/ppermute | solution.py:445
  6.3 6.6 %collective-permute-start.1 = (bf16[560,128]{1,0:T(8,128)(2,1)S(1)}, bf16[560,128]{1,0:T(8,128)(2,1)S(1)}, u32[]{:S(2)}, u32[]{:S(2)}) collective-permute-start(bf16[560,128]{1,0:T(8,128)(2,1)S(1)} %pad_maximum_fusion), channel_id=1, source_target_pairs={{0,8},{8,16},{16,24},{24,0},{1,9},{9,17},{17,25},{25,1},{2,10},{10... | collective-permute-start | bytes 430088 | tf_op jit(solution)/shard_map/ppermute | solution.py:458
  6.4 8.4 %collective-permute-start.2 = (bf16[560,128]{1,0:T(8,128)(2,1)S(1)}, bf16[560,128]{1,0:T(8,128)(2,1)S(1)}, u32[]{:S(2)}, u32[]{:S(2)}) collective-permute-start(bf16[560,128]{1,0:T(8,128)(2,1)S(1)} %pad_maximum_fusion), channel_id=1, source_target_pairs={{0,24},{8,0},{16,8},{24,16},{1,25},{9,1},{17,9},{25,17},{2,26},{10... | collective-permute-start | bytes 430088 | tf_op jit(solution)/shard_map/ppermute | solution.py:458
  9.1 6.3 %collective-permute-start.3 = (bf16[560,128]{1,0:T(8,128)(2,1)S(1)}, bf16[560,128]{1,0:T(8,128)(2,1)S(1)}, u32[]{:S(2)}, u32[]{:S(2)}) collective-permute-start(bf16[560,128]{1,0:T(8,128)(2,1)S(1)} %pad_maximum_fusion), channel_id=1, source_target_pairs={{0,16},{8,24},{16,0},{24,8},{1,17},{9,25},{17,1},{25,9},{2,18},{10... | collective-permute-start | bytes 430088 | tf_op jit(solution)/shard_map/ppermute | solution.py:458
  12.9 10.3 %collective-permute-start.10 = (bf16[1120,128]{1,0:T(8,128)(2,1)S(1)}, bf16[1120,128]{1,0:T(8,128)(2,1)S(1)}, u32[]{:S(2)}, u32[]{:S(2)}) collective-permute-start(bf16[1120,128]{1,0:T(8,128)(2,1)S(1)} %constant_dynamic-update-slice_fusion.refs_0_), channel_id=1, source_target_pairs={{0,32},{32,64},{64,96},{96,128},{128,160},{160,192},{192,224},{224... | collective-permute-start | bytes 860168 | tf_op jit(solution)/shard_map/ppermute | solution.py:458
  15.4 10.8 %collective-permute-start.5 = (bf16[1120,128]{1,0:T(8,128)(2,1)S(1)}, bf16[1120,128]{1,0:T(8,128)(2,1)S(1)}, u32[]{:S(2)}, u32[]{:S(2)}) collective-permute-start(bf16[1120,128]{1,0:T(8,128)(2,1)S(1)} %constant_dynamic-update-slice_fusion.5.refs_1_), channel_id=1, source_target_pairs={{0,224},{32,0},{64,32},{96,64},{128,96},{160,128},{192,160},{224,1... | collective-permute-start | bytes 860168 | tf_op jit(solution)/shard_map/ppermute | solution.py:458
  20.9 11.4 %collective-permute-start.4 = (bf16[1120,128]{1,0:T(8,128)(2,1)S(1)}, bf16[1120,128]{1,0:T(8,128)(2,1)S(1)}, u32[]{:S(2)}, u32[]{:S(2)}) collective-permute-start(bf16[1120,128]{1,0:T(8,128)(2,1)S(1)} %constant_dynamic-update-slice_fusion.refs_0_), channel_id=1, source_target_pairs={{0,224},{32,0},{64,32},{96,64},{128,96},{160,128},{192,160},{224,1... | collective-permute-start | bytes 860168 | tf_op jit(solution)/shard_map/ppermute | solution.py:458
  21.6 14.1 %collective-permute-start.13 = (bf16[1120,128]{1,0:T(8,128)(2,1)S(1)}, bf16[1120,128]{1,0:T(8,128)(2,1)S(1)}, u32[]{:S(2)}, u32[]{:S(2)}) collective-permute-start(bf16[1120,128]{1,0:T(8,128)(2,1)S(1)} %constant_dynamic-update-slice_fusion.5.refs_1_), channel_id=1, source_target_pairs={{0,32},{32,64},{64,96},{96,128},{128,160},{160,192},{192,224},{224... | collective-permute-start | bytes 860168 | tf_op jit(solution)/shard_map/ppermute | solution.py:458
  23.2 12.8 %collective-permute-start.11 = (bf16[1120,128]{1,0:T(8,128)(2,1)S(1)}, bf16[1120,128]{1,0:T(8,128)(2,1)S(1)}, u32[]{:S(2)}, u32[]{:S(2)}) collective-permute-start(bf16[1120,128]{1,0:T(8,128)(2,1)S(1)} %collective-permute-done.10.refs_12_), channel_id=1, source_target_pairs={{0,32},{32,64},{64,96},{96,128},{128,160},{160,192},{192,224},{224... | collective-permute-start | bytes 860168 | tf_op jit(solution)/shard_map/ppermute | solution.py:458
  26.2 12.3 %collective-permute-start.7 = (bf16[1120,128]{1,0:T(8,128)(2,1)S(1)}, bf16[1120,128]{1,0:T(8,128)(2,1)S(1)}, u32[]{:S(2)}, u32[]{:S(2)}) collective-permute-start(bf16[1120,128]{1,0:T(8,128)(2,1)S(1)} %collective-permute-done.5.refs_3_), channel_id=1, source_target_pairs={{0,224},{32,0},{64,32},{96,64},{128,96},{160,128},{192,160},{224,1... | collective-permute-start | bytes 860168 | tf_op jit(solution)/shard_map/ppermute | solution.py:458
  32.4 12.3 %collective-permute-start.6 = (bf16[1120,128]{1,0:T(8,128)(2,1)S(1)}, bf16[1120,128]{1,0:T(8,128)(2,1)}, u32[]{:S(2)}, u32[]{:S(2)}) collective-permute-start(bf16[1120,128]{1,0:T(8,128)(2,1)S(1)} %collective-permute-done.4.refs_2_), channel_id=1, source_target_pairs={{0,224},{32,0},{64,32},{96,64},{128,96},{160,128},{192,160},{224,1... | collective-permute-start | bytes 860168 | tf_op jit(solution)/shard_map/ppermute | solution.py:458
  35.8 12.4 %collective-permute-start.14 = (bf16[1120,128]{1,0:T(8,128)(2,1)S(1)}, bf16[1120,128]{1,0:T(8,128)(2,1)}, u32[]{:S(2)}, u32[]{:S(2)}) collective-permute-start(bf16[1120,128]{1,0:T(8,128)(2,1)S(1)} %collective-permute-done.13.refs_13_), channel_id=1, source_target_pairs={{0,32},{32,64},{64,96},{96,128},{128,160},{160,192},{192,224},{224... | collective-permute-start | bytes 860168 | tf_op jit(solution)/shard_map/ppermute | solution.py:458
  35.9 12.3 %collective-permute-start.12 = (bf16[1120,128]{1,0:T(8,128)(2,1)S(1)}, bf16[1120,128]{1,0:T(8,128)(2,1)}, u32[]{:S(2)}, u32[]{:S(2)}) collective-permute-start(bf16[1120,128]{1,0:T(8,128)(2,1)S(1)} %collective-permute-done.11.refs_10_), channel_id=1, source_target_pairs={{0,32},{32,64},{64,96},{96,128},{128,160},{160,192},{192,224},{224... | collective-permute-start | bytes 860168 | tf_op jit(solution)/shard_map/ppermute | solution.py:458
  38.5 12.3 %collective-permute-start.9 = (bf16[1120,128]{1,0:T(8,128)(2,1)S(1)}, bf16[1120,128]{1,0:T(8,128)(2,1)}, u32[]{:S(2)}, u32[]{:S(2)}) collective-permute-start(bf16[1120,128]{1,0:T(8,128)(2,1)S(1)} %collective-permute-done.7.refs_5_), channel_id=1, source_target_pairs={{0,224},{32,0},{64,32},{96,64},{128,96},{160,128},{192,160},{224,1... | collective-permute-start | bytes 860168 | tf_op jit(solution)/shard_map/ppermute | solution.py:458
  44.7 13.3 %collective-permute-start.8 = (bf16[1120,128]{1,0:T(8,128)(2,1)}, bf16[1120,128]{1,0:T(8,128)(2,1)}, u32[]{:S(2)}, u32[]{:S(2)}) collective-permute-start(bf16[1120,128]{1,0:T(8,128)(2,1)} %collective-permute-done.6.refs_4_), channel_id=1, source_target_pairs={{0,224},{32,0},{64,32},{96,64},{128,96},{160,128},{192,160},{224,1... | collective-permute-start | bytes 860168 | tf_op jit(solution)/shard_map/ppermute | solution.py:458
  48.2 9.8 %collective-permute-start.15 = (bf16[1120,128]{1,0:T(8,128)(2,1)}, bf16[1120,128]{1,0:T(8,128)(2,1)}, u32[]{:S(2)}, u32[]{:S(2)}) collective-permute-start(bf16[1120,128]{1,0:T(8,128)(2,1)} %collective-permute-done.14.refs_11_), channel_id=1, source_target_pairs={{0,32},{32,64},{64,96},{96,128},{128,160},{160,192},{192,224},{224... | collective-permute-start | bytes 860168 | tf_op jit(solution)/shard_map/ppermute | solution.py:458
  48.3 12.6 %collective-permute-start.16 = (bf16[1120,128]{1,0:T(8,128)(2,1)}, bf16[1120,128]{1,0:T(8,128)(2,1)S(1)}, u32[]{:S(2)}, u32[]{:S(2)}) collective-permute-start(bf16[1120,128]{1,0:T(8,128)(2,1)} %collective-permute-done.12.refs_8_), channel_id=1, source_target_pairs={{0,32},{32,64},{64,96},{96,128},{128,160},{160,192},{192,224},{224... | collective-permute-start | bytes 860168 | tf_op jit(solution)/shard_map/ppermute | solution.py:458
  50.8 12.4 %collective-permute-start.17 = (bf16[1120,128]{1,0:T(8,128)(2,1)}, bf16[1120,128]{1,0:T(8,128)(2,1)S(1)}, u32[]{:S(2)}, u32[]{:S(2)}) collective-permute-start(bf16[1120,128]{1,0:T(8,128)(2,1)} %collective-permute-done.9.refs_7_), channel_id=1, source_target_pairs={{0,224},{32,0},{64,32},{96,64},{128,96},{160,128},{192,160},{224,1... | collective-permute-start | bytes 860168 | tf_op jit(solution)/shard_map/ppermute | solution.py:458
  66.3 5.1 %collective-permute-start.18 = (bf16[3520,128]{1,0:T(8,128)(2,1)S(1)}, bf16[3520,128]{1,0:T(8,128)(2,1)S(1)}, u32[]{:S(2)}, u32[]{:S(2)}) collective-permute-start(bf16[3520,128]{1,0:T(8,128)(2,1)S(1)} %select_pieces.3), channel_id=1, source_target_pairs={{0,4},{4,0},{1,5},{5,1},{2,6},{6,2},{3,7},{7,3},{8,12},{12,8},{9,1... | collective-permute-start | bytes 2703368 | tf_op jit(solution)/shard_map/ppermute | solution.py:483
  71.5 12.4 %collective-permute-start.21 = (bf16[880,128]{1,0:T(8,128)(2,1)S(1)}, bf16[880,128]{1,0:T(8,128)(2,1)S(1)}, u32[]{:S(2)}, u32[]{:S(2)}) collective-permute-start(bf16[880,128]{1,0:T(8,128)(2,1)S(1)} %get-tuple-element.25), channel_id=1, source_target_pairs={{0,3},{1,0},{2,1},{3,2},{4,7},{5,4},{6,5},{7,6},{8,11},{9,8},{10,9... | collective-permute-start | bytes 675848 | tf_op jit(solution)/shard_map/ppermute | solution.py:458
  74.4 9.5 %collective-permute-start.20 = (bf16[880,128]{1,0:T(8,128)(2,1)S(1)}, bf16[880,128]{1,0:T(8,128)(2,1)S(1)}, u32[]{:S(2)}, u32[]{:S(2)}) collective-permute-start(bf16[880,128]{1,0:T(8,128)(2,1)S(1)} %get-tuple-element.26), channel_id=1, source_target_pairs={{0,2},{1,3},{2,0},{3,1},{4,6},{5,7},{6,4},{7,5},{8,10},{9,11},{10,... | collective-permute-start | bytes 675848 | tf_op jit(solution)/shard_map/ppermute | solution.py:458
  74.7 13.4 %collective-permute-start.19 = (bf16[880,128]{1,0:T(8,128)(2,1)S(1)}, bf16[880,128]{1,0:T(8,128)(2,1)S(1)}, u32[]{:S(2)}, u32[]{:S(2)}) collective-permute-start(bf16[880,128]{1,0:T(8,128)(2,1)S(1)} %get-tuple-element.27), channel_id=1, source_target_pairs={{0,1},{1,2},{2,3},{3,0},{4,5},{5,6},{6,7},{7,4},{8,9},{9,10},{10,1... | collective-permute-start | bytes 675848 | tf_op jit(solution)/shard_map/ppermute | solution.py:458
  (6 other events, 127.4 us)

commit v5 on v4

--- a/solution.py
+++ b/solution.py
@@ -5,6 +5,7 @@
 from jax.experimental import pallas as pl
 from jax.experimental.pallas import tpu as pltpu
 from jax.sharding import Mesh, PartitionSpec as P
+
 
 C = 32
 G = 8
@@ -20,6 +21,7 @@
 BLOCKS = 18
 ROWS = BLOCKS * 16
 DL = 16
+HALF = 28
 ZB, XB, CB = 8, 4, 2
 
 bf16 = jnp.bfloat16
@@ -251,7 +253,7 @@
 
 
 def volume_body(
-    facts, band0, band1, band2, band3, ref, summing, first_bias, second_bias, first_far, second_far, out_far,
+    facts, band0, band1, band2, band3, band4, ref, summing, first_bias, second_bias, first_far, second_far, out_far,
     turned, refx, factors, sums, padded, hidden, keep, wide, first, second, out, loaded, stored,
 ):
     first_copy = pltpu.make_async_copy(first_far, first, loaded.at[0])
@@ -264,8 +266,12 @@
 
     def total(slot):
         span = slice(slot * 16, slot * 16 + 16)
+        if slot < HALF:
+            opposite = band2[span, :].astype(f32)
+        else:
+            opposite = band4[slot * 16 - HALF * 16 : slot * 16 - HALF * 16 + 16, :].astype(f32)
         return (band0[span, :].astype(f32) + band1[span, :].astype(f32)) + (
-            band2[span, :].astype(f32) + band3[span, :].astype(f32)
+            opposite + band3[span, :].astype(f32)
         )
 
     lanes = [lane16 >= 32 * m for m in range(4)]
@@ -311,25 +317,24 @@
             cells = jnp.dot(factors[...], summing[...], preferred_element_type=f32)
             depth = 16 * view + dd - 2
             sums[0:ROWS, :] = jnp.where((depth >= 0) & (depth < NDISP), cells, 0.0)
-            low = [
-                [sums[block * 16 + b : block * 16 + b + 16, 128:256] for b in range(3)]
-                for block in range(BLOCKS)
-            ]
-            mixed = [
-                jnp.where(lane16 >= 96, cells[2], jnp.where(lane16 >= 80, cells[1], cells[0]))
-                for cells in low
-            ]
             from_right = (lane16 & 8) == 8
+
+            def mixed_cells(block):
+                low = [sums[block * 16 + b : block * 16 + b + 16, 128:256] for b in range(3)]
+                return low[2], jnp.where(lane16 >= 96, low[2], jnp.where(lane16 >= 80, low[1], low[0]))
+
+            this_low, this_mixed = mixed_cells(0)
+            last_mixed = this_mixed
             for block in range(BLOCKS):
                 at = block * 16
+                next_low, next_mixed = mixed_cells(min(block + 1, BLOCKS - 1))
                 head = jnp.where(lane16 < 64, sums[at : at + 16, 0:128], sums[at + 1 : at + 17, 0:128])
-                edge = jnp.where(
-                    from_right, mixed[min(block + 1, BLOCKS - 1)], mixed[max(block - 1, 0)]
-                )
-                tail = jnp.where(lane16 < 64, low[block][2], edge)
+                edge = jnp.where(from_right, next_mixed, last_mixed)
+                tail = jnp.where(lane16 < 64, this_low, edge)
                 line = pl.multiple_of(dd * ROWS + at, 16)
                 padded[pl.ds(line, 16), 0:128] = head.astype(bf16)
                 padded[pl.ds(line, 16), 128:256] = tail.astype(bf16)
+                this_low, last_mixed, this_mixed = next_low, this_mixed, next_mixed
         return carry
 
     lax.fori_loop(0, 5, cost_step, 0)
@@ -404,7 +409,7 @@
         volume_body,
         out_shape=jax.ShapeDtypeStruct((DL, H, W * CH), f32),
         in_specs=[pl.BlockSpec(memory_space=pltpu.SMEM)]
-        + [pl.BlockSpec(memory_space=pltpu.VMEM)] * 8
+        + [pl.BlockSpec(memory_space=pltpu.VMEM)] * 9
         + [pl.BlockSpec(memory_space=pl.ANY)] * 2,
         out_specs=pl.BlockSpec(memory_space=pl.ANY),
         scratch_shapes=[
@@ -453,6 +458,7 @@
         ],
         axis=0,
     )
+
     def shift(x, axis, by):
         count = lax.axis_size(axis)
         return lax.ppermute(x, axis, [(i, (i + by) % count) for i in range(count)])
@@ -483,11 +489,19 @@
     swapped = lax.ppermute(theirs, "c", [(0, 1), (1, 0)])
     own = select_pieces(links, wanted, early, last)
 
-    def part(step):
-        span = slice(step * PART, (step + 1) * PART)
-        return own[span] + swapped[span]
-
-    bands = [part(0)] + [shift(part(step), "views", step) for step in (1, 2, 3)]
+    def part(begin, end):
+        return own[begin:end] + swapped[begin:end]
+
+    middle = 2 * PART + HALF * 16
+    upward = shift(part(2 * PART, middle), "views", 1)
+    downward = shift(part(middle, 3 * PART), "views", -1)
+    bands = [
+        part(0, PART),
+        shift(part(PART, 2 * PART), "views", 1),
+        shift(upward, "views", 1),
+        shift(part(3 * PART, 4 * PART), "views", -1),
+        shift(downward, "views", -1),
+    ]
     return volume(facts, bands, ref, first, first_bias, second, second_bias)[None]
 
 

time: 107 us -> 106 us (level)
  waiting for transfers between devices: 37.1 us -> 31 us
  starting transfers between devices: 36 us -> 40.6 us
    ppermute x20 -> x23, waiting for transfers between devices: 37.1 us -> 31 us  [shift(): return lax.ppermute(x, axis, [(i, (i + by) % count) for i in range(count)])]
    ppermute x20 -> x23, starting transfers between devices: 30.9 us -> 35.5 us  [shift(): return lax.ppermute(x, axis, [(i, (i + by) % count) for i in range(count)])]
  transfers between devices with their start and end apart: 22 -> 25, of which waited for: 15 -> 16; matrix products, arithmetic and copies ran while one was open for 3% -> 3% of each run, Pallas kernels for 7% -> 7%
where the time goes in v5:
time: 106 us; the launch traced here: 105 us
  starting transfers between devices  40.6 us (38%)
  waiting for transfers between devices  31 us (29%)
  Pallas kernels  29.1 us (27%)
  local copies, waits for them, and re-layouts  2.71 us (3%)
  other arithmetic  1.2 us (1%)
    ppermute x23, starting transfers between devices, shift(): return lax.ppermute(x, axis, [(i, (i + by) % count) for i in range(count)])  35.5 us
    ppermute x23, waiting for transfers between devices, shift(): return lax.ppermute(x, axis, [(i, (i + by) % count) for i in range(count)])  31 us
    pallas_call x1, Pallas kernels, volume(): pl.pallas_call(volume_body, out_shape=jax.ShapeDtypeStruct((DL, H, W * CH...  18.2 us
    pallas_call x2, Pallas kernels, select_pieces(): pl.pallas_call(select_body, out_shape=jax.ShapeDtypeStruct((4 * PART, 128...  6.27 us
    ppermute x1, starting transfers between devices, on_device(): twin = lax.ppermute(names, 'c', [(0, 1), (1, 0)])  3.2 us
    pallas_call x1, Pallas kernels, spread_weights(): pl.pallas_call(spread_body, out_shape=(jax.ShapeDtypeStruct((3, 256, 256)...  2.89 us
  transfers between devices with their start and end apart: 25, of which 16 were waited for; matrix products, arithmetic and copies ran while one was open for 3% of the time, Pallas kernels for 7%

profile of v5, /device:TPU:1, one launch (start us, length us, event | category | flops | bytes accessed | tf_op | source)
XLA Modules:
  0.0 105.1 jit_solution(13832458121632089389)
XLA Ops:
  0.9 3.2 %collective-permute-start = (bf16[24]{0:T(256)(128)(2,1)S(1)}, bf16[24]{0:T(256)(128)(2,1)S(1)}, u32[]{:S(2)}, u32[]{:S(2)}) collective-permute-start(bf16[24]{0:T(256)(128)(2,1)S(1)} %reshape.92), channel_id=1, source_target_pairs={{0,4},{4,0},{1,5},{5,1},{2,6},{6,2},{3,7},{7,3},{8,12},{12,8},{9,1... | collective-permute-start | bytes 152 | tf_op jit(solution)/shard_map/ppermute | solution.py:450
  6.4 2.7 %collective-permute-start.2 = (bf16[560,128]{1,0:T(8,128)(2,1)S(1)}, bf16[560,128]{1,0:T(8,128)(2,1)S(1)}, u32[]{:S(2)}, u32[]{:S(2)}) collective-permute-start(bf16[560,128]{1,0:T(8,128)(2,1)S(1)} %pad_maximum_fusion), channel_id=1, source_target_pairs={{0,24},{8,0},{16,8},{24,16},{1,25},{9,1},{17,9},{25,17},{2,26},{10... | collective-permute-start | bytes 430088 | tf_op jit(solution)/shard_map/ppermute | solution.py:464
  9.1 3.8 %collective-permute-done.1 = bf16[560,128]{1,0:T(8,128)(2,1)S(1)} collective-permute-done((bf16[560,128]{1,0:T(8,128)(2,1)S(1)}, bf16[560,128]{1,0:T(8,128)(2,1)S(1)}, u32[]{:S(2)}, u32[]{:S(2)}) %collective-permute-start.1) | collective-permute-done | bytes 143392 | tf_op jit(solution)/shard_map/ppermute | solution.py:464
  13.0 1.8 %collective-permute-done.2 = bf16[560,128]{1,0:T(8,128)(2,1)S(1)} collective-permute-done((bf16[560,128]{1,0:T(8,128)(2,1)S(1)}, bf16[560,128]{1,0:T(8,128)(2,1)S(1)}, u32[]{:S(2)}, u32[]{:S(2)}) %collective-permute-start.2) | collective-permute-done | bytes 143392 | tf_op jit(solution)/shard_map/ppermute | solution.py:464
  15.4 5.5 %collective-permute-start.5 = (bf16[1120,128]{1,0:T(8,128)(2,1)S(1)}, bf16[1120,128]{1,0:T(8,128)(2,1)S(1)}, u32[]{:S(2)}, u32[]{:S(2)}) collective-permute-start(bf16[1120,128]{1,0:T(8,128)(2,1)S(1)} %constant_dynamic-update-slice_fusion.5.refs_1_), channel_id=1, source_target_pairs={{0,224},{32,0},{64,32},{96,64},{128,96},{160,128},{192,160},{224,1... | collective-permute-start | bytes 860168 | tf_op jit(solution)/shard_map/ppermute | solution.py:464
  23.2 3.0 %collective-permute-done.5.refs_3_ = bf16[1120,128]{1,0:T(8,128)(2,1)S(1)} collective-permute-done((bf16[1120,128]{1,0:T(8,128)(2,1)S(1)}, bf16[1120,128]{1,0:T(8,128)(2,1)S(1)}, u32[]{:S(2)}, u32[]{:S(2)}) %collective-permute-start.5) | collective-permute-done | bytes 286752 | tf_op jit(solution)/shard_map/ppermute | solution.py:464
  26.2 3.4 %collective-permute-start.7 = (bf16[1120,128]{1,0:T(8,128)(2,1)S(1)}, bf16[1120,128]{1,0:T(8,128)(2,1)S(1)}, u32[]{:S(2)}, u32[]{:S(2)}) collective-permute-start(bf16[1120,128]{1,0:T(8,128)(2,1)S(1)} %collective-permute-done.5.refs_3_), channel_id=1, source_target_pairs={{0,224},{32,0},{64,32},{96,64},{128,96},{160,128},{192,160},{224,1... | collective-permute-start | bytes 860168 | tf_op jit(solution)/shard_map/ppermute | solution.py:464
  29.6 2.7 %collective-permute-done.4.refs_2_ = bf16[1120,128]{1,0:T(8,128)(2,1)S(1)} collective-permute-done((bf16[1120,128]{1,0:T(8,128)(2,1)S(1)}, bf16[1120,128]{1,0:T(8,128)(2,1)S(1)}, u32[]{:S(2)}, u32[]{:S(2)}) %collective-permute-start.4) | collective-permute-done | bytes 286752 | tf_op jit(solution)/shard_map/ppermute | solution.py:464
  32.4 3.4 %collective-permute-start.6 = (bf16[1120,128]{1,0:T(8,128)(2,1)S(1)}, bf16[1120,128]{1,0:T(8,128)(2,1)}, u32[]{:S(2)}, u32[]{:S(2)}) collective-permute-start(bf16[1120,128]{1,0:T(8,128)(2,1)S(1)} %collective-permute-done.4.refs_2_), channel_id=1, source_target_pairs={{0,224},{32,0},{64,32},{96,64},{128,96},{160,128},{192,160},{224,1... | collective-permute-start | bytes 860168 | tf_op jit(solution)/shard_map/ppermute | solution.py:464
  35.9 2.6 %collective-permute-done.7.refs_5_ = bf16[1120,128]{1,0:T(8,128)(2,1)S(1)} collective-permute-done((bf16[1120,128]{1,0:T(8,128)(2,1)S(1)}, bf16[1120,128]{1,0:T(8,128)(2,1)S(1)}, u32[]{:S(2)}, u32[]{:S(2)}) %collective-permute-start.7) | collective-permute-done | bytes 286752 | tf_op jit(solution)/shard_map/ppermute | solution.py:464
  38.5 3.4 %collective-permute-start.9 = (bf16[1120,128]{1,0:T(8,128)(2,1)S(1)}, bf16[1120,128]{1,0:T(8,128)(2,1)}, u32[]{:S(2)}, u32[]{:S(2)}) collective-permute-start(bf16[1120,128]{1,0:T(8,128)(2,1)S(1)} %collective-permute-done.7.refs_5_), channel_id=1, source_target_pairs={{0,224},{32,0},{64,32},{96,64},{128,96},{160,128},{192,160},{224,1... | collective-permute-start | bytes 860168 | tf_op jit(solution)/shard_map/ppermute | solution.py:464
  41.9 2.7 %collective-permute-done.6.refs_4_ = bf16[1120,128]{1,0:T(8,128)(2,1)} collective-permute-done((bf16[1120,128]{1,0:T(8,128)(2,1)S(1)}, bf16[1120,128]{1,0:T(8,128)(2,1)}, u32[]{:S(2)}, u32[]{:S(2)}) %collective-permute-start.6) | collective-permute-done | bytes 286752 | tf_op jit(solution)/shard_map/ppermute | solution.py:464
  44.7 3.5 %collective-permute-start.8 = (bf16[1120,128]{1,0:T(8,128)(2,1)}, bf16[1120,128]{1,0:T(8,128)(2,1)}, u32[]{:S(2)}, u32[]{:S(2)}) collective-permute-start(bf16[1120,128]{1,0:T(8,128)(2,1)} %collective-permute-done.6.refs_4_), channel_id=1, source_target_pairs={{0,224},{32,0},{64,32},{96,64},{128,96},{160,128},{192,160},{224,1... | collective-permute-start | bytes 860168 | tf_op jit(solution)/shard_map/ppermute | solution.py:464
  48.3 2.5 %collective-permute-done.9.refs_7_ = bf16[1120,128]{1,0:T(8,128)(2,1)} collective-permute-done((bf16[1120,128]{1,0:T(8,128)(2,1)S(1)}, bf16[1120,128]{1,0:T(8,128)(2,1)}, u32[]{:S(2)}, u32[]{:S(2)}) %collective-permute-start.9) | collective-permute-done | bytes 286752 | tf_op jit(solution)/shard_map/ppermute | solution.py:464
  50.8 3.5 %collective-permute-start.17 = (bf16[1120,128]{1,0:T(8,128)(2,1)}, bf16[1120,128]{1,0:T(8,128)(2,1)S(1)}, u32[]{:S(2)}, u32[]{:S(2)}) collective-permute-start(bf16[1120,128]{1,0:T(8,128)(2,1)} %collective-permute-done.9.refs_7_), channel_id=1, source_target_pairs={{0,224},{32,0},{64,32},{96,64},{128,96},{160,128},{192,160},{224,1... | collective-permute-start | bytes 860168 | tf_op jit(solution)/shard_map/ppermute | solution.py:464
  54.9 2.9 %spread_weights.1 = (bf16[3,256,256]{2,1,0:T(8,128)(2,1)}, bf16[3,1024,256]{2,1,0:T(8,128)(2,1)}) custom-call(bf16[216,32]{1,0:T(8,128)(2,1)} %bitcast.19, bf16[864,32]{1,0:T(8,128)(2,1)} %bitcast.17), custom_call_target="tpu_custom_call" | custom-call | tf_op jit(solution)/shard_map/spread_weights/pallas_call | solution.py:82
  60.9 2.3 %collective-permute-done.17.refs_2_ = bf16[1120,128]{1,0:T(8,128)(2,1)S(1)} collective-permute-done((bf16[1120,128]{1,0:T(8,128)(2,1)}, bf16[1120,128]{1,0:T(8,128)(2,1)S(1)}, u32[]{:S(2)}, u32[]{:S(2)}) %collective-permute-start.17) | collective-permute-done | bytes 286752 | tf_op jit(solution)/shard_map/ppermute | solution.py:464
  63.2 3.1 %select_pieces.3 = bf16[3520,128]{1,0:T(8,128)(2,1)S(1)} custom-call(s32[256]{0:T(256)S(1)} %reshape.86.links, s32[4]{0:T(128)S(1)} %get-tuple-element.20.where_am_i, bf16[15680,128]{1,0:T(8,128)(2,1)S(1)} %merge_chunks.1.refs_0_, bf16[1120,128]{1,0:T(8,128)(2,1)S(1)} %collective-permute-done.16.refs_1_, bf16[1120,128]{1,0:T(8,128)(2,1)S(1)} %collective-permute-done.17.refs_2_), custom_call_target="tpu_custom_call" | custom-call | tf_op jit(solution)/shard_map/select_pieces/pallas_call | solution.py:229
  66.3 1.9 %collective-permute-start.18 = (bf16[3520,128]{1,0:T(8,128)(2,1)S(1)}, bf16[3520,128]{1,0:T(8,128)(2,1)S(1)}, u32[]{:S(2)}, u32[]{:S(2)}) collective-permute-start(bf16[3520,128]{1,0:T(8,128)(2,1)S(1)} %select_pieces.3), channel_id=1, source_target_pairs={{0,4},{4,0},{1,5},{5,1},{2,6},{6,2},{3,7},{7,3},{8,12},{12,8},{9,1... | collective-permute-start | bytes 2703368 | tf_op jit(solution)/shard_map/ppermute | solution.py:489
  68.2 3.1 %select_pieces.2 = bf16[3520,128]{1,0:T(8,128)(2,1)S(1)} custom-call(s32[256]{0:T(256)S(1)} %reshape.86.links, s32[4]{0:T(128)S(1)} %get-tuple-element.19.where_am_i, bf16[15680,128]{1,0:T(8,128)(2,1)S(1)} %merge_chunks.1.refs_0_, bf16[1120,128]{1,0:T(8,128)(2,1)S(1)} %collective-permute-done.16.refs_1_, bf16[1120,128]{1,0:T(8,128)(2,1)S(1)} %collective-permute-done.17.refs_2_), custom_call_target="tpu_custom_call" | custom-call | tf_op jit(solution)/shard_map/select_pieces/pallas_call | solution.py:229
  74.5 2.8 %collective-permute-start.23 = (bf16[432,128]{1,0:T(8,128)(2,1)S(1)}, bf16[432,128]{1,0:T(8,128)(2,1)S(1)}, u32[]{:S(2)}, u32[]{:S(2)}) collective-permute-start(bf16[432,128]{1,0:T(8,128)(2,1)S(1)} %slice_add_fusion.4), channel_id=1, source_target_pairs={{0,3},{1,0},{2,1},{3,2},{4,7},{5,4},{6,5},{7,6},{8,11},{9,8},{10,9... | collective-permute-start | bytes 331784 | tf_op jit(solution)/shard_map/ppermute | solution.py:464
  77.6 4.6 %collective-permute-done.23 = bf16[432,128]{1,0:T(8,128)(2,1)S(1)} collective-permute-done((bf16[432,128]{1,0:T(8,128)(2,1)S(1)}, bf16[432,128]{1,0:T(8,128)(2,1)S(1)}, u32[]{:S(2)}, u32[]{:S(2)}) %collective-permute-start.23) | collective-permute-done | bytes 110624 | tf_op jit(solution)/shard_map/ppermute | solution.py:464
  82.1 2.8 %collective-permute-start.24 = (bf16[432,128]{1,0:T(8,128)(2,1)S(1)}, bf16[432,128]{1,0:T(8,128)(2,1)S(1)}, u32[]{:S(2)}, u32[]{:S(2)}) collective-permute-start(bf16[432,128]{1,0:T(8,128)(2,1)S(1)} %collective-permute-done.23), channel_id=1, source_target_pairs={{0,3},{1,0},{2,1},{3,2},{4,7},{5,4},{6,5},{7,6},{8,11},{9,8},{10,9... | collective-permute-start | bytes 331784 | tf_op jit(solution)/shard_map/ppermute | solution.py:464
  86.7 18.2 %volume.1 = f32[16,8,4096]{2,1,0:T(8,128)} custom-call(s32[5]{0:T(128)S(1)} %pad_add_fusion.1.facts, bf16[880,128]{1,0:T(8,128)(2,1)S(1)} %get-tuple-element.27.band0, bf16[880,128]{1,0:T(8,128)(2,1)S(1)} %collective-permute-done.19.band1, bf16[448,128]{1,0:T(8,128)(2,1)S(1)} %collective-permute-done.21.band2, ...), custom_call_target="tpu_custom_call" | custom-call | tf_op jit(solution)/shard_map/volume/pallas_call | solution.py:408
  (79 shorter events, 15.1 us)
Async XLA Ops:
  0.9 5.3 %collective-permute-start = (bf16[24]{0:T(256)(128)(2,1)S(1)}, bf16[24]{0:T(256)(128)(2,1)S(1)}, u32[]{:S(2)}, u32[]{:S(2)}) collective-permute-start(bf16[24]{0:T(256)(128)(2,1)S(1)} %reshape.92), channel_id=1, source_target_pairs={{0,4},{4,0},{1,5},{5,1},{2,6},{6,2},{3,7},{7,3},{8,12},{12,8},{9,1... | collective-permute-start | bytes 152 | tf_op jit(solution)/shard_map/ppermute | solution.py:450
  6.3 6.6 %collective-permute-start.1 = (bf16[560,128]{1,0:T(8,128)(2,1)S(1)}, bf16[560,128]{1,0:T(8,128)(2,1)S(1)}, u32[]{:S(2)}, u32[]{:S(2)}) collective-permute-start(bf16[560,128]{1,0:T(8,128)(2,1)S(1)} %pad_maximum_fusion), channel_id=1, source_target_pairs={{0,8},{8,16},{16,24},{24,0},{1,9},{9,17},{17,25},{25,1},{2,10},{10... | collective-permute-start | bytes 430088 | tf_op jit(solution)/shard_map/ppermute | solution.py:464
  6.4 8.4 %collective-permute-start.2 = (bf16[560,128]{1,0:T(8,128)(2,1)S(1)}, bf16[560,128]{1,0:T(8,128)(2,1)S(1)}, u32[]{:S(2)}, u32[]{:S(2)}) collective-permute-start(bf16[560,128]{1,0:T(8,128)(2,1)S(1)} %pad_maximum_fusion), channel_id=1, source_target_pairs={{0,24},{8,0},{16,8},{24,16},{1,25},{9,1},{17,9},{25,17},{2,26},{10... | collective-permute-start | bytes 430088 | tf_op jit(solution)/shard_map/ppermute | solution.py:464
  9.1 6.3 %collective-permute-start.3 = (bf16[560,128]{1,0:T(8,128)(2,1)S(1)}, bf16[560,128]{1,0:T(8,128)(2,1)S(1)}, u32[]{:S(2)}, u32[]{:S(2)}) collective-permute-start(bf16[560,128]{1,0:T(8,128)(2,1)S(1)} %pad_maximum_fusion), channel_id=1, source_target_pairs={{0,16},{8,24},{16,0},{24,8},{1,17},{9,25},{17,1},{25,9},{2,18},{10... | collective-permute-start | bytes 430088 | tf_op jit(solution)/shard_map/ppermute | solution.py:464
  12.9 10.3 %collective-permute-start.10 = (bf16[1120,128]{1,0:T(8,128)(2,1)S(1)}, bf16[1120,128]{1,0:T(8,128)(2,1)S(1)}, u32[]{:S(2)}, u32[]{:S(2)}) collective-permute-start(bf16[1120,128]{1,0:T(8,128)(2,1)S(1)} %constant_dynamic-update-slice_fusion.refs_0_), channel_id=1, source_target_pairs={{0,32},{32,64},{64,96},{96,128},{128,160},{160,192},{192,224},{224... | collective-permute-start | bytes 860168 | tf_op jit(solution)/shard_map/ppermute | solution.py:464
  15.4 10.8 %collective-permute-start.5 = (bf16[1120,128]{1,0:T(8,128)(2,1)S(1)}, bf16[1120,128]{1,0:T(8,128)(2,1)S(1)}, u32[]{:S(2)}, u32[]{:S(2)}) collective-permute-start(bf16[1120,128]{1,0:T(8,128)(2,1)S(1)} %constant_dynamic-update-slice_fusion.5.refs_1_), channel_id=1, source_target_pairs={{0,224},{32,0},{64,32},{96,64},{128,96},{160,128},{192,160},{224,1... | collective-permute-start | bytes 860168 | tf_op jit(solution)/shard_map/ppermute | solution.py:464
  20.9 11.4 %collective-permute-start.4 = (bf16[1120,128]{1,0:T(8,128)(2,1)S(1)}, bf16[1120,128]{1,0:T(8,128)(2,1)S(1)}, u32[]{:S(2)}, u32[]{:S(2)}) collective-permute-start(bf16[1120,128]{1,0:T(8,128)(2,1)S(1)} %constant_dynamic-update-slice_fusion.refs_0_), channel_id=1, source_target_pairs={{0,224},{32,0},{64,32},{96,64},{128,96},{160,128},{192,160},{224,1... | collective-permute-start | bytes 860168 | tf_op jit(solution)/shard_map/ppermute | solution.py:464
  21.6 14.1 %collective-permute-start.13 = (bf16[1120,128]{1,0:T(8,128)(2,1)S(1)}, bf16[1120,128]{1,0:T(8,128)(2,1)S(1)}, u32[]{:S(2)}, u32[]{:S(2)}) collective-permute-start(bf16[1120,128]{1,0:T(8,128)(2,1)S(1)} %constant_dynamic-update-slice_fusion.5.refs_1_), channel_id=1, source_target_pairs={{0,32},{32,64},{64,96},{96,128},{128,160},{160,192},{192,224},{224... | collective-permute-start | bytes 860168 | tf_op jit(solution)/shard_map/ppermute | solution.py:464
  23.2 12.8 %collective-permute-start.11 = (bf16[1120,128]{1,0:T(8,128)(2,1)S(1)}, bf16[1120,128]{1,0:T(8,128)(2,1)S(1)}, u32[]{:S(2)}, u32[]{:S(2)}) collective-permute-start(bf16[1120,128]{1,0:T(8,128)(2,1)S(1)} %collective-permute-done.10.refs_12_), channel_id=1, source_target_pairs={{0,32},{32,64},{64,96},{96,128},{128,160},{160,192},{192,224},{224... | collective-permute-start | bytes 860168 | tf_op jit(solution)/shard_map/ppermute | solution.py:464
  26.2 12.3 %collective-permute-start.7 = (bf16[1120,128]{1,0:T(8,128)(2,1)S(1)}, bf16[1120,128]{1,0:T(8,128)(2,1)S(1)}, u32[]{:S(2)}, u32[]{:S(2)}) collective-permute-start(bf16[1120,128]{1,0:T(8,128)(2,1)S(1)} %collective-permute-done.5.refs_3_), channel_id=1, source_target_pairs={{0,224},{32,0},{64,32},{96,64},{128,96},{160,128},{192,160},{224,1... | collective-permute-start | bytes 860168 | tf_op jit(solution)/shard_map/ppermute | solution.py:464
  32.4 12.3 %collective-permute-start.6 = (bf16[1120,128]{1,0:T(8,128)(2,1)S(1)}, bf16[1120,128]{1,0:T(8,128)(2,1)}, u32[]{:S(2)}, u32[]{:S(2)}) collective-permute-start(bf16[1120,128]{1,0:T(8,128)(2,1)S(1)} %collective-permute-done.4.refs_2_), channel_id=1, source_target_pairs={{0,224},{32,0},{64,32},{96,64},{128,96},{160,128},{192,160},{224,1... | collective-permute-start | bytes 860168 | tf_op jit(solution)/shard_map/ppermute | solution.py:464
  35.8 12.4 %collective-permute-start.14 = (bf16[1120,128]{1,0:T(8,128)(2,1)S(1)}, bf16[1120,128]{1,0:T(8,128)(2,1)}, u32[]{:S(2)}, u32[]{:S(2)}) collective-permute-start(bf16[1120,128]{1,0:T(8,128)(2,1)S(1)} %collective-permute-done.13.refs_13_), channel_id=1, source_target_pairs={{0,32},{32,64},{64,96},{96,128},{128,160},{160,192},{192,224},{224... | collective-permute-start | bytes 860168 | tf_op jit(solution)/shard_map/ppermute | solution.py:464
  35.9 12.3 %collective-permute-start.12 = (bf16[1120,128]{1,0:T(8,128)(2,1)S(1)}, bf16[1120,128]{1,0:T(8,128)(2,1)}, u32[]{:S(2)}, u32[]{:S(2)}) collective-permute-start(bf16[1120,128]{1,0:T(8,128)(2,1)S(1)} %collective-permute-done.11.refs_10_), channel_id=1, source_target_pairs={{0,32},{32,64},{64,96},{96,128},{128,160},{160,192},{192,224},{224... | collective-permute-start | bytes 860168 | tf_op jit(solution)/shard_map/ppermute | solution.py:464
  38.5 12.3 %collective-permute-start.9 = (bf16[1120,128]{1,0:T(8,128)(2,1)S(1)}, bf16[1120,128]{1,0:T(8,128)(2,1)}, u32[]{:S(2)}, u32[]{:S(2)}) collective-permute-start(bf16[1120,128]{1,0:T(8,128)(2,1)S(1)} %collective-permute-done.7.refs_5_), channel_id=1, source_target_pairs={{0,224},{32,0},{64,32},{96,64},{128,96},{160,128},{192,160},{224,1... | collective-permute-start | bytes 860168 | tf_op jit(solution)/shard_map/ppermute | solution.py:464
  44.7 13.3 %collective-permute-start.8 = (bf16[1120,128]{1,0:T(8,128)(2,1)}, bf16[1120,128]{1,0:T(8,128)(2,1)}, u32[]{:S(2)}, u32[]{:S(2)}) collective-permute-start(bf16[1120,128]{1,0:T(8,128)(2,1)} %collective-permute-done.6.refs_4_), channel_id=1, source_target_pairs={{0,224},{32,0},{64,32},{96,64},{128,96},{160,128},{192,160},{224,1... | collective-permute-start | bytes 860168 | tf_op jit(solution)/shard_map/ppermute | solution.py:464
  48.2 9.8 %collective-permute-start.15 = (bf16[1120,128]{1,0:T(8,128)(2,1)}, bf16[1120,128]{1,0:T(8,128)(2,1)}, u32[]{:S(2)}, u32[]{:S(2)}) collective-permute-start(bf16[1120,128]{1,0:T(8,128)(2,1)} %collective-permute-done.14.refs_11_), channel_id=1, source_target_pairs={{0,32},{32,64},{64,96},{96,128},{128,160},{160,192},{192,224},{224... | collective-permute-start | bytes 860168 | tf_op jit(solution)/shard_map/ppermute | solution.py:464
  48.3 12.6 %collective-permute-start.16 = (bf16[1120,128]{1,0:T(8,128)(2,1)}, bf16[1120,128]{1,0:T(8,128)(2,1)S(1)}, u32[]{:S(2)}, u32[]{:S(2)}) collective-permute-start(bf16[1120,128]{1,0:T(8,128)(2,1)} %collective-permute-done.12.refs_8_), channel_id=1, source_target_pairs={{0,32},{32,64},{64,96},{96,128},{128,160},{160,192},{192,224},{224... | collective-permute-start | bytes 860168 | tf_op jit(solution)/shard_map/ppermute | solution.py:464
  50.8 12.4 %collective-permute-start.17 = (bf16[1120,128]{1,0:T(8,128)(2,1)}, bf16[1120,128]{1,0:T(8,128)(2,1)S(1)}, u32[]{:S(2)}, u32[]{:S(2)}) collective-permute-start(bf16[1120,128]{1,0:T(8,128)(2,1)} %collective-permute-done.9.refs_7_), channel_id=1, source_target_pairs={{0,224},{32,0},{64,32},{96,64},{128,96},{160,128},{192,160},{224,1... | collective-permute-start | bytes 860168 | tf_op jit(solution)/shard_map/ppermute | solution.py:464
  66.3 5.1 %collective-permute-start.18 = (bf16[3520,128]{1,0:T(8,128)(2,1)S(1)}, bf16[3520,128]{1,0:T(8,128)(2,1)S(1)}, u32[]{:S(2)}, u32[]{:S(2)}) collective-permute-start(bf16[3520,128]{1,0:T(8,128)(2,1)S(1)} %select_pieces.3), channel_id=1, source_target_pairs={{0,4},{4,0},{1,5},{5,1},{2,6},{6,2},{3,7},{7,3},{8,12},{12,8},{9,1... | collective-permute-start | bytes 2703368 | tf_op jit(solution)/shard_map/ppermute | solution.py:489
  71.4 6.1 %collective-permute-start.20 = (bf16[448,128]{1,0:T(8,128)(2,1)S(1)}, bf16[448,128]{1,0:T(8,128)(2,1)S(1)}, u32[]{:S(2)}, u32[]{:S(2)}) collective-permute-start(bf16[448,128]{1,0:T(8,128)(2,1)S(1)} %slice_add_fusion.3), channel_id=1, source_target_pairs={{0,1},{1,2},{2,3},{3,0},{4,5},{5,6},{6,7},{7,4},{8,9},{9,10},{10,1... | collective-permute-start | bytes 344072 | tf_op jit(solution)/shard_map/ppermute | solution.py:464
  72.9 13.7 %collective-permute-start.22 = (bf16[880,128]{1,0:T(8,128)(2,1)S(1)}, bf16[880,128]{1,0:T(8,128)(2,1)S(1)}, u32[]{:S(2)}, u32[]{:S(2)}) collective-permute-start(bf16[880,128]{1,0:T(8,128)(2,1)S(1)} %get-tuple-element.25), channel_id=1, source_target_pairs={{0,3},{1,0},{2,1},{3,2},{4,7},{5,4},{6,5},{7,6},{8,11},{9,8},{10,9... | collective-permute-start | bytes 675848 | tf_op jit(solution)/shard_map/ppermute | solution.py:464
  74.4 12.2 %collective-permute-start.19 = (bf16[880,128]{1,0:T(8,128)(2,1)S(1)}, bf16[880,128]{1,0:T(8,128)(2,1)S(1)}, u32[]{:S(2)}, u32[]{:S(2)}) collective-permute-start(bf16[880,128]{1,0:T(8,128)(2,1)S(1)} %get-tuple-element.26), channel_id=1, source_target_pairs={{0,1},{1,2},{2,3},{3,0},{4,5},{5,6},{6,7},{7,4},{8,9},{9,10},{10,1... | collective-permute-start | bytes 675848 | tf_op jit(solution)/shard_map/ppermute | solution.py:464
  74.5 7.7 %collective-permute-start.23 = (bf16[432,128]{1,0:T(8,128)(2,1)S(1)}, bf16[432,128]{1,0:T(8,128)(2,1)S(1)}, u32[]{:S(2)}, u32[]{:S(2)}) collective-permute-start(bf16[432,128]{1,0:T(8,128)(2,1)S(1)} %slice_add_fusion.4), channel_id=1, source_target_pairs={{0,3},{1,0},{2,1},{3,2},{4,7},{5,4},{6,5},{7,6},{8,11},{9,8},{10,9... | collective-permute-start | bytes 331784 | tf_op jit(solution)/shard_map/ppermute | solution.py:464
  77.6 9.1 %collective-permute-start.21 = (bf16[448,128]{1,0:T(8,128)(2,1)S(1)}, bf16[448,128]{1,0:T(8,128)(2,1)S(1)}, u32[]{:S(2)}, u32[]{:S(2)}) collective-permute-start(bf16[448,128]{1,0:T(8,128)(2,1)S(1)} %collective-permute-done.20), channel_id=1, source_target_pairs={{0,1},{1,2},{2,3},{3,0},{4,5},{5,6},{6,7},{7,4},{8,9},{9,10},{10,1... | collective-permute-start | bytes 344072 | tf_op jit(solution)/shard_map/ppermute | solution.py:464
  (9 other events, 235.3 us)

commit v6 on v5

--- a/solution.py
+++ b/solution.py
@@ -254,7 +254,7 @@
 
 def volume_body(
     facts, band0, band1, band2, band3, band4, ref, summing, first_bias, second_bias, first_far, second_far, out_far,
-    turned, refx, factors, sums, padded, hidden, keep, wide, first, second, out, loaded, stored,
+    turned, refx, factors, sums, padded, hidden0, hidden1, keep, wide, first, second, out, loaded, stored,
 ):
     first_copy = pltpu.make_async_copy(first_far, first, loaded.at[0])
     second_copy = pltpu.make_async_copy(second_far, second, loaded.at[1])
@@ -301,7 +301,9 @@
     inside &= (block <= jnp.where(facts[4] >= 0, BLOCKS - 1, BLOCKS - 2))
     keep[...] = jnp.where(inside, 1.0, 0.0)
     sums[ROWS:, :] = jnp.zeros((sums.shape[0] - ROWS, 256), f32)
-    hidden[ROWS:, :] = jnp.zeros((hidden.shape[0] - ROWS, 256), f32)
+    hidden_two = (hidden0, hidden1)
+    for hidden in hidden_two:
+        hidden[ROWS:, :] = jnp.zeros((hidden.shape[0] - ROWS, 256), f32)
 
     def cost_step(q, carry):
         for m in range(4):
@@ -312,9 +314,11 @@
                     top = product.astype(bf16)
                     rest = (product - top.astype(f32)).astype(bf16)
                     at = block * 16
-                    factors[at : at + 16, half * 128 : half * 128 + 128] = top
-                    factors[at : at + 16, 256 + half * 128 : 384 + half * 128] = rest
-            cells = jnp.dot(factors[...], summing[...], preferred_element_type=f32)
+                    factors[half, at : at + 16, :] = top
+                    factors[2 + half, at : at + 16, :] = rest
+            cells = jnp.dot(
+                jnp.concatenate([factors[k] for k in range(4)], axis=1), summing[...], preferred_element_type=f32
+            )
             depth = 16 * view + dd - 2
             sums[0:ROWS, :] = jnp.where((depth >= 0) & (depth < NDISP), cells, 0.0)
             from_right = (lane16 & 8) == 8
@@ -332,8 +336,8 @@
                 edge = jnp.where(from_right, next_mixed, last_mixed)
                 tail = jnp.where(lane16 < 64, this_low, edge)
                 line = pl.multiple_of(dd * ROWS + at, 16)
-                padded[pl.ds(line, 16), 0:128] = head.astype(bf16)
-                padded[pl.ds(line, 16), 128:256] = tail.astype(bf16)
+                padded[0, pl.ds(line, 16), :] = head.astype(bf16)
+                padded[1, pl.ds(line, 16), :] = tail.astype(bf16)
                 this_low, last_mixed, this_mixed = next_low, this_mixed, next_mixed
         return carry
 
@@ -341,11 +345,15 @@
 
     lane8 = lax.broadcasted_iota(jnp.int32, (8, 128), 1)
 
-    def hidden_step(step, carry):
+    def hidden_cells(step, hidden):
         cells = jnp.broadcast_to(first_bias[...], (ROWS, 256))
         for a in range(3):
             at = pl.multiple_of((step + a) * ROWS, 16)
-            cells = cells + jnp.dot(padded[pl.ds(at, ROWS), :], first[a], preferred_element_type=f32)
+            cells = cells + jnp.dot(
+                jnp.concatenate([padded[k, pl.ds(at, ROWS), :] for k in range(2)], axis=1),
+                first[a],
+                preferred_element_type=f32,
+            )
         depth = 16 * view + step - 1
         live = jnp.where((depth >= 0) & (depth < NDISP), keep[...], 0.0) > 0.5
         for part in range(2):
@@ -370,13 +378,17 @@
             two = block_cells(2 + 2 * pair)
             at = pl.multiple_of(step * 128 + pair * 16, 16)
             for part in range(8):
-                wide[pl.ds(at, 16), part * 128 : part * 128 + 128] = jnp.concatenate(
+                wide[part, pl.ds(at, 16), :] = jnp.concatenate(
                     [one[part], two[part]], axis=0
                 ).astype(bf16)
+
+    def hidden_step(pair, carry):
+        for k in range(2):
+            hidden_cells(pair * 2 + k, hidden_two[k])
         return carry
 
     first_copy.wait()
-    lax.fori_loop(0, DL + 2, hidden_step, 0)
+    lax.fori_loop(0, DL // 2 + 1, hidden_step, 0)
     second_copy.wait()
 
     def stores(step):
@@ -387,7 +399,11 @@
         cells = jnp.broadcast_to(second_bias[...], (512, 256))
         for a in range(3):
             at = pl.multiple_of((step * 4 + a) * 128, 128)
-            cells = cells + jnp.dot(wide[pl.ds(at, 512), :], second[a], preferred_element_type=f32)
+            cells = cells + jnp.dot(
+                jnp.concatenate([wide[k, pl.ds(at, 512), :] for k in range(8)], axis=1),
+                second[a],
+                preferred_element_type=f32,
+            )
         for d in range(4):
             for block in range(16):
                 at = d * 128 + block * 8
@@ -415,12 +431,13 @@
         scratch_shapes=[
             pltpu.VMEM((4 * 51, 16, 128), f32),
             pltpu.VMEM((2 * BLOCKS, 16, 128), f32),
-            pltpu.VMEM((ROWS, 512), bf16),
+            pltpu.VMEM((4, ROWS, 128), bf16),
             pltpu.VMEM((ROWS + 16, 256), f32),
-            pltpu.VMEM((20 * ROWS, 256), bf16),
+            pltpu.VMEM((2, 20 * ROWS, 128), bf16),
+            pltpu.VMEM((ROWS + 16, 256), f32),
             pltpu.VMEM((ROWS + 16, 256), f32),
             pltpu.VMEM((ROWS, 128), f32),
-            pltpu.VMEM((18 * 128, 1024), bf16),
+            pltpu.VMEM((8, 18 * 128, 128), bf16),
             pltpu.VMEM(first.shape, bf16),
             pltpu.VMEM(second.shape, bf16),
             pltpu.VMEM((DL, H, W * CH), f32),

time: 106 us -> 104 us (0.981)
  Pallas kernels: 29.1 us -> 26.9 us
    pallas_call x1, Pallas kernels: 18.2 us -> 16 us  [volume(): pl.pallas_call(volume_body, out_shape=jax.ShapeDtypeStruct((DL, H, W * CH...]
  transfers between devices with their start and end apart: 25 -> 25, of which waited for: 16 -> 16; matrix products, arithmetic and copies ran while one was open for 3% -> 3% of each run, Pallas kernels for 7% -> 8%
where the time goes in v6:
time: 104 us; the launch traced here: 103 us
  starting transfers between devices  40.6 us (39%)
  waiting for transfers between devices  31 us (30%)
  Pallas kernels  26.9 us (26%)
  local copies, waits for them, and re-layouts  2.71 us (3%)
  other arithmetic  1.2 us (1%)
    ppermute x23, starting transfers between devices, shift(): return lax.ppermute(x, axis, [(i, (i + by) % count) for i in range(count)])  35.5 us
    ppermute x23, waiting for transfers between devices, shift(): return lax.ppermute(x, axis, [(i, (i + by) % count) for i in range(count)])  31 us
    pallas_call x1, Pallas kernels, volume(): pl.pallas_call(volume_body, out_shape=jax.ShapeDtypeStruct((DL, H, W * CH...  16 us
    pallas_call x2, Pallas kernels, select_pieces(): pl.pallas_call(select_body, out_shape=jax.ShapeDtypeStruct((4 * PART, 128...  6.27 us
    ppermute x1, starting transfers between devices, on_device(): twin = lax.ppermute(names, 'c', [(0, 1), (1, 0)])  3.2 us
    pallas_call x1, Pallas kernels, spread_weights(): pl.pallas_call(spread_body, out_shape=(jax.ShapeDtypeStruct((3, 256, 256)...  2.89 us
  transfers between devices with their start and end apart: 25, of which 16 were waited for; matrix products, arithmetic and copies ran while one was open for 3% of the time, Pallas kernels for 8%

profile of v6, /device:TPU:1, one launch (start us, length us, event | category | flops | bytes accessed | tf_op | source)
XLA Modules:
  0.0 102.9 jit_solution(5958701201342795524)
XLA Ops:
  0.9 3.2 %collective-permute-start = (bf16[24]{0:T(256)(128)(2,1)S(1)}, bf16[24]{0:T(256)(128)(2,1)S(1)}, u32[]{:S(2)}, u32[]{:S(2)}) collective-permute-start(bf16[24]{0:T(256)(128)(2,1)S(1)} %reshape.92), channel_id=1, source_target_pairs={{0,4},{4,0},{1,5},{5,1},{2,6},{6,2},{3,7},{7,3},{8,12},{12,8},{9,1... | collective-permute-start | bytes 152 | tf_op jit(solution)/shard_map/ppermute | solution.py:467
  6.4 2.7 %collective-permute-start.2 = (bf16[560,128]{1,0:T(8,128)(2,1)S(1)}, bf16[560,128]{1,0:T(8,128)(2,1)S(1)}, u32[]{:S(2)}, u32[]{:S(2)}) collective-permute-start(bf16[560,128]{1,0:T(8,128)(2,1)S(1)} %pad_maximum_fusion), channel_id=1, source_target_pairs={{0,24},{8,0},{16,8},{24,16},{1,25},{9,1},{17,9},{25,17},{2,26},{10... | collective-permute-start | bytes 430088 | tf_op jit(solution)/shard_map/ppermute | solution.py:481
  9.1 3.8 %collective-permute-done.1 = bf16[560,128]{1,0:T(8,128)(2,1)S(1)} collective-permute-done((bf16[560,128]{1,0:T(8,128)(2,1)S(1)}, bf16[560,128]{1,0:T(8,128)(2,1)S(1)}, u32[]{:S(2)}, u32[]{:S(2)}) %collective-permute-start.1) | collective-permute-done | bytes 143392 | tf_op jit(solution)/shard_map/ppermute | solution.py:481
  13.0 1.8 %collective-permute-done.2 = bf16[560,128]{1,0:T(8,128)(2,1)S(1)} collective-permute-done((bf16[560,128]{1,0:T(8,128)(2,1)S(1)}, bf16[560,128]{1,0:T(8,128)(2,1)S(1)}, u32[]{:S(2)}, u32[]{:S(2)}) %collective-permute-start.2) | collective-permute-done | bytes 143392 | tf_op jit(solution)/shard_map/ppermute | solution.py:481
  15.4 5.5 %collective-permute-start.5 = (bf16[1120,128]{1,0:T(8,128)(2,1)S(1)}, bf16[1120,128]{1,0:T(8,128)(2,1)S(1)}, u32[]{:S(2)}, u32[]{:S(2)}) collective-permute-start(bf16[1120,128]{1,0:T(8,128)(2,1)S(1)} %constant_dynamic-update-slice_fusion.5.refs_1_), channel_id=1, source_target_pairs={{0,224},{32,0},{64,32},{96,64},{128,96},{160,128},{192,160},{224,1... | collective-permute-start | bytes 860168 | tf_op jit(solution)/shard_map/ppermute | solution.py:481
  23.2 3.0 %collective-permute-done.5.refs_3_ = bf16[1120,128]{1,0:T(8,128)(2,1)S(1)} collective-permute-done((bf16[1120,128]{1,0:T(8,128)(2,1)S(1)}, bf16[1120,128]{1,0:T(8,128)(2,1)S(1)}, u32[]{:S(2)}, u32[]{:S(2)}) %collective-permute-start.5) | collective-permute-done | bytes 286752 | tf_op jit(solution)/shard_map/ppermute | solution.py:481
  26.2 3.4 %collective-permute-start.7 = (bf16[1120,128]{1,0:T(8,128)(2,1)S(1)}, bf16[1120,128]{1,0:T(8,128)(2,1)S(1)}, u32[]{:S(2)}, u32[]{:S(2)}) collective-permute-start(bf16[1120,128]{1,0:T(8,128)(2,1)S(1)} %collective-permute-done.5.refs_3_), channel_id=1, source_target_pairs={{0,224},{32,0},{64,32},{96,64},{128,96},{160,128},{192,160},{224,1... | collective-permute-start | bytes 860168 | tf_op jit(solution)/shard_map/ppermute | solution.py:481
  29.6 2.7 %collective-permute-done.4.refs_2_ = bf16[1120,128]{1,0:T(8,128)(2,1)S(1)} collective-permute-done((bf16[1120,128]{1,0:T(8,128)(2,1)S(1)}, bf16[1120,128]{1,0:T(8,128)(2,1)S(1)}, u32[]{:S(2)}, u32[]{:S(2)}) %collective-permute-start.4) | collective-permute-done | bytes 286752 | tf_op jit(solution)/shard_map/ppermute | solution.py:481
  32.4 3.4 %collective-permute-start.6 = (bf16[1120,128]{1,0:T(8,128)(2,1)S(1)}, bf16[1120,128]{1,0:T(8,128)(2,1)}, u32[]{:S(2)}, u32[]{:S(2)}) collective-permute-start(bf16[1120,128]{1,0:T(8,128)(2,1)S(1)} %collective-permute-done.4.refs_2_), channel_id=1, source_target_pairs={{0,224},{32,0},{64,32},{96,64},{128,96},{160,128},{192,160},{224,1... | collective-permute-start | bytes 860168 | tf_op jit(solution)/shard_map/ppermute | solution.py:481
  35.9 2.6 %collective-permute-done.7.refs_5_ = bf16[1120,128]{1,0:T(8,128)(2,1)S(1)} collective-permute-done((bf16[1120,128]{1,0:T(8,128)(2,1)S(1)}, bf16[1120,128]{1,0:T(8,128)(2,1)S(1)}, u32[]{:S(2)}, u32[]{:S(2)}) %collective-permute-start.7) | collective-permute-done | bytes 286752 | tf_op jit(solution)/shard_map/ppermute | solution.py:481
  38.5 3.4 %collective-permute-start.9 = (bf16[1120,128]{1,0:T(8,128)(2,1)S(1)}, bf16[1120,128]{1,0:T(8,128)(2,1)}, u32[]{:S(2)}, u32[]{:S(2)}) collective-permute-start(bf16[1120,128]{1,0:T(8,128)(2,1)S(1)} %collective-permute-done.7.refs_5_), channel_id=1, source_target_pairs={{0,224},{32,0},{64,32},{96,64},{128,96},{160,128},{192,160},{224,1... | collective-permute-start | bytes 860168 | tf_op jit(solution)/shard_map/ppermute | solution.py:481
  41.9 2.7 %collective-permute-done.6.refs_4_ = bf16[1120,128]{1,0:T(8,128)(2,1)} collective-permute-done((bf16[1120,128]{1,0:T(8,128)(2,1)S(1)}, bf16[1120,128]{1,0:T(8,128)(2,1)}, u32[]{:S(2)}, u32[]{:S(2)}) %collective-permute-start.6) | collective-permute-done | bytes 286752 | tf_op jit(solution)/shard_map/ppermute | solution.py:481
  44.7 3.5 %collective-permute-start.8 = (bf16[1120,128]{1,0:T(8,128)(2,1)}, bf16[1120,128]{1,0:T(8,128)(2,1)}, u32[]{:S(2)}, u32[]{:S(2)}) collective-permute-start(bf16[1120,128]{1,0:T(8,128)(2,1)} %collective-permute-done.6.refs_4_), channel_id=1, source_target_pairs={{0,224},{32,0},{64,32},{96,64},{128,96},{160,128},{192,160},{224,1... | collective-permute-start | bytes 860168 | tf_op jit(solution)/shard_map/ppermute | solution.py:481
  48.3 2.5 %collective-permute-done.9.refs_7_ = bf16[1120,128]{1,0:T(8,128)(2,1)} collective-permute-done((bf16[1120,128]{1,0:T(8,128)(2,1)S(1)}, bf16[1120,128]{1,0:T(8,128)(2,1)}, u32[]{:S(2)}, u32[]{:S(2)}) %collective-permute-start.9) | collective-permute-done | bytes 286752 | tf_op jit(solution)/shard_map/ppermute | solution.py:481
  50.8 3.5 %collective-permute-start.17 = (bf16[1120,128]{1,0:T(8,128)(2,1)}, bf16[1120,128]{1,0:T(8,128)(2,1)S(1)}, u32[]{:S(2)}, u32[]{:S(2)}) collective-permute-start(bf16[1120,128]{1,0:T(8,128)(2,1)} %collective-permute-done.9.refs_7_), channel_id=1, source_target_pairs={{0,224},{32,0},{64,32},{96,64},{128,96},{160,128},{192,160},{224,1... | collective-permute-start | bytes 860168 | tf_op jit(solution)/shard_map/ppermute | solution.py:481
  54.9 2.9 %spread_weights.1 = (bf16[3,256,256]{2,1,0:T(8,128)(2,1)}, bf16[3,1024,256]{2,1,0:T(8,128)(2,1)}) custom-call(bf16[216,32]{1,0:T(8,128)(2,1)} %bitcast.19, bf16[864,32]{1,0:T(8,128)(2,1)} %bitcast.17), custom_call_target="tpu_custom_call" | custom-call | tf_op jit(solution)/shard_map/spread_weights/pallas_call | solution.py:82
  60.9 2.3 %collective-permute-done.17.refs_2_ = bf16[1120,128]{1,0:T(8,128)(2,1)S(1)} collective-permute-done((bf16[1120,128]{1,0:T(8,128)(2,1)}, bf16[1120,128]{1,0:T(8,128)(2,1)S(1)}, u32[]{:S(2)}, u32[]{:S(2)}) %collective-permute-start.17) | collective-permute-done | bytes 286752 | tf_op jit(solution)/shard_map/ppermute | solution.py:481
  63.2 3.1 %select_pieces.3 = bf16[3520,128]{1,0:T(8,128)(2,1)S(1)} custom-call(s32[256]{0:T(256)S(1)} %reshape.86.links, s32[4]{0:T(128)S(1)} %get-tuple-element.20.where_am_i, bf16[15680,128]{1,0:T(8,128)(2,1)S(1)} %merge_chunks.1.refs_0_, bf16[1120,128]{1,0:T(8,128)(2,1)S(1)} %collective-permute-done.16.refs_1_, bf16[1120,128]{1,0:T(8,128)(2,1)S(1)} %collective-permute-done.17.refs_2_), custom_call_target="tpu_custom_call" | custom-call | tf_op jit(solution)/shard_map/select_pieces/pallas_call | solution.py:229
  66.3 1.9 %collective-permute-start.18 = (bf16[3520,128]{1,0:T(8,128)(2,1)S(1)}, bf16[3520,128]{1,0:T(8,128)(2,1)S(1)}, u32[]{:S(2)}, u32[]{:S(2)}) collective-permute-start(bf16[3520,128]{1,0:T(8,128)(2,1)S(1)} %select_pieces.3), channel_id=1, source_target_pairs={{0,4},{4,0},{1,5},{5,1},{2,6},{6,2},{3,7},{7,3},{8,12},{12,8},{9,1... | collective-permute-start | bytes 2703368 | tf_op jit(solution)/shard_map/ppermute | solution.py:506
  68.2 3.1 %select_pieces.2 = bf16[3520,128]{1,0:T(8,128)(2,1)S(1)} custom-call(s32[256]{0:T(256)S(1)} %reshape.86.links, s32[4]{0:T(128)S(1)} %get-tuple-element.19.where_am_i, bf16[15680,128]{1,0:T(8,128)(2,1)S(1)} %merge_chunks.1.refs_0_, bf16[1120,128]{1,0:T(8,128)(2,1)S(1)} %collective-permute-done.16.refs_1_, bf16[1120,128]{1,0:T(8,128)(2,1)S(1)} %collective-permute-done.17.refs_2_), custom_call_target="tpu_custom_call" | custom-call | tf_op jit(solution)/shard_map/select_pieces/pallas_call | solution.py:229
  74.5 2.8 %collective-permute-start.23 = (bf16[432,128]{1,0:T(8,128)(2,1)S(1)}, bf16[432,128]{1,0:T(8,128)(2,1)S(1)}, u32[]{:S(2)}, u32[]{:S(2)}) collective-permute-start(bf16[432,128]{1,0:T(8,128)(2,1)S(1)} %slice_add_fusion.4), channel_id=1, source_target_pairs={{0,3},{1,0},{2,1},{3,2},{4,7},{5,4},{6,5},{7,6},{8,11},{9,8},{10,9... | collective-permute-start | bytes 331784 | tf_op jit(solution)/shard_map/ppermute | solution.py:481
  77.6 4.6 %collective-permute-done.23 = bf16[432,128]{1,0:T(8,128)(2,1)S(1)} collective-permute-done((bf16[432,128]{1,0:T(8,128)(2,1)S(1)}, bf16[432,128]{1,0:T(8,128)(2,1)S(1)}, u32[]{:S(2)}, u32[]{:S(2)}) %collective-permute-start.23) | collective-permute-done | bytes 110624 | tf_op jit(solution)/shard_map/ppermute | solution.py:481
  82.1 2.8 %collective-permute-start.24 = (bf16[432,128]{1,0:T(8,128)(2,1)S(1)}, bf16[432,128]{1,0:T(8,128)(2,1)S(1)}, u32[]{:S(2)}, u32[]{:S(2)}) collective-permute-start(bf16[432,128]{1,0:T(8,128)(2,1)S(1)} %collective-permute-done.23), channel_id=1, source_target_pairs={{0,3},{1,0},{2,1},{3,2},{4,7},{5,4},{6,5},{7,6},{8,11},{9,8},{10,9... | collective-permute-start | bytes 331784 | tf_op jit(solution)/shard_map/ppermute | solution.py:481
  86.7 16.0 %volume.1 = f32[16,8,4096]{2,1,0:T(8,128)} custom-call(s32[5]{0:T(128)S(1)} %pad_add_fusion.1.facts, bf16[880,128]{1,0:T(8,128)(2,1)S(1)} %get-tuple-element.27.band0, bf16[880,128]{1,0:T(8,128)(2,1)S(1)} %collective-permute-done.19.band1, bf16[448,128]{1,0:T(8,128)(2,1)S(1)} %collective-permute-done.21.band2, ...), custom_call_target="tpu_custom_call" | custom-call | tf_op jit(solution)/shard_map/volume/pallas_call | solution.py:424
  (79 shorter events, 15.1 us)
Async XLA Ops:
  0.9 5.3 %collective-permute-start = (bf16[24]{0:T(256)(128)(2,1)S(1)}, bf16[24]{0:T(256)(128)(2,1)S(1)}, u32[]{:S(2)}, u32[]{:S(2)}) collective-permute-start(bf16[24]{0:T(256)(128)(2,1)S(1)} %reshape.92), channel_id=1, source_target_pairs={{0,4},{4,0},{1,5},{5,1},{2,6},{6,2},{3,7},{7,3},{8,12},{12,8},{9,1... | collective-permute-start | bytes 152 | tf_op jit(solution)/shard_map/ppermute | solution.py:467
  6.3 6.6 %collective-permute-start.1 = (bf16[560,128]{1,0:T(8,128)(2,1)S(1)}, bf16[560,128]{1,0:T(8,128)(2,1)S(1)}, u32[]{:S(2)}, u32[]{:S(2)}) collective-permute-start(bf16[560,128]{1,0:T(8,128)(2,1)S(1)} %pad_maximum_fusion), channel_id=1, source_target_pairs={{0,8},{8,16},{16,24},{24,0},{1,9},{9,17},{17,25},{25,1},{2,10},{10... | collective-permute-start | bytes 430088 | tf_op jit(solution)/shard_map/ppermute | solution.py:481
  6.4 8.4 %collective-permute-start.2 = (bf16[560,128]{1,0:T(8,128)(2,1)S(1)}, bf16[560,128]{1,0:T(8,128)(2,1)S(1)}, u32[]{:S(2)}, u32[]{:S(2)}) collective-permute-start(bf16[560,128]{1,0:T(8,128)(2,1)S(1)} %pad_maximum_fusion), channel_id=1, source_target_pairs={{0,24},{8,0},{16,8},{24,16},{1,25},{9,1},{17,9},{25,17},{2,26},{10... | collective-permute-start | bytes 430088 | tf_op jit(solution)/shard_map/ppermute | solution.py:481
  9.1 6.3 %collective-permute-start.3 = (bf16[560,128]{1,0:T(8,128)(2,1)S(1)}, bf16[560,128]{1,0:T(8,128)(2,1)S(1)}, u32[]{:S(2)}, u32[]{:S(2)}) collective-permute-start(bf16[560,128]{1,0:T(8,128)(2,1)S(1)} %pad_maximum_fusion), channel_id=1, source_target_pairs={{0,16},{8,24},{16,0},{24,8},{1,17},{9,25},{17,1},{25,9},{2,18},{10... | collective-permute-start | bytes 430088 | tf_op jit(solution)/shard_map/ppermute | solution.py:481
  12.9 10.3 %collective-permute-start.10 = (bf16[1120,128]{1,0:T(8,128)(2,1)S(1)}, bf16[1120,128]{1,0:T(8,128)(2,1)S(1)}, u32[]{:S(2)}, u32[]{:S(2)}) collective-permute-start(bf16[1120,128]{1,0:T(8,128)(2,1)S(1)} %constant_dynamic-update-slice_fusion.refs_0_), channel_id=1, source_target_pairs={{0,32},{32,64},{64,96},{96,128},{128,160},{160,192},{192,224},{224... | collective-permute-start | bytes 860168 | tf_op jit(solution)/shard_map/ppermute | solution.py:481
  15.4 10.8 %collective-permute-start.5 = (bf16[1120,128]{1,0:T(8,128)(2,1)S(1)}, bf16[1120,128]{1,0:T(8,128)(2,1)S(1)}, u32[]{:S(2)}, u32[]{:S(2)}) collective-permute-start(bf16[1120,128]{1,0:T(8,128)(2,1)S(1)} %constant_dynamic-update-slice_fusion.5.refs_1_), channel_id=1, source_target_pairs={{0,224},{32,0},{64,32},{96,64},{128,96},{160,128},{192,160},{224,1... | collective-permute-start | bytes 860168 | tf_op jit(solution)/shard_map/ppermute | solution.py:481
  20.9 11.4 %collective-permute-start.4 = (bf16[1120,128]{1,0:T(8,128)(2,1)S(1)}, bf16[1120,128]{1,0:T(8,128)(2,1)S(1)}, u32[]{:S(2)}, u32[]{:S(2)}) collective-permute-start(bf16[1120,128]{1,0:T(8,128)(2,1)S(1)} %constant_dynamic-update-slice_fusion.refs_0_), channel_id=1, source_target_pairs={{0,224},{32,0},{64,32},{96,64},{128,96},{160,128},{192,160},{224,1... | collective-permute-start | bytes 860168 | tf_op jit(solution)/shard_map/ppermute | solution.py:481
  21.6 14.1 %collective-permute-start.13 = (bf16[1120,128]{1,0:T(8,128)(2,1)S(1)}, bf16[1120,128]{1,0:T(8,128)(2,1)S(1)}, u32[]{:S(2)}, u32[]{:S(2)}) collective-permute-start(bf16[1120,128]{1,0:T(8,128)(2,1)S(1)} %constant_dynamic-update-slice_fusion.5.refs_1_), channel_id=1, source_target_pairs={{0,32},{32,64},{64,96},{96,128},{128,160},{160,192},{192,224},{224... | collective-permute-start | bytes 860168 | tf_op jit(solution)/shard_map/ppermute | solution.py:481
  23.2 12.8 %collective-permute-start.11 = (bf16[1120,128]{1,0:T(8,128)(2,1)S(1)}, bf16[1120,128]{1,0:T(8,128)(2,1)S(1)}, u32[]{:S(2)}, u32[]{:S(2)}) collective-permute-start(bf16[1120,128]{1,0:T(8,128)(2,1)S(1)} %collective-permute-done.10.refs_12_), channel_id=1, source_target_pairs={{0,32},{32,64},{64,96},{96,128},{128,160},{160,192},{192,224},{224... | collective-permute-start | bytes 860168 | tf_op jit(solution)/shard_map/ppermute | solution.py:481
  26.2 12.3 %collective-permute-start.7 = (bf16[1120,128]{1,0:T(8,128)(2,1)S(1)}, bf16[1120,128]{1,0:T(8,128)(2,1)S(1)}, u32[]{:S(2)}, u32[]{:S(2)}) collective-permute-start(bf16[1120,128]{1,0:T(8,128)(2,1)S(1)} %collective-permute-done.5.refs_3_), channel_id=1, source_target_pairs={{0,224},{32,0},{64,32},{96,64},{128,96},{160,128},{192,160},{224,1... | collective-permute-start | bytes 860168 | tf_op jit(solution)/shard_map/ppermute | solution.py:481
  32.4 12.3 %collective-permute-start.6 = (bf16[1120,128]{1,0:T(8,128)(2,1)S(1)}, bf16[1120,128]{1,0:T(8,128)(2,1)}, u32[]{:S(2)}, u32[]{:S(2)}) collective-permute-start(bf16[1120,128]{1,0:T(8,128)(2,1)S(1)} %collective-permute-done.4.refs_2_), channel_id=1, source_target_pairs={{0,224},{32,0},{64,32},{96,64},{128,96},{160,128},{192,160},{224,1... | collective-permute-start | bytes 860168 | tf_op jit(solution)/shard_map/ppermute | solution.py:481
  35.8 12.4 %collective-permute-start.14 = (bf16[1120,128]{1,0:T(8,128)(2,1)S(1)}, bf16[1120,128]{1,0:T(8,128)(2,1)}, u32[]{:S(2)}, u32[]{:S(2)}) collective-permute-start(bf16[1120,128]{1,0:T(8,128)(2,1)S(1)} %collective-permute-done.13.refs_13_), channel_id=1, source_target_pairs={{0,32},{32,64},{64,96},{96,128},{128,160},{160,192},{192,224},{224... | collective-permute-start | bytes 860168 | tf_op jit(solution)/shard_map/ppermute | solution.py:481
  35.9 12.3 %collective-permute-start.12 = (bf16[1120,128]{1,0:T(8,128)(2,1)S(1)}, bf16[1120,128]{1,0:T(8,128)(2,1)}, u32[]{:S(2)}, u32[]{:S(2)}) collective-permute-start(bf16[1120,128]{1,0:T(8,128)(2,1)S(1)} %collective-permute-done.11.refs_10_), channel_id=1, source_target_pairs={{0,32},{32,64},{64,96},{96,128},{128,160},{160,192},{192,224},{224... | collective-permute-start | bytes 860168 | tf_op jit(solution)/shard_map/ppermute | solution.py:481
  38.5 12.3 %collective-permute-start.9 = (bf16[1120,128]{1,0:T(8,128)(2,1)S(1)}, bf16[1120,128]{1,0:T(8,128)(2,1)}, u32[]{:S(2)}, u32[]{:S(2)}) collective-permute-start(bf16[1120,128]{1,0:T(8,128)(2,1)S(1)} %collective-permute-done.7.refs_5_), channel_id=1, source_target_pairs={{0,224},{32,0},{64,32},{96,64},{128,96},{160,128},{192,160},{224,1... | collective-permute-start | bytes 860168 | tf_op jit(solution)/shard_map/ppermute | solution.py:481
  44.7 13.3 %collective-permute-start.8 = (bf16[1120,128]{1,0:T(8,128)(2,1)}, bf16[1120,128]{1,0:T(8,128)(2,1)}, u32[]{:S(2)}, u32[]{:S(2)}) collective-permute-start(bf16[1120,128]{1,0:T(8,128)(2,1)} %collective-permute-done.6.refs_4_), channel_id=1, source_target_pairs={{0,224},{32,0},{64,32},{96,64},{128,96},{160,128},{192,160},{224,1... | collective-permute-start | bytes 860168 | tf_op jit(solution)/shard_map/ppermute | solution.py:481
  48.2 9.8 %collective-permute-start.15 = (bf16[1120,128]{1,0:T(8,128)(2,1)}, bf16[1120,128]{1,0:T(8,128)(2,1)}, u32[]{:S(2)}, u32[]{:S(2)}) collective-permute-start(bf16[1120,128]{1,0:T(8,128)(2,1)} %collective-permute-done.14.refs_11_), channel_id=1, source_target_pairs={{0,32},{32,64},{64,96},{96,128},{128,160},{160,192},{192,224},{224... | collective-permute-start | bytes 860168 | tf_op jit(solution)/shard_map/ppermute | solution.py:481
  48.3 12.6 %collective-permute-start.16 = (bf16[1120,128]{1,0:T(8,128)(2,1)}, bf16[1120,128]{1,0:T(8,128)(2,1)S(1)}, u32[]{:S(2)}, u32[]{:S(2)}) collective-permute-start(bf16[1120,128]{1,0:T(8,128)(2,1)} %collective-permute-done.12.refs_8_), channel_id=1, source_target_pairs={{0,32},{32,64},{64,96},{96,128},{128,160},{160,192},{192,224},{224... | collective-permute-start | bytes 860168 | tf_op jit(solution)/shard_map/ppermute | solution.py:481
  50.8 12.4 %collective-permute-start.17 = (bf16[1120,128]{1,0:T(8,128)(2,1)}, bf16[1120,128]{1,0:T(8,128)(2,1)S(1)}, u32[]{:S(2)}, u32[]{:S(2)}) collective-permute-start(bf16[1120,128]{1,0:T(8,128)(2,1)} %collective-permute-done.9.refs_7_), channel_id=1, source_target_pairs={{0,224},{32,0},{64,32},{96,64},{128,96},{160,128},{192,160},{224,1... | collective-permute-start | bytes 860168 | tf_op jit(solution)/shard_map/ppermute | solution.py:481
  66.3 5.1 %collective-permute-start.18 = (bf16[3520,128]{1,0:T(8,128)(2,1)S(1)}, bf16[3520,128]{1,0:T(8,128)(2,1)S(1)}, u32[]{:S(2)}, u32[]{:S(2)}) collective-permute-start(bf16[3520,128]{1,0:T(8,128)(2,1)S(1)} %select_pieces.3), channel_id=1, source_target_pairs={{0,4},{4,0},{1,5},{5,1},{2,6},{6,2},{3,7},{7,3},{8,12},{12,8},{9,1... | collective-permute-start | bytes 2703368 | tf_op jit(solution)/shard_map/ppermute | solution.py:506
  71.4 6.1 %collective-permute-start.20 = (bf16[448,128]{1,0:T(8,128)(2,1)S(1)}, bf16[448,128]{1,0:T(8,128)(2,1)S(1)}, u32[]{:S(2)}, u32[]{:S(2)}) collective-permute-start(bf16[448,128]{1,0:T(8,128)(2,1)S(1)} %slice_add_fusion.3), channel_id=1, source_target_pairs={{0,1},{1,2},{2,3},{3,0},{4,5},{5,6},{6,7},{7,4},{8,9},{9,10},{10,1... | collective-permute-start | bytes 344072 | tf_op jit(solution)/shard_map/ppermute | solution.py:481
  72.9 13.7 %collective-permute-start.22 = (bf16[880,128]{1,0:T(8,128)(2,1)S(1)}, bf16[880,128]{1,0:T(8,128)(2,1)S(1)}, u32[]{:S(2)}, u32[]{:S(2)}) collective-permute-start(bf16[880,128]{1,0:T(8,128)(2,1)S(1)} %get-tuple-element.25), channel_id=1, source_target_pairs={{0,3},{1,0},{2,1},{3,2},{4,7},{5,4},{6,5},{7,6},{8,11},{9,8},{10,9... | collective-permute-start | bytes 675848 | tf_op jit(solution)/shard_map/ppermute | solution.py:481
  74.4 12.2 %collective-permute-start.19 = (bf16[880,128]{1,0:T(8,128)(2,1)S(1)}, bf16[880,128]{1,0:T(8,128)(2,1)S(1)}, u32[]{:S(2)}, u32[]{:S(2)}) collective-permute-start(bf16[880,128]{1,0:T(8,128)(2,1)S(1)} %get-tuple-element.26), channel_id=1, source_target_pairs={{0,1},{1,2},{2,3},{3,0},{4,5},{5,6},{6,7},{7,4},{8,9},{9,10},{10,1... | collective-permute-start | bytes 675848 | tf_op jit(solution)/shard_map/ppermute | solution.py:481
  74.5 7.7 %collective-permute-start.23 = (bf16[432,128]{1,0:T(8,128)(2,1)S(1)}, bf16[432,128]{1,0:T(8,128)(2,1)S(1)}, u32[]{:S(2)}, u32[]{:S(2)}) collective-permute-start(bf16[432,128]{1,0:T(8,128)(2,1)S(1)} %slice_add_fusion.4), channel_id=1, source_target_pairs={{0,3},{1,0},{2,1},{3,2},{4,7},{5,4},{6,5},{7,6},{8,11},{9,8},{10,9... | collective-permute-start | bytes 331784 | tf_op jit(solution)/shard_map/ppermute | solution.py:481
  77.6 9.1 %collective-permute-start.21 = (bf16[448,128]{1,0:T(8,128)(2,1)S(1)}, bf16[448,128]{1,0:T(8,128)(2,1)S(1)}, u32[]{:S(2)}, u32[]{:S(2)}) collective-permute-start(bf16[448,128]{1,0:T(8,128)(2,1)S(1)} %collective-permute-done.20), channel_id=1, source_target_pairs={{0,1},{1,2},{2,3},{3,0},{4,5},{5,6},{6,7},{7,4},{8,9},{9,10},{10,1... | collective-permute-start | bytes 344072 | tf_op jit(solution)/shard_map/ppermute | solution.py:481
  (9 other events, 235.3 us)
